TPU v7x, 32 devices: a whole 2x2x4 slice. The times are simulated.
32 devices in a mesh: seq: 8 (over y, x, core), blk: 4 (over z).
Axes of the slice: x: 2, y: 2, z: 4, core: 2. Of those that a mesh axis runs over, the one named last changes fastest.
Arguments:
- states: bfloat16 [8, 2560, 768], P('seq', 'blk'), may hold values from -6 to 6
- cotangent: bfloat16 [8, 2560, 768], P('seq', 'blk'), may hold values from -6 to 6
- lengths: int32 [8, 5], P('seq'), may hold values from 64 to 512, as said below
- w_qkv: bfloat16 [768, 2304], P(('seq', 'blk')), may hold values from -0.21875 to 0.21875
- w_out: bfloat16 [768, 768], P(('seq', 'blk')), may hold values from -1.75 to 1.75
- w_up: bfloat16 [768, 3072], P(('seq', 'blk')), may hold values from -0.21875 to 0.21875
- w_down: bfloat16 [3072, 768], P(('seq', 'blk')), may hold values from -0.109375 to 0.109375
- vectors: bfloat16 [13, 768], P(None, ('seq', 'blk'))
- up_bias: bfloat16 [3072], P(('seq', 'blk')), may hold values from -1.796875 to 1.796875
Outputs:
- result: bfloat16 [8, 2560, 768], P('seq', 'blk')
- grad_states: bfloat16 [8, 2560, 768], P('seq', 'blk')
- grad_qkv: float32 [768, 2304], P(('seq', 'blk'))
- grad_out: float32 [768, 768], P(('seq', 'blk'))
- grad_up: float32 [768, 3072], P(('seq', 'blk'))
- grad_down: float32 [3072, 768], P(('seq', 'blk'))
- grad_vectors: float32 [13, 768], P(None, ('seq', 'blk'))
- grad_up_bias: float32 [3072], P(('seq', 'blk'))
Inputs may be any that keep to these rules, and one draw needn't show every extreme that they name: `lengths`: every sequence's first pass has all 512 slots live; a later pass has between 64 and 512 live slots, the live ones first.
All inputs are finite; a program needn't handle non-finite values.
Results may differ from a plain program's by a relative error of at most 0.015.
Values may be sent and summed in bfloat16 or wider, within the bound.
No kernel may reach another device: no remote copies, remote signals or barrier semaphores. Data moves between devices by JAX's collectives and lax.ppermute only.
A program may use at most 192 MiB of HBM per device.

v0:
```python
import jax
import jax.numpy as jnp
from jax import lax
from jax.sharding import PartitionSpec as P

HEAD = 64
PASSES = 5
PASS_SLOTS = 512


highest = lax.Precision.HIGHEST
masked_value = -1e30


def layer_norm(values, gain, offset):
    centre = values - jnp.mean(values, axis=-1, keepdims=True)
    spread = jnp.mean(centre * centre, axis=-1, keepdims=True)
    return centre * lax.rsqrt(spread + 1e-05) * gain + offset


def gelu_tanh(values):
    return jax.nn.gelu(values, approximate=True)


def live_slots(slot_index, pass_lengths):
    matches = (slot_index // PASS_SLOTS)[:, None] == jnp.arange(PASSES, dtype=jnp.int32)[None, :]
    bounds = jnp.sum(jnp.where(matches, pass_lengths[None, :], 0), axis=1)
    return slot_index % PASS_SLOTS < bounds


def visible(query_slots, key_slots, key_live):
    earlier = key_slots[None, :] // PASS_SLOTS <= query_slots[:, None] // PASS_SLOTS
    before = key_slots[None, :] % PASS_SLOTS <= query_slots[:, None] % PASS_SLOTS
    return earlier & before & key_live[None, :]


def tile_scores(queries, key_rows, tile_mask):
    scores = (
        jnp.einsum("qhe,khe->hqk", queries, key_rows, preferred_element_type=jnp.float32) * 0.125
    )
    return jnp.where(tile_mask[None], scores, masked_value)


def keep_state(carried):
    return carried


def attend(queries, key_rows, value_rows, query_slots, key_live, top_pass):
    row_count, head_count, width_head = queries.shape
    key_slots = jnp.arange(key_rows.shape[0], dtype=jnp.int32)
    masks = []
    running = (
        jnp.full((head_count, row_count), masked_value, jnp.float32),
        jnp.zeros((head_count, row_count), jnp.float32),
    )
    for tile_index in range(PASSES):
        lower_edge = tile_index * PASS_SLOTS
        tile_keys = key_rows[lower_edge : lower_edge + PASS_SLOTS]
        tile_mask = visible(
            query_slots,
            key_slots[lower_edge : lower_edge + PASS_SLOTS],
            key_live[lower_edge : lower_edge + PASS_SLOTS],
        )
        masks.append(tile_mask)

        def accumulate(carried):
            scores = tile_scores(queries, tile_keys, tile_mask)
            newest = jnp.maximum(carried[0], jnp.max(scores, axis=-1))
            shares = jnp.where(tile_mask[None], jnp.exp(scores - newest[..., None]), 0.0)
            return (newest, carried[1] * jnp.exp(carried[0] - newest) + jnp.sum(shares, axis=-1))

        running = lax.cond(tile_index <= top_pass, accumulate, keep_state, running)
    log_total = running[0] + jnp.log(running[1])
    mixture = jnp.zeros((row_count, head_count, width_head), jnp.float32)
    for tile_index in range(PASSES):
        lower_edge = tile_index * PASS_SLOTS
        tile_keys = key_rows[lower_edge : lower_edge + PASS_SLOTS]
        tile_values = value_rows[lower_edge : lower_edge + PASS_SLOTS]
        tile_mask = masks[tile_index]

        def combine(carried):
            scores = tile_scores(queries, tile_keys, tile_mask)
            chances = jnp.where(
                tile_mask[None], jnp.exp(scores - log_total[..., None]), 0.0
            ).astype(jnp.bfloat16)
            return carried + jnp.einsum(
                "hqk,khe->qhe", chances, tile_values, preferred_element_type=jnp.float32
            )

        mixture = lax.cond(tile_index <= top_pass, combine, keep_state, mixture)
    return (mixture, log_total, masks)


def pair_gradients(queries, grad_rows, log_total, row_delta, key_rows, value_rows, tile_mask):
    scores = tile_scores(queries, key_rows, tile_mask)
    chances = jnp.where(tile_mask[None], jnp.exp(scores - log_total[..., None]), 0.0)
    grad_chances = jnp.einsum(
        "qhe,khe->hqk", grad_rows, value_rows, preferred_element_type=jnp.float32
    )
    grad_scores = (chances * (grad_chances - row_delta[..., None])).astype(jnp.bfloat16)
    found = []
    found.append(
        0.125
        * jnp.einsum("hqk,khe->qhe", grad_scores, key_rows, preferred_element_type=jnp.float32)
    )
    found.append(
        0.125 * jnp.einsum("hqk,qhe->khe", grad_scores, queries, preferred_element_type=jnp.float32)
    )
    found.append(
        jnp.einsum(
            "hqk,qhe->khe",
            chances.astype(jnp.bfloat16),
            grad_rows,
            preferred_element_type=jnp.float32,
        )
    )
    return found


def query_tiles(queries, grad_rows, log_total, row_delta, key_rows, value_rows, masks, top_pass):
    row_count, head_count, width_head = queries.shape
    grad_query = jnp.zeros((row_count, head_count, width_head), jnp.float32)
    key_parts = []
    for tile_index in range(PASSES):
        lower_edge = tile_index * PASS_SLOTS
        tile_keys = key_rows[lower_edge : lower_edge + PASS_SLOTS]
        tile_values = value_rows[lower_edge : lower_edge + PASS_SLOTS]
        tile_mask = masks[tile_index]

        def both_sides(current):
            found = pair_gradients(
                queries, grad_rows, log_total, row_delta, tile_keys, tile_values, tile_mask
            )
            joined = jnp.concatenate(
                [
                    found[1].reshape(PASS_SLOTS, head_count * width_head),
                    found[2].reshape(PASS_SLOTS, head_count * width_head),
                ],
                axis=1,
            )
            return (current + found[0], joined)

        def skip_tile(current):
            return (current, jnp.zeros((PASS_SLOTS, 2 * head_count * width_head), jnp.float32))

        grad_query, joined = lax.cond(tile_index <= top_pass, both_sides, skip_tile, grad_query)
        key_parts.append(joined)
    return (grad_query, key_parts)


def on_device(states, cotangent, lengths, w_qkv, w_out, w_up, w_down, vectors, up_bias):
    full_qkv, full_out, full_up, full_down, full_table, full_bias = (
        lax.all_gather(w_qkv, ("seq", "blk"), axis=0, tiled=True),
        lax.all_gather(w_out, ("seq", "blk"), axis=0, tiled=True),
        lax.all_gather(w_up, ("seq", "blk"), axis=0, tiled=True),
        lax.all_gather(w_down, ("seq", "blk"), axis=0, tiled=True),
        lax.all_gather(vectors, ("seq", "blk"), axis=1, tiled=True),
        lax.all_gather(up_bias, ("seq", "blk"), axis=0, tiled=True),
    )
    table = full_table.astype(jnp.float32)
    bias_up = full_bias.astype(jnp.float32)
    seq_count, row_count, width = states.shape
    head_count = width // HEAD
    block_count = lax.axis_size("blk")
    first_slot = lax.axis_index("blk") * row_count
    count = seq_count * row_count
    query_slots = first_slot + jnp.arange(row_count, dtype=jnp.int32)
    all_slots = jnp.arange(row_count * block_count, dtype=jnp.int32)
    top_pass = (first_slot + row_count - 1) // PASS_SLOTS
    pass_table = (
        (query_slots // PASS_SLOTS)[:, None] == jnp.arange(PASSES, dtype=jnp.int32)[None, :]
    ).astype(jnp.float32)
    query_live = [live_slots(query_slots, lengths[0])]
    key_live = [live_slots(all_slots, lengths[0])]
    live_weight = jnp.stack(query_live).astype(jnp.float32).reshape(count, 1)
    start = (
        states.astype(jnp.float32) + jnp.dot(pass_table, table[:PASSES], precision=highest)[None]
    ).reshape(count, width)
    normed_a = layer_norm(start, table[5], table[6]).astype(jnp.bfloat16)
    bias_three = jnp.concatenate([table[7], jnp.zeros_like(table[7]), table[8]])
    projected = (
        jnp.dot(normed_a, full_qkv, preferred_element_type=jnp.float32) + bias_three
    ).astype(jnp.bfloat16)
    query_flat = projected[:, :width].reshape(seq_count, row_count, width)
    local_pairs = projected[:, width:].reshape(seq_count, row_count, 2 * width)
    whole_pairs = lax.all_gather(local_pairs, "blk", axis=1, tiled=True)
    slot_total = row_count * block_count
    log_totals = []
    index = 0
    mixture, log_total, masks = attend(
        query_flat[index].reshape(row_count, head_count, HEAD),
        whole_pairs[index, :, :width].reshape(slot_total, head_count, HEAD),
        whole_pairs[index, :, width:].reshape(slot_total, head_count, HEAD),
        query_slots,
        key_live[index],
        top_pass,
    )
    mixtures = [mixture.reshape(row_count, width)]
    log_totals.append(log_total)
    all_masks = [masks]
    mixture = jnp.stack(mixtures).reshape(count, width)
    log_totals = jnp.stack(log_totals)
    heads_out = mixture.astype(jnp.bfloat16)
    middle = start + live_weight * (
        jnp.dot(heads_out, full_out, preferred_element_type=jnp.float32) + table[9]
    )
    normed_b = layer_norm(middle, table[10], table[11]).astype(jnp.bfloat16)
    up_sum = jnp.dot(normed_b, full_up, preferred_element_type=jnp.float32) + bias_up
    activated, gelu_pull = jax.vjp(gelu_tanh, up_sum)
    hidden = activated.astype(jnp.bfloat16)
    outcome = middle + live_weight * (
        jnp.dot(hidden, full_down, preferred_element_type=jnp.float32) + table[12]
    )
    incoming = cotangent.astype(jnp.float32).reshape(count, width)
    grad_branch = (live_weight * incoming).astype(jnp.bfloat16)
    grad_down = jnp.einsum("nf,nd->fd", hidden, grad_branch, preferred_element_type=jnp.float32)
    grad_hidden = jnp.einsum(
        "nd,fd->nf", grad_branch, full_down, preferred_element_type=jnp.float32
    )
    grad_upsum = gelu_pull(grad_hidden)[0].astype(jnp.bfloat16)
    grad_up = jnp.einsum("nd,nf->df", normed_b, grad_upsum, preferred_element_type=jnp.float32)
    grad_normb = jnp.einsum("nf,df->nd", grad_upsum, full_up, preferred_element_type=jnp.float32)
    norm_pull_b = jax.vjp(layer_norm, middle, table[10], table[11])[1]
    middle_part, gain_grad_b, shift_grad_b = norm_pull_b(grad_normb)
    grad_middle = incoming + middle_part
    grad_attn = (live_weight * grad_middle).astype(jnp.bfloat16)
    grad_out = jnp.einsum("nd,ne->de", heads_out, grad_attn, preferred_element_type=jnp.float32)
    grad_heads = jnp.einsum(
        "ne,de->nd", grad_attn, full_out, preferred_element_type=jnp.float32
    ).astype(jnp.bfloat16)
    row_deltas = jnp.sum(
        (grad_heads.astype(jnp.float32) * mixture).reshape(seq_count, row_count, head_count, HEAD),
        axis=-1,
    ).transpose(0, 2, 1)
    grad_rows = grad_heads.reshape(seq_count, row_count, width)
    index = 0
    grad_query, key_parts = query_tiles(
        query_flat[index].reshape(row_count, head_count, HEAD),
        grad_rows[index].reshape(row_count, head_count, HEAD),
        log_totals[index],
        row_deltas[index],
        whole_pairs[index, :, :width].reshape(slot_total, head_count, HEAD),
        whole_pairs[index, :, width:].reshape(slot_total, head_count, HEAD),
        all_masks[index],
        top_pass,
    )
    grad_queries = [grad_query.reshape(row_count, width)]
    partials = [jnp.concatenate(key_parts, axis=0)]
    pair_grads = lax.psum_scatter(
        jnp.stack(partials).astype(jnp.bfloat16), "blk", scatter_dimension=1, tiled=True
    ).astype(jnp.float32)
    grad_projected = jnp.concatenate([jnp.stack(grad_queries), pair_grads], axis=-1).reshape(
        count, 3 * width
    )
    grad_projected = grad_projected.astype(jnp.bfloat16)
    grad_qkv = jnp.einsum("nd,ne->de", normed_a, grad_projected, preferred_element_type=jnp.float32)
    column_sums = jnp.sum(grad_projected.astype(jnp.float32), axis=0)
    grad_norma = jnp.einsum(
        "ne,de->nd", grad_projected, full_qkv, preferred_element_type=jnp.float32
    )
    norm_pull_a = jax.vjp(layer_norm, start, table[5], table[6])[1]
    start_part, gain_grad_a, shift_grad_a = norm_pull_a(grad_norma)
    grad_start = grad_middle + start_part
    grad_embed = jnp.einsum(
        "rp,srd->pd", pass_table, grad_start.reshape(seq_count, row_count, width), precision=highest
    )
    small_grads = jnp.stack(
        [
            gain_grad_a,
            shift_grad_a,
            column_sums[:width],
            column_sums[2 * width :],
            jnp.sum(grad_attn.astype(jnp.float32), axis=0),
            gain_grad_b,
            shift_grad_b,
            jnp.sum(grad_branch.astype(jnp.float32), axis=0),
        ]
    )
    vector_grads = jnp.concatenate([grad_embed, small_grads], axis=0)
    bias_grads = jnp.sum(grad_upsum.astype(jnp.float32), axis=0)
    owned_grads = (
        lax.psum_scatter(grad_qkv, ("seq", "blk"), scatter_dimension=0, tiled=True),
        lax.psum_scatter(grad_out, ("seq", "blk"), scatter_dimension=0, tiled=True),
        lax.psum_scatter(grad_up, ("seq", "blk"), scatter_dimension=0, tiled=True),
        lax.psum_scatter(grad_down, ("seq", "blk"), scatter_dimension=0, tiled=True),
        lax.psum_scatter(vector_grads, ("seq", "blk"), scatter_dimension=1, tiled=True),
        lax.psum_scatter(bias_grads, ("seq", "blk"), scatter_dimension=0, tiled=True),
    )
    return (
        outcome.astype(jnp.bfloat16).reshape(seq_count, row_count, width),
        grad_start.astype(jnp.bfloat16).reshape(seq_count, row_count, width),
        owned_grads[0],
        owned_grads[1],
        owned_grads[2],
        owned_grads[3],
        owned_grads[4],
        owned_grads[5],
    )


def solution(mesh):
    placed = (
        P("seq", "blk", None),
        P("seq", "blk", None),
        P("seq", None),
        P(("seq", "blk"), None),
        P(("seq", "blk"), None),
        P(("seq", "blk"), None),
        P(("seq", "blk"), None),
        P(None, ("seq", "blk")),
        P(("seq", "blk")),
    )
    return jax.shard_map(
        on_device,
        mesh=mesh,
        in_specs=placed,
        out_specs=(
            P("seq", "blk", None),
            P("seq", "blk", None),
            P(("seq", "blk"), None),
            P(("seq", "blk"), None),
            P(("seq", "blk"), None),
            P(("seq", "blk"), None),
            P(None, ("seq", "blk")),
            P(("seq", "blk")),
        ),
        check_vma=False,
    )
```

profile of v0, /device:TPU:0, one launch (start us, length us, event | category | flops | bytes accessed | tf_op | source)
XLA Modules:
  0.0 1322.0 jit_solution(16944562241491706908)
XLA Ops:
  8.0 71.2 %all-gather.1 = bf16[32,24,13]{1,2,0:T(8,128)(2,1)S(1)} all-gather(bf16[1,24,13]{1,2,0:T(8,128)(2,1)} %bitcast.316), channel_id=1, replica_groups=mesh['seq'=8,'blk'=4] {'seq','blk'}, dimensions={0}, use_global_device_ids=true | all-gather | bytes 20592 | tf_op jit(solution)/shard_map/all_gather | solution.py:157
  82.3 4.9 add_convert_fusion
  92.5 43.7 %all-reduce = bf16[3072]{0:T(1024)(128)(2,1)S(1)} all-reduce(bf16[3072]{0:T(1024)(128)(2,1)S(1)} %dynamic-update-slice), channel_id=1, replica_groups=mesh['seq'=8,'blk'=4] {'seq','blk'}, use_global_device_ids=true, to_apply=%add | all-reduce | flops 3072 | bytes 12288
  136.5 4.3 and_and_fusion
  144.6 84.3 %all-gather.16.cloned.1.call-done = bf16[2560,1536]{1,0:T(8,128)(2,1)} async-done(((bf16[640,1536]{1,0:T(8,128)(2,1)}), bf16[2560,1536]{1,0:T(8,128)(2,1)}) %all-gather.16.cloned.1.call-update) | async-done | bytes 7864336 | tf_op jit(solution)/shard_map/all_gather | solution.py:186
  228.9 5.6 fusion.154
  234.6 2.3 copy.124
  239.2 2.4 copy.122
  248.5 2.3 copy.116
  253.1 2.4 copy.112
  255.4 2.3 copy.110
  257.7 21.0 %conditional.15 = (f32[12,640]{1,0:T(8,128)}, f32[12,640]{1,0:T(8,128)S(1)}) conditional(s32[]{:T(128)} %convert_element_type.175, () %tuple.147, (pred[640,512]{1,0:T(8,128)(4,1)}, bf16[640,12,64]{0,2,1:T(8,128)(2,1)S(1)}, bf16[512,12,64]{0,2,1:T(8,128)(2,1)}) %tuple.363), branch_computations={%region_4.5_spmd, %region_5.8_spmd} | conditional | flops 534796800 | bytes 34783248 | solution.py:72
  259.7 9.1 fusion
  269.4 9.3 select_reduce_fusion
  278.7 22.3 %conditional.16 = ((f32[12,640]{1,0:T(8,128)}, f32[12,640]{1,0:T(8,128)S(1)})) conditional(s32[]{:T(128)} %convert_element_type.174, (f32[12,640]{1,0:T(8,128)}, f32[12,640]{1,0:T(8,128)S(1)}) %conditional.15, (pred[640,512]{1,0:T(8,128)(4,1)}, bf16[640,12,64]{0,2,1:T(8,128)(2,1)S(1)}, bf16[512,12,64]{0,2,1:T(8,128)(2,1)}, f32[12,640]{1,0:T(8,128)}, ...), branch_computations={%region_8.9_spmd, %region_9.12_spmd} | conditional | flops 534789120 | bytes 34936856 | solution.py:72
  280.4 9.1 fusion.1
  290.2 9.4 select_reduce_fusion.1
  301.2 5.4 conditional.18
  306.6 5.7 conditional.19
  313.1 16.4 %conditional.20 = (f32[640,12,64]{0,2,1:T(8,128)}) conditional(s32[]{:T(128)} %convert_element_type.175, () %tuple.146, (pred[640,512]{1,0:T(8,128)(4,1)}, bf16[640,12,64]{0,2,1:T(8,128)(2,1)S(1)}, bf16[512,12,64]{0,2,1:T(8,128)(2,1)}, f32[12,640]{1,0:T(8,128)S(1)}, bf16[512,12,64]{0,2,1:T(8,128)(2,1)}) %tuple.384), branch_computations={%region_24.25_spmd, %region_25.26_spmd} | conditional | flops 1026293760 | bytes 4880392 | solution.py:90
  319.6 9.8 fusion.6
  329.4 10.0 conditional.21
  329.4 10.0 bitcast_add_fusion
  340.8 5.6 conditional.24
  340.8 2.6 bitcast_convert_fusion
  343.4 3.0 copy.134
  346.4 2.8 fusion.158
  350.9 9.4 fusion.151
  360.3 53.4 %all-gather.14.cloned.1.call-done = bf16[3072,768]{1,0:T(8,128)(2,1)} async-done(((bf16[96,768]{1,0:T(8,128)(2,1)}), bf16[3072,768]{1,0:T(8,128)(2,1)}) %all-gather.14.cloned.1.call-update) | async-done | bytes 4718608 | tf_op jit(solution)/shard_map/all_gather | solution.py:156
  413.7 12.2 convert_reduce_fusion
  426.0 4.1 multiply_reduce_fusion
  441.1 27.6 %conditional.25 = (f32[640,12,64]{0,2,1:T(8,128)S(1)}, bf16[1,512,1536]{1,2,0:T(8,128)(2,1)S(1)}) conditional(s32[]{:T(128)} %convert_element_type.175, () %tuple.158, (pred[640,512]{1,0:T(8,128)(4,1)S(1)}, bf16[640,12,64]{0,2,1:T(8,128)(2,1)S(1)}, bf16[512,12,64]{0,2,1:T(8,128)(2,1)}, f32[12,640]{1,0:T(8,128)S(1)}, ...), branch_computations={%region_39.40_spmd, %region_40.41_spmd} | conditional | flops 2568192000 | bytes 157640848 | solution.py:146
  441.1 3.5 fusion.159
  444.6 5.4 copy-done.6
  450.0 4.9 fusion.23
  454.9 9.5 multiply_convert_fusion
  465.9 2.5 multiply_bitcast_fusion
  469.8 28.3 %conditional.26 = (f32[640,12,64]{0,2,1:T(8,128)S(1)}, bf16[1,512,1536]{1,2,0:T(8,128)(2,1)S(1)}) conditional(s32[]{:T(128)} %convert_element_type.174, f32[640,12,64]{0,2,1:T(8,128)S(1)} %get-tuple-element.385, (pred[640,512]{1,0:T(8,128)(4,1)}, bf16[640,12,64]{0,2,1:T(8,128)(2,1)S(1)}, bf16[512,12,64]{0,2,1:T(8,128)(2,1)}, ...), branch_computations={%region_41.42_spmd, %region_42.43_spmd} | conditional | flops 2568683520 | bytes 164063440 | solution.py:146
  469.8 3.5 fusion.160
  473.3 5.4 copy-done.7
  478.8 5.6 fusion.31
  484.4 9.6 multiply_convert_fusion.1
  494.1 2.5 bitcast_add_fusion.3
  501.1 4.6 conditional.28
  506.8 7.1 conditional.29
  513.9 2.9 constant_dynamic-update-slice_fusion.4
  516.8 2.7 constant_dynamic-update-slice_fusion.3
  519.6 2.7 constant_dynamic-update-slice_fusion.2
  524.9 32.3 %copy.128 = bf16[1,2560,1536]{2,0,1:T(2,128)(2,1)} copy(bf16[1,2560,1536]{1,2,0:T(8,128)(2,1)} %constant_dynamic-update-slice_fusion) | data formatting | bytes 15728640
  557.2 10.8 copy.138
  569.2 3.7 fusion.164
  573.4 12.3 fusion.144
  586.4 10.4 fusion.150
  598.0 202.9 %reduce-scatter.17.cloned.1.call-done = bf16[640,1536]{1,0:T(8,128)(2,1)} async-done(((bf16[2560,1536]{1,0:T(8,128)(2,1)}), bf16[640,1536]{1,0:T(8,128)(2,1)}) %reduce-scatter.17.cloned.1.call-update) | async-done | bytes 1966096
  800.9 5.2 reshape_bitcast_fusion
  806.1 8.7 copy.129
  815.0 7.7 fusion.73
  822.8 11.4 fusion.79
  834.3 3.1 multiply_reduce_fusion.1
  841.5 41.9 %all-reduce.3 = (f32[13,768]{1,0:T(8,128)S(1)}, f32[3072]{0:T(1024)S(1)}) all-reduce(f32[13,768]{1,0:T(8,128)S(1)} %concatenate.72, f32[3072]{0:T(1024)S(1)} %copy-done.78), channel_id=8, replica_groups=mesh['seq'=8,'blk'=4] {'seq','blk'}, use_global_device_ids=true, to_apply=%region_63.64.clone | all-reduce | flops 13056 | bytes 104448
  884.7 22.3 %reduce-scatter.11.cloned.1.call-done = f32[24,768]{1,0:T(8,128)} async-done(((f32[768,768]{1,0:T(8,128)}), f32[24,768]{1,0:T(8,128)}) %reduce-scatter.11.cloned.1.call-update) | async-done | bytes 73744 | tf_op jit(solution)/shard_map/reduce_scatter | solution.py:283
  907.0 141.7 %reduce-scatter.15.cloned.1.call-done = f32[96,768]{1,0:T(8,128)} async-done(((f32[3072,768]{1,0:T(8,128)}), f32[96,768]{1,0:T(8,128)}) %reduce-scatter.15.cloned.1.call-update) | async-done | bytes 294928 | tf_op jit(solution)/shard_map/reduce_scatter | solution.py:285
  1048.7 141.6 %reduce-scatter.13.cloned.1.call-done = f32[24,3072]{1,0:T(8,128)} async-done(((f32[768,3072]{1,0:T(8,128)}), f32[24,3072]{1,0:T(8,128)}) %reduce-scatter.13.cloned.1.call-update) | async-done | bytes 294928 | tf_op jit(solution)/shard_map/reduce_scatter | solution.py:284
  1190.3 124.6 %reduce-scatter.9.cloned.1.call-done = f32[24,2304]{1,0:T(8,128)} async-done(((f32[768,2304]{1,0:T(8,128)}), f32[24,2304]{1,0:T(8,128)}) %reduce-scatter.9.cloned.1.call-update) | async-done | bytes 221200 | tf_op jit(solution)/shard_map/reduce_scatter | solution.py:282
  (250 shorter events, 65.1 us)
Async XLA Ops:
  7.2 75.1 %all-gather.8.cloned.1.call-start = ((), (), s32[]{:S(2)}) async-start(), calls=%async_computation.5 | async-start | bytes 3649536 | tf_op jit(solution)/shard_map/all_gather | solution.py:153
  7.9 221.0 %all-gather.16.cloned.1.call-start = ((), (), s32[]{:S(2)}) async-start(), calls=%async_computation.13 | async-start | bytes 9830400 | tf_op jit(solution)/shard_map/all_gather | solution.py:186
  79.4 57.2 %copy-start.60 = (s32[640]{0:T(1024)}, s32[640]{0:T(1024)S(1)}, u32[]{:S(2)}) copy-start(s32[640]{0:T(1024)S(1)} %add_select_fusion.3) | copy-start | bytes 7684
  80.0 7.2 copy-start.68
  80.0 7.2 copy-start.80
  80.0 270.8 %copy-start.58 = (f32[768]{0:T(1024)}, f32[768]{0:T(1024)S(1)}, u32[]{:S(2)}) copy-start(f32[768]{0:T(1024)S(1)} %get-tuple-element.624) | copy-start | bytes 9220
  80.0 350.1 %copy-start.54 = (f32[768]{0:T(1024)}, f32[768]{0:T(1024)S(1)}, u32[]{:S(2)}) copy-start(f32[768]{0:T(1024)S(1)} %get-tuple-element.622) | copy-start | bytes 9220
  81.8 264.5 %copy-start = (f32[1,640,768]{2,1,0:T(8,128)}, f32[1,640,768]{2,1,0:T(8,128)S(1)}, u32[]{:S(2)}) copy-start(f32[1,640,768]{2,1,0:T(8,128)S(1)} %get-tuple-element.674) | copy-start | bytes 5898244
  81.8 5.4 copy-start.62
  82.2 5.0 copy-start.64
  82.2 5.0 copy-start.70
  82.3 10.0 copy-start.87
  82.3 54.0 %copy-start.84 = (s32[1,5]{1,0:T(1,128)S(1)}, s32[1,5]{1,0:T(1,128)}, u32[]{:S(2)}) copy-start(s32[1,5]{1,0:T(1,128)} %param.41) | copy-start | bytes 64
  90.2 256.1 %all-gather.10.cloned.1.call-start = ((), (), s32[]{:S(2)}) async-start(), calls=%async_computation.6 | async-start | bytes 1216512 | tf_op jit(solution)/shard_map/all_gather | solution.py:154
  91.0 259.9 %all-gather.12.cloned.1.call-start = ((), (), s32[]{:S(2)}) async-start(), calls=%async_computation.7 | async-start | bytes 4866048 | tf_op jit(solution)/shard_map/all_gather | solution.py:155
  91.5 322.1 %all-gather.14.cloned.1.call-start = ((), (), s32[]{:S(2)}) async-start(), calls=%async_computation.8 | async-start | bytes 4866048 | tf_op jit(solution)/shard_map/all_gather | solution.py:156
  92.1 708.8 %reduce-scatter.17.cloned.1.call-start = ((), (), s32[]{:S(2)}) async-start(), calls=%async_computation.14 | async-start | bytes 9830400
  136.2 277.5 %copy-start.76 = (f32[3072]{0:T(1024)}, f32[3072]{0:T(1024)S(1)}, u32[]{:S(2)}) copy-start(f32[3072]{0:T(1024)S(1)} %convert_element_type.180) | copy-start | bytes 36868
  136.5 294.4 %copy-start.74 = (f32[640]{0:T(1024)}, f32[640]{0:T(1024)S(1)}, u32[]{:S(2)}) copy-start(f32[640]{0:T(1024)S(1)} %compare_convert_fusion) | copy-start | bytes 7684
  329.4 10.0 copy-start.33
  349.2 80.9 %copy-start.52 = (f32[640]{0:T(1024)}, f32[640]{0:T(1024)S(1)}, u32[]{:S(2)}) copy-start(f32[640]{0:T(1024)S(1)} %broadcast_multiply_fusion) | copy-start | bytes 7684
  350.8 79.3 %copy-start.56 = (f32[640]{0:T(1024)}, f32[640]{0:T(1024)S(1)}, u32[]{:S(2)}) copy-start(f32[640]{0:T(1024)S(1)} %fusion.106) | copy-start | bytes 7684
  360.3 65.7 %copy-start.5 = (f32[640,768]{1,0:T(8,128)S(1)}, f32[640,768]{1,0:T(8,128)}, u32[]{:S(2)}) copy-start(f32[640,768]{1,0:T(8,128)} %copy-done.4) | copy-start | bytes 5898244
  413.7 12.3 copy-start.85
  425.9 4.1 copy-start.28
  425.9 6.2 copy-start.26
  430.1 3.3 copy-start.17
  430.1 3.3 copy-start.37
  430.9 4.5 copy-start.66
  433.4 2.0 copy-start.23
  433.4 7.7 copy-start.36
  441.1 8.9 copy-start.38
  444.6 5.4 copy-start.6
  450.0 4.9 copy-start.47
  468.7 29.5 %copy-start.34 = (pred[640,512]{1,0:T(8,128)(4,1)S(1)}, pred[640,512]{1,0:T(8,128)(4,1)}, u32[]{:S(2)}) copy-start(pred[640,512]{1,0:T(8,128)(4,1)} %get-tuple-element.664) | copy-start | bytes 983044
  469.8 8.9 copy-start.35
  469.8 8.9 copy-start.39
  473.3 5.4 copy-start.7
  478.7 5.6 copy-start.46
  484.4 9.7 copy-start.14
  499.9 5.8 copy-start.31
  513.9 8.3 copy-start.22
  568.0 5.4 copy-start.75
  568.0 5.4 copy-start.77
  568.0 339.0 %reduce-scatter.11.cloned.1.call-start = ((), (), s32[]{:S(2)}) async-start(), calls=%async_computation.10 | async-start | bytes 2433024 | tf_op jit(solution)/shard_map/reduce_scatter | solution.py:283
  572.9 475.8 %reduce-scatter.15.cloned.1.call-start = ((), (), s32[]{:S(2)}) async-start(), calls=%async_computation.12 | async-start | bytes 9732096 | tf_op jit(solution)/shard_map/reduce_scatter | solution.py:285
  585.7 604.6 %reduce-scatter.13.cloned.1.call-start = ((), (), s32[]{:S(2)}) async-start(), calls=%async_computation.11 | async-start | bytes 9732096 | tf_op jit(solution)/shard_map/reduce_scatter | solution.py:284
  596.8 218.0 %copy-start.63 = (f32[640]{0:T(1024)S(1)}, f32[640]{0:T(1024)}, u32[]{:S(2)}) copy-start(f32[640]{0:T(1024)} %copy-done.62) | copy-start | bytes 7684
  596.9 218.0 %copy-start.69 = (f32[768]{0:T(1024)S(1)}, f32[768]{0:T(1024)}, u32[]{:S(2)}) copy-start(f32[768]{0:T(1024)} %copy-done.68) | copy-start | bytes 9220
  596.9 218.0 %copy-start.71 = (f32[640]{0:T(1024)S(1)}, f32[640]{0:T(1024)}, u32[]{:S(2)}) copy-start(f32[640]{0:T(1024)} %copy-done.70) | copy-start | bytes 7684
  596.9 218.0 %copy-start.81 = (f32[768]{0:T(1024)S(1)}, f32[768]{0:T(1024)}, u32[]{:S(2)}) copy-start(f32[768]{0:T(1024)} %copy-done.80) | copy-start | bytes 9220
  596.9 718.1 %reduce-scatter.9.cloned.1.call-start = ((), (), s32[]{:S(2)}) async-start(), calls=%async_computation.9 | async-start | bytes 7299072 | tf_op jit(solution)/shard_map/reduce_scatter | solution.py:282
  598.0 216.9 %copy-start.1 = (f32[1,640,768]{2,1,0:T(8,128)S(1)}, f32[1,640,768]{2,1,0:T(8,128)}, u32[]{:S(2)}) copy-start(f32[1,640,768]{2,1,0:T(8,128)} %copy-done) | copy-start | bytes 5898244
  598.0 216.9 %copy-start.25 = (bf16[640,12,64]{0,2,1:T(8,128)(2,1)S(1)}, bf16[640,12,64]{0,2,1:T(8,128)(2,1)}, u32[]{:S(2)}) copy-start(bf16[640,12,64]{0,2,1:T(8,128)(2,1)} %convert.25) | copy-start | bytes 2949124
  814.9 7.8 copy-start.83
  814.9 7.8 copy-start.82
  814.9 7.8 copy-start.73
  815.0 7.8 copy-start.72
  815.0 7.9 copy-start.79
  822.8 11.4 copy-start.16
  822.8 11.4 copy-start.86
  834.3 3.7 copy-start.65
  837.5 3.2 copy-start.61
  838.0 3.5 copy-start.78
  (18 other events, 22.0 us)
Sparse Core Ops, SparseCore 0:
  10.8 63.1 all-gather.7
  90.4 138.5 all-gather.15
  231.7 52.1 all-gather.9
  286.6 62.5 all-gather.11
  351.8 61.8 all-gather.13
  568.1 232.7 reduce-scatter.16
  806.8 100.1 reduce-scatter.10
  913.5 135.2 reduce-scatter.14
  1055.2 135.0 reduce-scatter.12
  1196.4 118.5 reduce-scatter.8
where the time goes:
time: 1330 us; the launch traced here: 1320 us
  waiting for transfers between devices  774 us (58%)
  matrix products  169 us (13%)
  blocking collectives  157 us (12%)
  local copies, waits for them, and re-layouts  138 us (10%)
  other arithmetic  37.2 us (3%)
  loops' own time  31.1 us (2%)
  between operations  15.4 us (1%)
    unnamed x11, waiting for transfers between devices  205 us
    reduce_scatter x1, waiting for transfers between devices, on_device(): lax.psum_scatter(grad_down, ('seq', 'blk'), scatter_dimension=0, tiled=True)  142 us
    reduce_scatter x1, waiting for transfers between devices, on_device(): lax.psum_scatter(grad_up, ('seq', 'blk'), scatter_dimension=0, tiled=True)  142 us
    reduce_scatter x1, waiting for transfers between devices, on_device(): lax.psum_scatter(grad_qkv, ('seq', 'blk'), scatter_dimension=0, tiled=True)  125 us
    unnamed x2, blocking collectives  85.6 us
    all_gather x1, waiting for transfers between devices, on_device(): whole_pairs = lax.all_gather(local_pairs, 'blk', axis=1, tiled=True)  84.3 us
    unnamed x137, local copies, waits for them, and re-layouts  80.3 us
    all_gather x1, blocking collectives, on_device(): lax.all_gather(vectors, ('seq', 'blk'), axis=1, tiled=True)  71.2 us
  transfers between devices with their start and end apart: 10, of which 7 were waited for; matrix products, arithmetic and copies ran while one was open for 14% of the time, Pallas kernels for 0%

commit v1 on v0

v1 whole, which is shorter than its diff:
```python
import functools

import jax
import jax.numpy as jnp
from jax import lax
from jax.experimental import pallas as pl
from jax.experimental.pallas import tpu as pltpu
from jax.sharding import PartitionSpec as P

HEAD = 64
PASSES = 5
PASS_SLOTS = 512

masked_value = -1e30
both = ("seq", "blk")
f32 = jnp.float32
bf16 = jnp.bfloat16


def layer_norm(values, gain, offset):
    centre = values - jnp.mean(values, axis=-1, keepdims=True)
    spread = jnp.mean(centre * centre, axis=-1, keepdims=True)
    return centre * lax.rsqrt(spread + 1e-05) * gain + offset


def gelu_tanh(values):
    return jax.nn.gelu(values, approximate=True)


def contract(left, right, dims):
    return lax.dot_general(left, right, (dims, ((), ())), preferred_element_type=f32)


def tile_visible(length):
    key_place = lax.broadcasted_iota(jnp.int32, (PASS_SLOTS, PASS_SLOTS), 0)
    query_place = lax.broadcasted_iota(jnp.int32, (PASS_SLOTS, PASS_SLOTS), 1)
    return (key_place <= query_place) & (key_place < length)


def head_only(rows, head):
    lanes = lax.broadcasted_iota(jnp.int32, rows.shape, 1)
    return jnp.where(lanes // HEAD == head, rows, jnp.zeros_like(rows))


def forward_kernel(lengths, packed, out, totals, value_t):
    width = out.shape[1]
    heads = width // HEAD
    value_t[...] = packed[:, 2 * width :].astype(f32).T.astype(bf16)

    def query_pass(query_index, _):
        query_rows = pl.ds(query_index * PASS_SLOTS, PASS_SLOTS)
        queries = packed[query_rows, :width]
        queries = [head_only(queries, h) * jnp.asarray(0.125, bf16) for h in range(heads)]

        def key_pass(key_index, carried):
            start = pl.multiple_of(key_index * PASS_SLOTS, PASS_SLOTS)
            key_rows = pl.ds(start, PASS_SLOTS)
            keys = packed[key_rows, width : 2 * width]
            shown = tile_visible(lengths[0, key_index])
            updated = []
            for h in range(heads):
                top, total, acc = carried[h]
                scores = contract(keys, queries[h], ((1,), (1,)))
                scores = jnp.where(shown, scores, masked_value)
                newest = jnp.maximum(top, jnp.max(scores, axis=0, keepdims=True))
                shares = jnp.exp(scores - newest)
                fade = jnp.exp(top - newest)
                total = total * fade + jnp.sum(shares, axis=0, keepdims=True)
                values = value_t[h * HEAD : (h + 1) * HEAD, key_rows]
                acc = acc * fade + contract(values, shares.astype(bf16), ((1,), (0,)))
                updated.append((newest, total, acc))
            return tuple(updated)

        empty = (
            jnp.full((1, PASS_SLOTS), masked_value, f32),
            jnp.zeros((1, PASS_SLOTS), f32),
            jnp.zeros((HEAD, PASS_SLOTS), f32),
        )
        found = lax.fori_loop(0, query_index + 1, key_pass, (empty,) * heads)
        mixed = jnp.concatenate([acc / total for _, total, acc in found], axis=0)
        out[query_rows, :] = mixed.T.astype(bf16)
        for h, (top, total, _) in enumerate(found):
            totals[pl.ds(query_index, 1), h, :] = top + jnp.log(total)
        return 0

    lax.fori_loop(0, PASSES, query_pass, 0)


def backward_kernel(lengths, packed, mixed, grad, totals, out, grad_query, grad_key, grad_value):
    width = mixed.shape[1]
    heads = width // HEAD
    grad_query[...] = jnp.zeros_like(grad_query)
    eighth = jnp.asarray(0.125, bf16)

    def key_pass(key_index, _):
        key_rows = pl.ds(pl.multiple_of(key_index * PASS_SLOTS, PASS_SLOTS), PASS_SLOTS)
        keys = packed[key_rows, width : 2 * width] * eighth
        values = packed[key_rows, 2 * width :]
        keys = [head_only(keys, h) for h in range(heads)]
        values = [head_only(values, h) for h in range(heads)]
        shown = tile_visible(lengths[0, key_index])
        grad_key[...] = jnp.zeros_like(grad_key)
        grad_value[...] = jnp.zeros_like(grad_value)

        def query_pass(query_index, _):
            query_rows = pl.ds(pl.multiple_of(query_index * PASS_SLOTS, PASS_SLOTS), PASS_SLOTS)
            queries = packed[query_rows, :width]
            grads = grad[query_rows, :]
            product = (grads.astype(f32) * mixed[query_rows, :].astype(f32)).T
            scaled = queries * eighth
            add_query = add_key = add_value = 0.0
            for h in range(heads):
                delta = jnp.sum(product[h * HEAD : (h + 1) * HEAD], axis=0, keepdims=True)
                scores = contract(keys[h], queries, ((1,), (1,)))
                total = totals[pl.ds(query_index, 1), h, :]
                shares = jnp.where(shown, jnp.exp(scores - total), 0.0)
                grad_shares = contract(values[h], grads, ((1,), (1,)))
                grad_scores = (shares * (grad_shares - delta)).astype(bf16)
                add_value += contract(shares.astype(bf16), head_only(grads, h), ((1,), (0,)))
                add_key += contract(grad_scores, head_only(scaled, h), ((1,), (0,)))
                add_query += contract(grad_scores, keys[h], ((0,), (0,)))
            grad_query[query_rows, :] += add_query
            grad_key[...] += add_key
            grad_value[...] += add_value
            return 0

        lax.fori_loop(key_index, PASSES, query_pass, 0)
        out[key_rows, width : 2 * width] = grad_key[...].astype(bf16)
        out[key_rows, 2 * width :] = grad_value[...].astype(bf16)
        return 0

    lax.fori_loop(0, PASSES, key_pass, 0)
    out[:, :width] = grad_query[...].astype(bf16)


in_vmem = functools.partial(pl.BlockSpec, memory_space=pltpu.VMEM)
in_smem = functools.partial(pl.BlockSpec, memory_space=pltpu.SMEM)


def attend(lengths, packed):
    slots, triple = packed.shape
    width = triple // 3
    return pl.pallas_call(
        forward_kernel,
        out_shape=(
            jax.ShapeDtypeStruct((slots, width), bf16),
            jax.ShapeDtypeStruct((PASSES, width // HEAD, PASS_SLOTS), f32),
        ),
        in_specs=[in_smem(), in_vmem()],
        out_specs=(in_vmem(), in_vmem()),
        scratch_shapes=[pltpu.VMEM((width, slots), bf16)],
        compiler_params=pltpu.CompilerParams(vmem_limit_bytes=48 << 20),
        name="attend",
    )(lengths, packed)


def attend_back(lengths, packed, mixed, grad, totals):
    slots, width = mixed.shape
    return pl.pallas_call(
        backward_kernel,
        out_shape=jax.ShapeDtypeStruct(packed.shape, bf16),
        in_specs=[in_smem(), in_vmem(), in_vmem(), in_vmem(), in_vmem()],
        out_specs=in_vmem(),
        scratch_shapes=[
            pltpu.VMEM((slots, width), f32),
            pltpu.VMEM((PASS_SLOTS, width), f32),
            pltpu.VMEM((PASS_SLOTS, width), f32),
        ],
        compiler_params=pltpu.CompilerParams(vmem_limit_bytes=48 << 20),
        name="attend_back",
    )(lengths, packed, mixed, grad, totals)


def by_group(rows, groups):
    count, triple = rows.shape
    return rows.reshape(count, 3, groups, -1).swapaxes(1, 2).reshape(count, triple)


def by_kind(rows, groups):
    count, triple = rows.shape
    return rows.reshape(count, groups, 3, -1).swapaxes(1, 2).reshape(count, triple)


def to_heads(rows):
    return lax.all_to_all(rows, "blk", 1, 0, tiled=True)


def to_slots(rows):
    return lax.all_to_all(rows, "blk", 0, 1, tiled=True)


def norm_back(values, gain, grad):
    centre = values - jnp.mean(values, axis=-1, keepdims=True)
    spread = jnp.mean(centre * centre, axis=-1, keepdims=True)
    scale = lax.rsqrt(spread + 1e-05)
    hat = centre * scale
    edge = grad * gain
    part = scale * (
        edge
        - jnp.mean(edge, axis=-1, keepdims=True)
        - hat * jnp.mean(edge * hat, axis=-1, keepdims=True)
    )
    return part, jnp.sum(grad * hat, axis=0), jnp.sum(grad, axis=0)


def on_device(states, cotangent, lengths, w_qkv, w_out, w_up, w_down, vectors, up_bias):
    _, row_count, width = states.shape
    groups = lax.axis_size("blk")
    own = w_qkv.shape[0]
    wide = w_up.shape[1]
    ratio = wide // width
    vector_count = vectors.shape[0]
    first = jnp.concatenate(
        [
            by_group(w_qkv, groups),
            vectors.T,
            up_bias.reshape(own, ratio),
            jnp.zeros((own, 128 - vector_count - ratio), bf16),
        ],
        axis=1,
    )
    first = lax.all_gather(first, both, axis=0, tiled=True)
    second = jnp.concatenate([w_out, w_up, w_down.reshape(own, wide)], axis=1)
    second, _ = lax.optimization_barrier((second, first[:8, :128]))
    second = lax.all_gather(second, both, axis=0, tiled=True)
    full_qkv = first[:, : 3 * width]
    table = first[:, 3 * width : 3 * width + vector_count].astype(f32).T
    bias_up = first[:, 3 * width + vector_count : 3 * width + vector_count + ratio]
    bias_up = bias_up.astype(f32).reshape(wide)
    full_out = second[:, :width]
    full_up = second[:, width : width + wide]
    full_down = second[:, width + wide :].reshape(wide, width)

    slots = lax.axis_index("blk") * row_count + jnp.arange(row_count, dtype=jnp.int32)
    pass_of = (slots // PASS_SLOTS)[:, None] == jnp.arange(PASSES, dtype=jnp.int32)[None, :]
    bounds = jnp.sum(jnp.where(pass_of, lengths[0][None, :], 0), axis=1)
    live = (slots % PASS_SLOTS < bounds).astype(f32)[:, None]
    pass_table = pass_of.astype(f32)

    added = jnp.zeros((row_count, width), f32)
    for index in range(PASSES):
        added = jnp.where(pass_of[:, index : index + 1], table[index], added)
    start = states[0].astype(f32) + added
    normed_a = layer_norm(start, table[5], table[6]).astype(bf16)
    bias_three = jnp.concatenate([table[7], jnp.zeros_like(table[7]), table[8]])
    bias_three = by_group(bias_three[None], groups)
    projected = (contract(normed_a, full_qkv, ((1,), (0,))) + bias_three).astype(bf16)
    packed = to_heads(projected)
    mixed, totals = attend(lengths, packed)
    heads_out = to_slots(mixed)
    middle = start + live * (contract(heads_out, full_out, ((1,), (0,))) + table[9])
    normed_b = layer_norm(middle, table[10], table[11]).astype(bf16)
    up_sum = contract(normed_b, full_up, ((1,), (0,))) + bias_up
    activated, gelu_pull = jax.vjp(gelu_tanh, up_sum)
    hidden = activated.astype(bf16)
    outcome = middle + live * (contract(hidden, full_down, ((1,), (0,))) + table[12])

    incoming = cotangent[0].astype(f32)
    grad_branch = (live * incoming).astype(bf16)
    grad_down = contract(hidden, grad_branch, ((0,), (0,)))
    grad_hidden = contract(grad_branch, full_down, ((1,), (1,)))
    grad_upsum = gelu_pull(grad_hidden)[0].astype(bf16)
    grad_up = contract(normed_b, grad_upsum, ((0,), (0,)))
    grad_normb = contract(grad_upsum, full_up, ((1,), (1,)))
    middle_part, gain_grad_b, shift_grad_b = norm_back(middle, table[10], grad_normb)
    grad_middle = incoming + middle_part
    grad_attn = (live * grad_middle).astype(bf16)
    grad_out = contract(heads_out, grad_attn, ((0,), (0,)))
    grad_heads = contract(grad_attn, full_out, ((1,), (1,))).astype(bf16)
    late = jnp.concatenate(
        [grad_out.astype(bf16), grad_up.astype(bf16), grad_down.astype(bf16).reshape(width, wide)],
        axis=1,
    )
    late = lax.psum_scatter(late, both, scatter_dimension=0, tiled=True)

    grad_packed = attend_back(lengths, packed, mixed, to_heads(grad_heads), totals)
    grad_projected = to_slots(grad_packed)
    grad_qkv = contract(normed_a, grad_projected, ((0,), (0,)))
    column_sums = by_kind(jnp.sum(grad_projected.astype(f32), axis=0)[None], groups)[0]
    grad_norma = contract(grad_projected, full_qkv, ((1,), (1,)))
    start_part, gain_grad_a, shift_grad_a = norm_back(start, table[5], grad_norma)
    grad_start = grad_middle + start_part
    grad_embed = [
        jnp.sum(jnp.where(pass_of[:, index : index + 1], grad_start, 0.0), axis=0)
        for index in range(PASSES)
    ]
    vector_grads = jnp.stack(
        grad_embed
        + [
            gain_grad_a,
            shift_grad_a,
            column_sums[:width],
            column_sums[2 * width :],
            jnp.sum(grad_attn.astype(f32), axis=0),
            gain_grad_b,
            shift_grad_b,
            jnp.sum(grad_branch.astype(f32), axis=0),
        ]
    )
    bias_grads = jnp.sum(grad_upsum.astype(f32), axis=0)
    last = jnp.concatenate(
        [
            grad_qkv.astype(bf16),
            vector_grads.T.astype(bf16),
            bias_grads.reshape(width, ratio).astype(bf16),
            jnp.zeros((width, 128 - vector_count - ratio), bf16),
        ],
        axis=1,
    )
    last = lax.psum_scatter(last, both, scatter_dimension=0, tiled=True).astype(f32)
    late = late.astype(f32)
    edge = 3 * width + vector_count
    return (
        outcome.astype(bf16)[None],
        grad_start.astype(bf16)[None],
        by_kind(last[:, : 3 * width], groups),
        late[:, :width],
        late[:, width : width + wide],
        late[:, width + wide :].reshape(own * ratio, width),
        last[:, 3 * width : edge].T,
        last[:, edge : edge + ratio].reshape(own * ratio),
    )


def solution(mesh):
    split = P(both, None)
    return jax.shard_map(
        on_device,
        mesh=mesh,
        in_specs=(
            P("seq", "blk", None),
            P("seq", "blk", None),
            P("seq", None),
            split,
            split,
            split,
            split,
            P(None, both),
            P(both),
        ),
        out_specs=(
            P("seq", "blk", None),
            P("seq", "blk", None),
            split,
            split,
            split,
            split,
            P(None, both),
            P(both),
        ),
        check_vma=False,
    )
```

time: 1330 us -> 739 us (0.56)
  waiting for transfers between devices: 774 us -> 336 us
  matrix products: 169 us -> 78.7 us
  local copies, waits for them, and re-layouts: 138 us -> 69 us
  Pallas kernels: 0 us -> 66.2 us
  loops' own time: 31.1 us -> 0 us
  other arithmetic: 37.2 us -> 17.6 us
  blocking collectives: 157 us -> 140 us
    reduce_scatter x4 -> x1, waiting for transfers between devices: 430 us -> 142 us  [on_device(): late = lax.psum_scatter(late, both, scatter_dimension=0, tiled=True)]
    unnamed x11 -> x5, waiting for transfers between devices: 205 us -> 45 us
    all_to_all x0 -> x2, blocking collectives: none -> 140 us  [to_heads(): return lax.all_to_all(rows, 'blk', 1, 0, tiled=True)]
    dot_general x28 -> x12, matrix products: 169 us -> 78.7 us  [contract(): lax.dot_general(left, right, (dims, ((), ())), preferred_element_type=f32)]
    all_to_all x0 -> x2, waiting for transfers between devices: none -> 88.2 us  [to_slots(): return lax.all_to_all(rows, 'blk', 0, 1, tiled=True)]
    unnamed x2 -> x0, blocking collectives: 85.6 us -> none
    all_gather x5 -> x2, waiting for transfers between devices: 138 us -> 61.2 us  [the longest x1 61.2 us: on_device(): first = lax.all_gather(first, both, axis=0, tiled=True)]
    unnamed x137 -> x48, local copies, waits for them, and re-layouts: 80.3 us -> 7.13 us
  transfers between devices with their start and end apart: 10 -> 6, of which waited for: 7 -> 5; matrix products, arithmetic and copies ran while one was open for 14% -> 11% of each run, Pallas kernels for 0% -> 4%
where the time goes in v1:
time: 739 us; the launch traced here: 730 us
  waiting for transfers between devices  336 us (45%)
  blocking collectives  140 us (19%)
  matrix products  78.7 us (11%)
  local copies, waits for them, and re-layouts  69 us (9%)
  Pallas kernels  66.2 us (9%)
  other arithmetic  17.6 us (2%)
  between operations  14.5 us (2%)
  starting transfers between devices  7.74 us (1%)
    reduce_scatter x1, waiting for transfers between devices, on_device(): late = lax.psum_scatter(late, both, scatter_dimension=0, tiled=True)  142 us
    all_to_all x2, blocking collectives, to_heads(): return lax.all_to_all(rows, 'blk', 1, 0, tiled=True)  140 us
    all_to_all x2, waiting for transfers between devices, to_slots(): return lax.all_to_all(rows, 'blk', 0, 1, tiled=True)  88.2 us
    dot_general x12, matrix products, contract(): lax.dot_general(left, right, (dims, ((), ())), preferred_element_type=f32)  78.7 us
    all_gather x1, waiting for transfers between devices, on_device(): first = lax.all_gather(first, both, axis=0, tiled=True)  61.2 us
    unnamed x5, waiting for transfers between devices  45 us
    pallas_call x1, Pallas kernels, attend_back(): pl.pallas_call(backward_kernel, out_shape=jax.ShapeDtypeStruct(packed.sha...  40 us
    pallas_call x1, Pallas kernels, attend(): pl.pallas_call(forward_kernel, out_shape=(jax.ShapeDtypeStruct((slots, wi...  26.3 us
  transfers between devices with their start and end apart: 6, of which 5 were waited for; matrix products, arithmetic and copies ran while one was open for 11% of the time, Pallas kernels for 4%

profile of v1, /device:TPU:0, one launch (start us, length us, event | category | flops | bytes accessed | tf_op | source)
XLA Modules:
  0.0 730.3 jit_solution(17209307263439118572)
XLA Ops:
  7.2 0.8 copy.72
  8.0 0.7 reshape.461
  8.7 1.1 reshape.459
  10.1 0.7 concatenate.15
  10.9 1.0 reshape.462
  11.9 1.7 pad_maximum_fusion.1
  13.7 61.2 %all-gather.3.cloned.1.call-done = bf16[768,2432]{1,0:T(8,128)(2,1)} async-done(((bf16[24,2432]{1,0:T(8,128)(2,1)}), bf16[768,2432]{1,0:T(8,128)(2,1)}) %all-gather.3.cloned.1.call-update) | async-done | bytes 3735568 | tf_op jit(solution)/shard_map/all_gather | solution.py:222
  74.9 1.0 convert_bitcast_fusion.3
  75.9 2.6 slice_reduce_fusion.2
  78.7 0.8 fusion.25
  79.5 0.9 multiply_reduce_fusion.5
  80.5 6.8 add_convert_fusion
  87.3 4.1 copy.74
  91.4 113.3 %all_to_all.76 = bf16[640,4,576]{0,2,1:T(8,128)(2,1)} all-to-all(bf16[640,4,576]{0,2,1:T(8,128)(2,1)S(1)} %bitcast.97), channel_id=1, replica_groups=mesh['seq'=8,'blk'=4] {'blk'}, dimensions={1} | all-to-all | bytes 5898240 | tf_op jit(solution)/shard_map/all_to_all | solution.py:185
  204.8 3.4 copy.75
  208.2 26.3 %attend.1 = (bf16[2560,192]{1,0:T(8,128)(2,1)S(1)}, f32[5,3,512]{2,1,0:T(4,128)S(1)}) custom-call(s32[1,5]{1,0:T(1,128)S(1)} %copy-done.4, bf16[2560,576]{1,0:T(8,128)(2,1)S(1)} %bitcast.87), custom_call_target="tpu_custom_call" | custom-call | tf_op jit(solution)/shard_map/attend/pallas_call | solution.py:143
  234.5 1.1 copy-done.1
  235.6 2.3 copy.76
  237.9 3.7 all-to-all-start.1
  241.8 1.0 slice_convert_fusion
  243.0 23.0 %all-to-all-done.1 = bf16[4,640,192]{1,2,0:T(8,128)(2,1)S(1)} async-done(((bf16[4,640,192]{1,2,0:T(8,128)(2,1)}), bf16[4,640,192]{1,2,0:T(8,128)(2,1)S(1)}, u32[]{:S(2)}, u32[]{:S(2)}) %all-to-all-start.1) | async-done | bytes 983072 | tf_op jit(solution)/shard_map/all_to_all | solution.py:189
  266.0 3.5 fusion.66
  269.9 5.2 slice.162
  275.1 8.4 %reshape.463 = bf16[3072,768]{1,0:T(8,128)(2,1)} reshape(bf16[768,3072]{1,0:T(8,128)(2,1)} %slice.162) | data formatting | bytes 9437184 | tf_op jit(solution)/shard_map/reshape | solution.py:232
  283.6 8.1 %fusion.9 = f32[640,3072]{1,0:T(8,128)} fusion(bf16[768,6912]{1,0:T(8,128)(2,1)} %all-gather.5.cloned.1.call-done, f32[640,768]{1,0:T(8,128)S(1)} %get-tuple-element.85, f32[768]{0:T(1024)S(1)} %get-tuple-element.59, f32[768]{0:T(1024)S(1)} %get-tuple-element.57, f32[640]{0:T(1024)S(1)} %add_rsqrt_fusion, f32[640]{0:T(1024)S(1)} %broadcast_multiply_fusion.4), kind=kOutput, calls=%fused_computation.17 | convolution fusion | flops 3022356480 | bytes 14560256 | tf_op jit(solution)/shard_map/dot_general | solution.py:31
  291.6 11.4 %fusion.67 = (bf16[3072]{0:T(1024)(128)(2,1)S(1)}, bf16[640,3072]{1,0:T(8,128)(2,1)}) fusion(f32[640,3072]{1,0:T(8,128)} %fusion.9, f32[3072]{0:T(1024)S(1)} %reshape.470, bf16[3072,768]{1,0:T(8,128)(2,1)S(1)} %copy-done.10, bf16[1,640,768]{2,1,0:T(8,128)(2,1)S(1)} %copy-done.12, f32[640]{0:T(1024)S(1)} %fusion.61), kind=kOutput, calls=%fused_computation.141 | convolution fusion | flops 3064624128 | bytes 17519104 | tf_op jit(solution)/shard_map/dot_general | solution.py:31
  303.1 5.8 multiply_reduce_fusion
  308.9 2.2 fusion.63
  311.0 0.9 copy-done.16
  312.0 1.0 convolution_convert_fusion.4
  312.9 0.6 copy.77
  313.6 26.7 %all_to_all.77 = bf16[640,4,192]{0,2,1:T(8,128)(2,1)S(1)} all-to-all(bf16[640,4,192]{0,2,1:T(8,128)(2,1)S(1)} %bitcast.99), channel_id=1, replica_groups=mesh['seq'=8,'blk'=4] {'blk'}, dimensions={1} | all-to-all | bytes 1966080 | tf_op jit(solution)/shard_map/all_to_all | solution.py:185
  340.3 1.4 copy.78
  341.7 1.3 copy-done.2
  343.0 1.3 copy-done.3
  344.4 40.0 %attend_back.1 = bf16[2560,576]{1,0:T(8,128)(2,1)S(1)} custom-call(s32[1,5]{1,0:T(1,128)S(1)} %copy-done.4, bf16[2560,576]{1,0:T(8,128)(2,1)} %bitcast.88, bf16[2560,192]{1,0:T(8,128)(2,1)S(1)} %copy-done.2, bf16[2560,192]{1,0:T(8,128)(2,1)S(1)} %bitcast.91, f32[5,3,512]{2,1,0:T(4,128)S(1)} %get-tuple-element.11.totals), custom_call_target="tpu_custom_call" | custom-call | tf_op jit(solution)/shard_map/attend_back/pallas_call | solution.py:159
  384.3 2.9 copy.79
  387.2 3.7 all-to-all-start.3
  391.0 0.4 convert_element_type.130
  391.5 65.2 %all-to-all-done.3 = bf16[4,640,576]{1,2,0:T(8,128)(2,1)S(1)} async-done(((bf16[4,640,576]{1,2,0:T(8,128)(2,1)}), bf16[4,640,576]{1,2,0:T(8,128)(2,1)S(1)}, u32[]{:S(2)}, u32[]{:S(2)}) %all-to-all-start.3) | async-done | bytes 2949152 | tf_op jit(solution)/shard_map/all_to_all | solution.py:189
  456.6 7.1 convolution_convert_fusion.2
  463.8 3.7 multiply_reduce_fusion.1
  467.5 3.5 select_reduce_fusion
  471.1 0.5 bitcast_reduce_fusion
  472.1 6.6 concatenate.18
  478.9 1.0 copy-done.13
  479.9 10.7 %convolution_convert_fusion = bf16[3072,768]{1,0:T(8,128)(2,1)} fusion(bf16[1,640,768]{2,1,0:T(8,128)(2,1)S(1)} %copy-done.13, f32[640]{0:T(1024)S(1)} %fusion.61, f32[640,3072]{1,0:T(8,128)} %fusion.9, f32[3072]{0:T(1024)S(1)} %reshape.470), kind=kOutput, calls=%fused_computation.12 | convolution fusion | flops 3043393536 | bytes 13580800 | tf_op jit(solution)/shard_map/dot_general | solution.py:31
  490.6 9.0 %reshape.466 = bf16[768,3072]{1,0:T(8,128)(2,1)} reshape(bf16[3072,768]{1,0:T(8,128)(2,1)} %convolution_convert_fusion) | data formatting | bytes 9437184 | tf_op jit(solution)/shard_map/reshape | solution.py:271
  499.5 3.6 convolution_convert_fusion.3
  503.1 2.5 copy.82
  505.6 6.7 convolution_convert_fusion.1
  512.3 4.6 pad_maximum_fusion
  517.0 10.4 %fusion.24 = bf16[1,640,768]{2,1,0:T(8,128)(2,1)} fusion(f32[640,768]{1,0:T(8,128)S(1)} %copy-done.8, bf16[3072,768]{1,0:T(8,128)(2,1)} %reshape.463, f32[768]{0:T(1024)S(1)} %get-tuple-element.58, f32[640]{0:T(1024)S(1)} %fusion.61, f32[640,3072]{1,0:T(8,128)} %fusion.9, f32[3072]{0:T(1024)S(1)} %reshape.470), kind=kOutput, calls=%fused_computation.60 | convolution fusion | flops 3041525760 | bytes 15549952 | tf_op jit(solution)/shard_map/dot_general | solution.py:31
  527.4 44.9 %reduce-scatter.7.cloned.1.call-done = bf16[24,2432]{1,0:T(8,128)(2,1)} async-done(((bf16[768,2432]{1,0:T(8,128)(2,1)}), bf16[24,2432]{1,0:T(8,128)(2,1)}) %reduce-scatter.7.cloned.1.call-update) | async-done | bytes 116752
  572.3 0.8 slice.171
  573.1 0.6 reshape.468
  573.7 0.9 convert_element_type.131
  574.6 0.7 copy.83
  575.3 0.9 slice.166
  576.6 0.9 reshape.465
  577.5 142.1 %reduce-scatter.5.cloned.1.call-done = bf16[24,6912]{1,0:T(8,128)(2,1)} async-done(((bf16[768,6912]{1,0:T(8,128)(2,1)}), bf16[24,6912]{1,0:T(8,128)(2,1)}) %reduce-scatter.5.cloned.1.call-update) | async-done | bytes 331792 | tf_op jit(solution)/shard_map/reduce_scatter | solution.py:274
  719.6 1.7 fusion.65
  721.3 0.8 reshape.467
  722.1 1.4 slice.167
  (95 shorter events, 2.7 us)
Async XLA Ops:
  7.2 67.7 %all-gather.3.cloned.1.call-start = ((), (), s32[]{:S(2)}) async-start(), calls=%async_computation.6 | async-start | bytes 3852288 | tf_op jit(solution)/shard_map/all_gather | solution.py:222
  10.9 255.1 %all-gather.5.cloned.1.call-start = ((), (), s32[]{:S(2)}) async-start(), calls=%async_computation.7 | async-start | bytes 10948608 | tf_op jit(solution)/shard_map/all_gather | solution.py:225
  75.8 2.8 copy-start.5
  204.8 3.5 copy-start.4
  208.2 29.7 %copy-start = (bf16[4,640,576]{2,1,0:T(8,128)(2,1)}, bf16[4,640,576]{2,1,0:T(8,128)(2,1)S(1)}, u32[]{:S(2)}) copy-start(bf16[4,640,576]{2,1,0:T(8,128)(2,1)S(1)} %copy.75) | copy-start | bytes 8847364
  234.5 1.1 copy-start.1
  237.9 28.1 %all-to-all-start.1 = ((bf16[4,640,192]{1,2,0:T(8,128)(2,1)}), bf16[4,640,192]{1,2,0:T(8,128)(2,1)S(1)}, u32[]{:S(2)}, u32[]{:S(2)}) async-start(bf16[4,640,192]{1,2,0:T(8,128)(2,1)} %copy.76), calls=%async_computation.1 | async-start | bytes 1966080 | tf_op jit(solution)/shard_map/all_to_all | solution.py:189
  266.0 3.5 copy-start.14
  269.5 39.3 %copy-start.7 = (f32[640,768]{1,0:T(8,128)}, f32[640,768]{1,0:T(8,128)S(1)}, u32[]{:S(2)}) copy-start(f32[640,768]{1,0:T(8,128)S(1)} %get-tuple-element.85) | copy-start | bytes 5898244
  283.5 8.1 %copy-start.10 = (bf16[3072,768]{1,0:T(8,128)(2,1)S(1)}, bf16[3072,768]{1,0:T(8,128)(2,1)}, u32[]{:S(2)}) copy-start(bf16[3072,768]{1,0:T(8,128)(2,1)} %reshape.463) | copy-start | bytes 14155780
  283.6 8.1 %copy-start.12 = (bf16[1,640,768]{2,1,0:T(8,128)(2,1)S(1)}, bf16[1,640,768]{2,1,0:T(8,128)(2,1)}, u32[]{:S(2)}) copy-start(bf16[1,640,768]{2,1,0:T(8,128)(2,1)} %param.10) | copy-start | bytes 2949124
  283.6 19.5 %slice-start.2 = ((s8[10616832]{0:T(1024)(128)(4,1)}), s8[4194304]{0:T(1024)(128)(4,1)S(1)}, s32[]{:S(2)}) async-start(s8[10616832]{0:T(1024)(128)(4,1)} %bitcast.101), calls=%async_computation.12 | async-start | bytes 8388608
  291.6 11.4 %slice-start.3 = ((s8[10616832]{0:T(1024)(128)(4,1)}), s8[4194304]{0:T(1024)(128)(4,1)S(1)}, s32[]{:S(2)}) async-start(s8[10616832]{0:T(1024)(128)(4,1)} %bitcast.101), calls=%async_computation.13 | async-start | bytes 8388608
  291.6 11.4 %slice-start.4 = ((s8[10616832]{0:T(1024)(128)(4,1)}), s8[2228224]{0:T(1024)(128)(4,1)S(1)}, s32[]{:S(2)}) async-start(s8[10616832]{0:T(1024)(128)(4,1)} %bitcast.101), calls=%async_computation.14 | async-start | bytes 4456448
  311.0 0.9 copy-start.16
  341.7 1.3 copy-start.2
  343.0 1.3 copy-start.3
  387.2 69.4 %all-to-all-start.3 = ((bf16[4,640,576]{1,2,0:T(8,128)(2,1)}), bf16[4,640,576]{1,2,0:T(8,128)(2,1)S(1)}, u32[]{:S(2)}, u32[]{:S(2)}) async-start(bf16[4,640,576]{1,2,0:T(8,128)(2,1)} %copy.79), calls=%async_computation.3 | async-start | bytes 5898240 | tf_op jit(solution)/shard_map/all_to_all | solution.py:189
  390.9 181.4 %reduce-scatter.7.cloned.1.call-start = ((), (), s32[]{:S(2)}) async-start(), calls=%async_computation.9 | async-start | bytes 3852288
  456.6 7.1 copy-start.6
  456.6 7.1 copy-start.17
  463.8 3.8 copy-start.9
  478.7 1.2 copy-start.13
  478.7 240.9 %reduce-scatter.5.cloned.1.call-start = ((), (), s32[]{:S(2)}) async-start(), calls=%async_computation.8 | async-start | bytes 10948608 | tf_op jit(solution)/shard_map/reduce_scatter | solution.py:274
  490.6 9.0 %copy-start.15 = (bf16[4,640,192]{1,2,0:T(8,128)(2,1)S(1)}, bf16[4,640,192]{1,2,0:T(8,128)(2,1)}, u32[]{:S(2)}) copy-start(bf16[4,640,192]{1,2,0:T(8,128)(2,1)} %copy-done.14) | copy-start | bytes 2949124
  499.5 6.0 copy-start.8
  503.1 9.2 %slice-start = ((s8[4718592]{0:T(1024)(128)(4,1)}), s8[524288]{0:T(1024)(128)(4,1)S(1)}, s32[]{:S(2)}) async-start(s8[4718592]{0:T(1024)(128)(4,1)} %bitcast.93), calls=%async_computation.10 | async-start | bytes 1048576
  505.6 6.7 slice-start.1
  505.6 6.7 copy-start.11
Sparse Core Ops, SparseCore 0:
  11.4 63.4 all-gather.2
  77.7 124.7 all-gather.4
  478.8 93.4 reduce-scatter.6
  578.3 141.2 reduce-scatter.4

commit v2 on v1

--- a/solution.py
+++ b/solution.py
@@ -4,12 +4,14 @@
 import jax.numpy as jnp
 from jax import lax
 from jax.experimental import pallas as pl
+from jax.experimental.layout import Layout, with_layout_constraint
 from jax.experimental.pallas import tpu as pltpu
 from jax.sharding import PartitionSpec as P
 
 HEAD = 64
 PASSES = 5
 PASS_SLOTS = 512
+SPLIT = 2
 
 masked_value = -1e30
 both = ("seq", "blk")
@@ -42,9 +44,18 @@
     return jnp.where(lanes // HEAD == head, rows, jnp.zeros_like(rows))
 
 
-def forward_kernel(lengths, packed, out, totals, value_t):
+def place_pieces(here, pieces, whole):
+    rows = pieces[0].shape[0]
+    for step, piece in enumerate(pieces):
+        at = pl.multiple_of((here ^ step) * rows, rows)
+        whole[pl.ds(at, rows), :] = piece[...]
+
+
+def forward_kernel(lengths, here, *refs):
+    packed, out, totals, value_t = refs[-4:]
     width = out.shape[1]
     heads = width // HEAD
+    place_pieces(here[0], refs[:-4], packed)
     value_t[...] = packed[:, 2 * width :].astype(f32).T.astype(bf16)
 
     def query_pass(query_index, _):
@@ -86,10 +97,33 @@
     lax.fori_loop(0, PASSES, query_pass, 0)
 
 
-def backward_kernel(lengths, packed, mixed, grad, totals, out, grad_query, grad_key, grad_value):
+def first_backward_kernel(lengths, here, packed, mixed, totals, *refs):
+    out, grad, grad_query, grad_key, grad_value = refs[-5:]
+    place_pieces(here[0], refs[:-5], grad)
+    grad_query[...] = jnp.zeros_like(grad_query)
+    backward_passes(
+        0, SPLIT, lengths, packed, mixed, grad, totals, out, grad_query, grad_key, grad_value
+    )
+
+
+def second_backward_kernel(
+    lengths, packed, mixed, totals, grad, begun, query_in, out, grad_query, grad_key, grad_value
+):
+    width = mixed.shape[1]
+    grad_query[...] = query_in[...]
+    out[: SPLIT * PASS_SLOTS, width:] = begun[...]
+    backward_passes(
+        SPLIT, PASSES, lengths, packed, mixed, grad, totals, out, grad_query, grad_key, grad_value
+    )
+    out[:, :width] = grad_query[...].astype(bf16)
+
+
+def backward_passes(
+    first, last, lengths, packed, mixed, grad, totals, out, grad_query, grad_key, grad_value
+):
     width = mixed.shape[1]
     heads = width // HEAD
-    grad_query[...] = jnp.zeros_like(grad_query)
+    offset = out.shape[1] - 3 * width
     eighth = jnp.asarray(0.125, bf16)
 
     def key_pass(key_index, _):
@@ -125,41 +159,62 @@
             return 0
 
         lax.fori_loop(key_index, PASSES, query_pass, 0)
-        out[key_rows, width : 2 * width] = grad_key[...].astype(bf16)
-        out[key_rows, 2 * width :] = grad_value[...].astype(bf16)
+        out[key_rows, width + offset : 2 * width + offset] = grad_key[...].astype(bf16)
+        out[key_rows, 2 * width + offset :] = grad_value[...].astype(bf16)
         return 0
 
-    lax.fori_loop(0, PASSES, key_pass, 0)
-    out[:, :width] = grad_query[...].astype(bf16)
+    lax.fori_loop(first, last, key_pass, 0)
 
 
 in_vmem = functools.partial(pl.BlockSpec, memory_space=pltpu.VMEM)
 in_smem = functools.partial(pl.BlockSpec, memory_space=pltpu.SMEM)
 
 
-def attend(lengths, packed):
-    slots, triple = packed.shape
+def attend(lengths, here, pieces):
+    rows, triple = pieces[0].shape
+    slots = rows * len(pieces)
     width = triple // 3
     return pl.pallas_call(
         forward_kernel,
         out_shape=(
+            jax.ShapeDtypeStruct((slots, triple), bf16),
             jax.ShapeDtypeStruct((slots, width), bf16),
             jax.ShapeDtypeStruct((PASSES, width // HEAD, PASS_SLOTS), f32),
         ),
-        in_specs=[in_smem(), in_vmem()],
-        out_specs=(in_vmem(), in_vmem()),
+        in_specs=[in_smem(), in_smem()] + [in_vmem()] * len(pieces),
+        out_specs=(in_vmem(), in_vmem(), in_vmem()),
         scratch_shapes=[pltpu.VMEM((width, slots), bf16)],
         compiler_params=pltpu.CompilerParams(vmem_limit_bytes=48 << 20),
         name="attend",
-    )(lengths, packed)
-
-
-def attend_back(lengths, packed, mixed, grad, totals):
+    )(lengths, here, *pieces)
+
+
+def attend_back_first(lengths, here, packed, mixed, totals, pieces):
     slots, width = mixed.shape
     return pl.pallas_call(
-        backward_kernel,
+        first_backward_kernel,
+        out_shape=(
+            jax.ShapeDtypeStruct((SPLIT * PASS_SLOTS, 2 * width), bf16),
+            jax.ShapeDtypeStruct((slots, width), bf16),
+            jax.ShapeDtypeStruct((slots, width), f32),
+        ),
+        in_specs=[in_smem(), in_smem()] + [in_vmem()] * (3 + len(pieces)),
+        out_specs=(in_vmem(), in_vmem(), in_vmem()),
+        scratch_shapes=[
+            pltpu.VMEM((PASS_SLOTS, width), f32),
+            pltpu.VMEM((PASS_SLOTS, width), f32),
+        ],
+        compiler_params=pltpu.CompilerParams(vmem_limit_bytes=48 << 20),
+        name="attend_back_first",
+    )(lengths, here, packed, mixed, totals, *pieces)
+
+
+def attend_back_second(lengths, packed, mixed, totals, grad, begun, query_in):
+    slots, width = mixed.shape
+    return pl.pallas_call(
+        second_backward_kernel,
         out_shape=jax.ShapeDtypeStruct(packed.shape, bf16),
-        in_specs=[in_smem(), in_vmem(), in_vmem(), in_vmem(), in_vmem()],
+        in_specs=[in_smem()] + [in_vmem()] * 6,
         out_specs=in_vmem(),
         scratch_shapes=[
             pltpu.VMEM((slots, width), f32),
@@ -167,33 +222,130 @@
             pltpu.VMEM((PASS_SLOTS, width), f32),
         ],
         compiler_params=pltpu.CompilerParams(vmem_limit_bytes=48 << 20),
-        name="attend_back",
-    )(lengths, packed, mixed, grad, totals)
+        name="attend_back_second",
+    )(lengths, packed, mixed, totals, grad, begun, query_in)
+
+
+def row_major(values):
+    return with_layout_constraint(values, Layout(tuple(range(values.ndim))))
+
+
+def after(values, *others):
+    return lax.optimization_barrier((values, others))[0]
+
+
+def swap_with(values, axis, step):
+    size = lax.axis_size(axis)
+    return lax.ppermute(values, axis, [(i, i ^ step) for i in range(size)])
+
+
+def axis_bits(axis):
+    size = lax.axis_size(axis)
+    assert size & (size - 1) == 0
+    return [(axis, 1 << n) for n in reversed(range(size.bit_length() - 1))]
+
+
+def bit_order(flip):
+    places = axis_bits("seq") + axis_bits("blk")
+    near = axis_bits("seq")
+    far = near[:-1][::-1] if flip else near[:-1]
+    return places, axis_bits("blk") + far + near[-1:]
+
+
+def own_bit(bit):
+    return (lax.axis_index(bit[0]) & bit[1]) != 0
+
+
+class Gather:
+    def __init__(self, piece, flip):
+        self.places, self.order = bit_order(flip)
+        self.shape = piece.shape
+        self.piece = piece
+        self.done = []
+
+    def grow(self, count=None):
+        count = len(self.order) if count is None else count
+        for bit in self.order[:count]:
+            other = swap_with(self.piece, *bit)
+            self.done = sorted(self.done + [bit], key=self.places.index)
+            mine = own_bit(bit)
+            low = jnp.where(mine, other, self.piece)
+            high = jnp.where(mine, self.piece, other)
+            self.piece = jnp.stack([low, high], axis=self.done.index(bit))
+        self.order = self.order[count:]
+        return self.piece
+
+    def whole(self):
+        return self.grow().reshape((-1,) + self.shape[1:])
+
+
+class Scatter:
+    def __init__(self, whole, flip):
+        self.left, order = bit_order(flip)
+        self.order = order[::-1]
+        rows = whole.shape[0] >> len(order)
+        self.piece = whole.reshape((2,) * len(order) + (rows,) + whole.shape[1:])
+
+    def send(self):
+        bit, self.order = self.order[0], self.order[1:]
+        at = self.left.index(bit)
+        self.left = [place for place in self.left if place != bit]
+        low = lax.index_in_dim(self.piece, 0, at, keepdims=False)
+        high = lax.index_in_dim(self.piece, 1, at, keepdims=False)
+        mine = own_bit(bit)
+        self.bit = bit
+        self.sent = jnp.where(mine, low, high)
+        self.kept = jnp.where(mine, high, low)
+        return (self.sent, self.kept)
+
+    def receive(self):
+        other = swap_with(self.sent, *self.bit)
+        self.piece = (self.kept.astype(f32) + other.astype(f32)).astype(bf16)
+
+    def finish(self):
+        while self.order:
+            self.send()
+            self.receive()
+        return self.piece
+
+
+def swap_pieces(pieces):
+    return [swap_with(piece, "blk", step) if step else piece for step, piece in enumerate(pieces)]
+
+
+def in_order(pieces):
+    here = lax.axis_index("blk")
+    result = jnp.zeros((len(pieces),) + pieces[0].shape, pieces[0].dtype)
+    for step, piece in enumerate(pieces):
+        result = lax.dynamic_update_index_in_dim(result, piece, here ^ step, 0)
+    return result
+
+
+def at_group(values, group):
+    return lax.dynamic_index_in_dim(values, group, 0, keepdims=False)
 
 
 def by_group(rows, groups):
     count, triple = rows.shape
-    return rows.reshape(count, 3, groups, -1).swapaxes(1, 2).reshape(count, triple)
-
-
-def by_kind(rows, groups):
-    count, triple = rows.shape
-    return rows.reshape(count, groups, 3, -1).swapaxes(1, 2).reshape(count, triple)
-
-
-def to_heads(rows):
-    return lax.all_to_all(rows, "blk", 1, 0, tiled=True)
-
-
-def to_slots(rows):
-    return lax.all_to_all(rows, "blk", 0, 1, tiled=True)
-
-
-def norm_back(values, gain, grad):
+    rows = rows.reshape(count, 3, groups, -1)
+    return [rows[:, :, g].reshape(count, triple // groups) for g in range(groups)]
+
+
+def by_kind(parts):
+    count, columns = parts[0].shape
+    parts = [part.reshape(count, 3, columns // 3) for part in parts]
+    return jnp.concatenate(parts, axis=2).reshape(count, -1)
+
+
+def norm_parts(values):
     centre = values - jnp.mean(values, axis=-1, keepdims=True)
     spread = jnp.mean(centre * centre, axis=-1, keepdims=True)
     scale = lax.rsqrt(spread + 1e-05)
-    hat = centre * scale
+    return centre * scale, scale
+
+
+def norm_back(values, gain, grad):
+    hat, scale = norm_parts(values)
     edge = grad * gain
     part = scale * (
         edge
@@ -210,32 +362,39 @@
     wide = w_up.shape[1]
     ratio = wide // width
     vector_count = vectors.shape[0]
-    first = jnp.concatenate(
-        [
-            by_group(w_qkv, groups),
-            vectors.T,
-            up_bias.reshape(own, ratio),
-            jnp.zeros((own, 128 - vector_count - ratio), bf16),
-        ],
-        axis=1,
-    )
-    first = lax.all_gather(first, both, axis=0, tiled=True)
-    second = jnp.concatenate([w_out, w_up, w_down.reshape(own, wide)], axis=1)
-    second, _ = lax.optimization_barrier((second, first[:8, :128]))
-    second = lax.all_gather(second, both, axis=0, tiled=True)
-    full_qkv = first[:, : 3 * width]
-    table = first[:, 3 * width : 3 * width + vector_count].astype(f32).T
-    bias_up = first[:, 3 * width + vector_count : 3 * width + vector_count + ratio]
-    bias_up = bias_up.astype(f32).reshape(wide)
-    full_out = second[:, :width]
-    full_up = second[:, width : width + wide]
-    full_down = second[:, width + wide :].reshape(wide, width)
+    share = width // groups
+    span = 3 * share
+    small = vector_count + ratio
+
+    parts = by_group(w_qkv, groups)
+    half = groups // 2
+    extra = [vectors.T, up_bias.reshape(own, ratio), jnp.zeros((own, -small % 128), bf16)]
+    here = lax.axis_index("blk").astype(jnp.int32)
+    streams = [
+        Gather(jnp.concatenate(parts[:half] + extra, axis=1), False),
+        Gather(jnp.concatenate(parts[half:], axis=1), True),
+    ]
+    blk_steps = len(axis_bits("blk"))
+    begun = [stream.grow(blk_steps) for stream in streams]
+    w_out, w_up, w_down = after((w_out, w_up, w_down), begun)
+    later = [Gather(w_up, False), Gather(w_down, True), Gather(w_out, False)]
+    for one in later:
+        one.grow(blk_steps)
+    first = [stream.whole() for stream in streams]
+    for one in later:
+        one.piece = after(one.piece, first)
+        one.grow(1)
+    full_qkv = jnp.stack(
+        [part[:, g * span : (g + 1) * span] for part in first for g in range(half)]
+    )
+    corner = first[0][:, half * span : half * span + small]
+    table = corner[:, :vector_count].astype(f32).T
+    bias_up = corner[:, vector_count:].astype(f32).reshape(wide)
 
     slots = lax.axis_index("blk") * row_count + jnp.arange(row_count, dtype=jnp.int32)
     pass_of = (slots // PASS_SLOTS)[:, None] == jnp.arange(PASSES, dtype=jnp.int32)[None, :]
     bounds = jnp.sum(jnp.where(pass_of, lengths[0][None, :], 0), axis=1)
     live = (slots % PASS_SLOTS < bounds).astype(f32)[:, None]
-    pass_table = pass_of.astype(f32)
 
     added = jnp.zeros((row_count, width), f32)
     for index in range(PASSES):
@@ -243,41 +402,84 @@
     start = states[0].astype(f32) + added
     normed_a = layer_norm(start, table[5], table[6]).astype(bf16)
     bias_three = jnp.concatenate([table[7], jnp.zeros_like(table[7]), table[8]])
-    bias_three = by_group(bias_three[None], groups)
-    projected = (contract(normed_a, full_qkv, ((1,), (0,))) + bias_three).astype(bf16)
-    packed = to_heads(projected)
-    mixed, totals = attend(lengths, packed)
-    heads_out = to_slots(mixed)
+    bias_three = jnp.stack(by_group(bias_three[None], groups))
+
+    def project(group):
+        rows = contract(normed_a, at_group(full_qkv, group), ((1,), (0,)))
+        return (rows + at_group(bias_three, group)).astype(bf16)
+
+    pieces = [row_major(project(here ^ step)) for step in range(groups)]
+    for one in later:
+        one.piece = after(one.piece, pieces)
+    full_up, full_down, full_out = [one.whole() for one in later]
+    packed, mixed, totals = attend(lengths, here[None], swap_pieces(pieces))
+    grouped = mixed.reshape(groups, row_count, share)
+    pieces = swap_pieces([at_group(grouped, here ^ step) for step in range(groups)])
+    heads_out = in_order(pieces)
+    heads_out = jnp.concatenate([heads_out[g] for g in range(groups)], axis=1)
     middle = start + live * (contract(heads_out, full_out, ((1,), (0,))) + table[9])
     normed_b = layer_norm(middle, table[10], table[11]).astype(bf16)
     up_sum = contract(normed_b, full_up, ((1,), (0,))) + bias_up
     activated, gelu_pull = jax.vjp(gelu_tanh, up_sum)
     hidden = activated.astype(bf16)
-    outcome = middle + live * (contract(hidden, full_down, ((1,), (0,))) + table[12])
-
     incoming = cotangent[0].astype(f32)
     grad_branch = (live * incoming).astype(bf16)
-    grad_down = contract(hidden, grad_branch, ((0,), (0,)))
     grad_hidden = contract(grad_branch, full_down, ((1,), (1,)))
     grad_upsum = gelu_pull(grad_hidden)[0].astype(bf16)
-    grad_up = contract(normed_b, grad_upsum, ((0,), (0,)))
     grad_normb = contract(grad_upsum, full_up, ((1,), (1,)))
     middle_part, gain_grad_b, shift_grad_b = norm_back(middle, table[10], grad_normb)
     grad_middle = incoming + middle_part
     grad_attn = (live * grad_middle).astype(bf16)
-    grad_out = contract(heads_out, grad_attn, ((0,), (0,)))
-    grad_heads = contract(grad_attn, full_out, ((1,), (1,))).astype(bf16)
-    late = jnp.concatenate(
-        [grad_out.astype(bf16), grad_up.astype(bf16), grad_down.astype(bf16).reshape(width, wide)],
-        axis=1,
-    )
-    late = lax.psum_scatter(late, both, scatter_dimension=0, tiled=True)
-
-    grad_packed = attend_back(lengths, packed, mixed, to_heads(grad_heads), totals)
-    grad_projected = to_slots(grad_packed)
-    grad_qkv = contract(normed_a, grad_projected, ((0,), (0,)))
-    column_sums = by_kind(jnp.sum(grad_projected.astype(f32), axis=0)[None], groups)[0]
-    grad_norma = contract(grad_projected, full_qkv, ((1,), (1,)))
+    out_rows = full_out.reshape(groups, share, width)
+
+    def to_mixture(group):
+        return contract(grad_attn, at_group(out_rows, group), ((1,), (1,))).astype(bf16)
+
+    pieces = [row_major(to_mixture(here ^ step)) for step in range(groups)]
+    hidden_late, grad_branch_late, grad_upsum_late, grad_attn_late = after(
+        (hidden, grad_branch, grad_upsum, grad_attn), pieces
+    )
+    grad_down = contract(hidden_late, grad_branch_late, ((0,), (0,))).astype(bf16)
+    grad_up = contract(normed_b, grad_upsum_late, ((0,), (0,))).astype(bf16)
+    grad_out = contract(heads_out, grad_attn_late, ((0,), (0,))).astype(bf16)
+    late = [Scatter(grad_down, True), Scatter(grad_up, False), Scatter(grad_out, False)]
+    sent = [one.send() for one in late]
+    pieces = after(swap_pieces(pieces), sent)
+    for one in late:
+        one.receive()
+    done, grad_heads, grad_query = attend_back_first(
+        lengths, here[None], packed, mixed, totals, pieces
+    )
+    for one in late:
+        one.piece = after(one.piece, done)
+    sent = [one.send() for one in late]
+    grad_query = after(grad_query, sent)
+    for one in late:
+        one.receive()
+    grad_packed = attend_back_second(
+        lengths, packed, mixed, totals, grad_heads, done, grad_query
+    )
+    grad_packed = grad_packed.reshape(groups, row_count, span)
+    pieces = [row_major(at_group(grad_packed, here ^ step)) for step in range(groups)]
+    for one in late:
+        one.piece = after(one.piece, pieces)
+    sent = [one.send() for one in late]
+    for one in late:
+        one.receive()
+    pieces = after(swap_pieces(pieces), sent)
+    grad_projected = in_order(pieces)
+    grad_down, grad_up, grad_out = [one.finish() for one in late]
+    outcome = middle + live * (contract(hidden, full_down, ((1,), (0,))) + table[12])
+
+    grad_qkv = [
+        row_major(contract(normed_a, grad_projected[g], ((0,), (0,))).astype(bf16))
+        for g in range(groups)
+    ]
+    sums = jnp.sum(grad_projected.astype(f32), axis=1)
+    column_sums = by_kind([sums[g : g + 1] for g in range(groups)])[0]
+    grad_norma = sum(
+        contract(grad_projected[g], full_qkv[g], ((1,), (1,))) for g in range(groups)
+    )
     start_part, gain_grad_a, shift_grad_a = norm_back(start, table[5], grad_norma)
     grad_start = grad_middle + start_part
     grad_embed = [
@@ -298,27 +500,23 @@
         ]
     )
     bias_grads = jnp.sum(grad_upsum.astype(f32), axis=0)
-    last = jnp.concatenate(
-        [
-            grad_qkv.astype(bf16),
-            vector_grads.T.astype(bf16),
-            bias_grads.reshape(width, ratio).astype(bf16),
-            jnp.zeros((width, 128 - vector_count - ratio), bf16),
-        ],
-        axis=1,
-    )
-    last = lax.psum_scatter(last, both, scatter_dimension=0, tiled=True).astype(f32)
-    late = late.astype(f32)
-    edge = 3 * width + vector_count
+    extra = [vector_grads.T.astype(bf16), bias_grads.reshape(width, ratio).astype(bf16)]
+    extra = extra + [jnp.zeros((width, -small % 128), bf16)]
+    sums_qkv = [
+        Scatter(jnp.concatenate(grad_qkv[:half] + extra, axis=1), False).finish().astype(f32),
+        Scatter(jnp.concatenate(grad_qkv[half:], axis=1), True).finish().astype(f32),
+    ]
+    extra = sums_qkv[0][:, half * span :]
+    sums_qkv = [part[:, g * span : (g + 1) * span] for part in sums_qkv for g in range(half)]
     return (
         outcome.astype(bf16)[None],
         grad_start.astype(bf16)[None],
-        by_kind(last[:, : 3 * width], groups),
-        late[:, :width],
-        late[:, width : width + wide],
-        late[:, width + wide :].reshape(own * ratio, width),
-        last[:, 3 * width : edge].T,
-        last[:, edge : edge + ratio].reshape(own * ratio),
+        by_kind(sums_qkv),
+        grad_out.astype(f32),
+        grad_up.astype(f32),
+        grad_down.astype(f32),
+        extra[:, :vector_count].T,
+        extra[:, vector_count:small].reshape(own * ratio),
     )
 
 

time: 739 us -> 578 us (0.78)
  blocking collectives: 140 us -> 0 us
  waiting for transfers between devices: 336 us -> 243 us
  starting transfers between devices: 7.74 us -> 82.6 us
  other arithmetic: 17.6 us -> 49.7 us
  matrix products: 78.7 us -> 58.2 us
  between operations: 14.5 us -> 2.79 us
  local copies, waits for them, and re-layouts: 69 us -> 59.1 us
  Pallas kernels: 66.2 us -> 74.3 us
    ppermute x0 -> x62, waiting for transfers between devices: none -> 243 us  [swap_with(): return lax.ppermute(values, axis, [(i, i ^ step) for i in range(size)])]
    reduce_scatter x1 -> x0, waiting for transfers between devices: 142 us -> none  [on_device(): late = lax.psum_scatter(late, both, scatter_dimension=0, tiled=True)]
    all_to_all x2 -> x0, blocking collectives: 140 us -> none  [to_heads(): return lax.all_to_all(rows, 'blk', 1, 0, tiled=True)]
    all_to_all x2 -> x0, waiting for transfers between devices: 88.2 us -> none  [to_slots(): return lax.all_to_all(rows, 'blk', 0, 1, tiled=True)]
    ppermute x0 -> x62, starting transfers between devices: none -> 82.6 us  [swap_with(): return lax.ppermute(values, axis, [(i, i ^ step) for i in range(size)])]
    all_gather x2 -> x0, waiting for transfers between devices: 61.2 us -> none  [the longest x1 61.2 us: on_device(): first = lax.all_gather(first, both, axis=0, tiled=True)]
    unnamed x5 -> x0, waiting for transfers between devices: 45 us -> none
    dot_general x12 -> x24, matrix products: 78.7 us -> 58.2 us  [contract(): lax.dot_general(left, right, (dims, ((), ())), preferred_element_type=f32)]
  transfers between devices with their start and end apart: 6 -> 62, of which waited for: 5 -> 33; matrix products, arithmetic and copies ran while one was open for 11% -> 18% of each run, Pallas kernels for 4% -> 5%
where the time goes in v2:
time: 578 us; the launch traced here: 569 us
  waiting for transfers between devices  243 us (42%)
  starting transfers between devices  82.6 us (14%)
  Pallas kernels  74.3 us (13%)
  local copies, waits for them, and re-layouts  59.1 us (10%)
  matrix products  58.2 us (10%)
  other arithmetic  49.7 us (9%)
    ppermute x62, waiting for transfers between devices, swap_with(): return lax.ppermute(values, axis, [(i, i ^ step) for i in range(size)])  243 us
    ppermute x62, starting transfers between devices, swap_with(): return lax.ppermute(values, axis, [(i, i ^ step) for i in range(size)])  82.6 us
    dot_general x24, matrix products, contract(): lax.dot_general(left, right, (dims, ((), ())), preferred_element_type=f32)  58.2 us
    pallas_call x1, Pallas kernels, attend(): pl.pallas_call(forward_kernel, out_shape=(jax.ShapeDtypeStruct((slots, tr...  28.1 us
    pallas_call x1, Pallas kernels, attend_back_first(): pl.pallas_call(first_backward_kernel, out_shape=(jax.ShapeDtypeStruct((SP...  26 us
    pallas_call x1, Pallas kernels, attend_back_second(): pl.pallas_call(second_backward_kernel, out_shape=jax.ShapeDtypeStruct(pac...  20.2 us
    unnamed x130, local copies, waits for them, and re-layouts  17.8 us
    another operation x50, other arithmetic, grow(): self.piece = jnp.stack([low, high], axis=self.done.index(bit))  16.2 us
  transfers between devices with their start and end apart: 62, of which 33 were waited for; matrix products, arithmetic and copies ran while one was open for 18% of the time, Pallas kernels for 5%

profile of v2, /device:TPU:0, one launch (start us, length us, event | category | flops | bytes accessed | tf_op | source)
XLA Modules:
  0.0 569.3 jit_solution(17567442154014982023)
XLA Ops:
  4.3 4.1 collective-permute-start
  9.5 4.4 collective-permute-done.5
  16.3 3.7 collective-permute-done.6
  21.3 3.1 collective-permute-start.16
  24.4 1.9 collective-permute-done.16
  26.4 1.8 collective-permute-start.17
  31.4 3.0 collective-permute-start.21
  34.5 8.2 %collective-permute-done.21 = bf16[24,3072]{1,0:T(8,128)(2,1)S(1)} collective-permute-done((bf16[24,3072]{1,0:T(8,128)(2,1)S(1)}, bf16[24,3072]{1,0:T(8,128)(2,1)S(1)}, u32[]{:S(2)}, u32[]{:S(2)}) %collective-permute-start.21) | collective-permute-done | bytes 147488 | tf_op jit(solution)/shard_map/ppermute | solution.py:239
  43.1 2.2 collective-permute-done.26
  46.8 5.9 %collective-permute-done.22 = bf16[2,24,3072]{2,1,0:T(8,128)(2,1)S(1)} collective-permute-done((bf16[2,24,3072]{2,1,0:T(8,128)(2,1)S(1)}, bf16[2,24,3072]{2,1,0:T(8,128)(2,1)S(1)}, u32[]{:S(2)}, u32[]{:S(2)}) %collective-permute-start.22) | collective-permute-done | bytes 294944 | tf_op jit(solution)/shard_map/ppermute | solution.py:239
  52.8 5.0 collective-permute-done.27
  63.5 2.8 slice_reduce_fusion
  66.3 2.0 slice_bitcast_fusion.3
  73.0 3.1 fusion.25
  83.5 1.9 collective-permute-start.11
  89.8 2.1 add_convert_fusion.9.refs_0_
  93.3 9.2 %collective-permute-done.23 = bf16[2,2,24,3072]{3,2,1,0:T(8,128)(2,1)S(1)} collective-permute-done((bf16[2,2,24,3072]{3,2,1,0:T(8,128)(2,1)}, bf16[2,2,24,3072]{3,2,1,0:T(8,128)(2,1)S(1)}, u32[]{:S(2)}, u32[]{:S(2)}) %collective-permute-start.23) | collective-permute-done | bytes 589856 | tf_op jit(solution)/shard_map/ppermute | solution.py:239
  105.5 6.9 %collective-permute-done.19 = bf16[2,2,2,24,768]{4,3,2,1,0:T(8,128)(2,1)S(1)} collective-permute-done((bf16[2,2,2,24,768]{4,3,2,1,0:T(8,128)(2,1)S(1)}, bf16[2,2,2,24,768]{4,3,2,1,0:T(8,128)(2,1)S(1)}, u32[]{:S(2)}, u32[]{:S(2)}) %collective-permute-start.19) | collective-permute-done | bytes 294944 | tf_op jit(solution)/shard_map/ppermute | solution.py:239
  115.5 20.2 %collective-permute-done.11 = bf16[640,576]{0,1:T(8,128)(2,1)} collective-permute-done((bf16[640,576]{0,1:T(8,128)(2,1)}, bf16[640,576]{0,1:T(8,128)(2,1)}, u32[]{:S(2)}, u32[]{:S(2)}) %collective-permute-start.11) | collective-permute-done | bytes 737312 | tf_op jit(solution)/shard_map/ppermute | solution.py:239
  138.7 28.1 %attend.1 = (bf16[2560,576]{1,0:T(8,128)(2,1)}, bf16[2560,192]{1,0:T(8,128)(2,1)S(1)}, f32[5,3,512]{2,1,0:T(4,128)S(1)}) custom-call(s32[1,5]{1,0:T(1,128)S(1)} %copy-done.1, s32[1]{0:T(128)} %bitcast.15.here, bf16[640,576]{1,0:T(8,128)(2,1)S(1)} %add_convert_fusion.9.refs_0_, bf16[640,576]{1,0:T(8,128)(2,1)S(1)} %copy.130.refs_1_, ...), custom_call_target="tpu_custom_call" | custom-call | tf_op jit(solution)/shard_map/attend/pallas_call | solution.py:177
  167.0 13.6 %collective-permute-start.13 = (bf16[640,192]{1,0:T(8,128)(2,1)S(1)}, bf16[640,192]{1,0:T(8,128)(2,1)S(1)}, u32[]{:S(2)}, u32[]{:S(2)}) collective-permute-start(bf16[640,192]{1,0:T(8,128)(2,1)S(1)} %get-tuple-element.189), channel_id=1, source_target_pairs={{0,1},{1,0},{2,3},{3,2},{4,5},{5,4},{6,7},{7,6},{8,9},{9,8},{10,11... | collective-permute-start | bytes 737288 | tf_op jit(solution)/shard_map/ppermute | solution.py:239
  183.9 8.1 %collective-permute-done.13 = bf16[640,192]{1,0:T(8,128)(2,1)S(1)} collective-permute-done((bf16[640,192]{1,0:T(8,128)(2,1)S(1)}, bf16[640,192]{1,0:T(8,128)(2,1)S(1)}, u32[]{:S(2)}, u32[]{:S(2)}) %collective-permute-start.13) | collective-permute-done | bytes 245792 | tf_op jit(solution)/shard_map/ppermute | solution.py:239
  192.0 1.9 collective-permute-start.15
  194.0 13.6 %collective-permute-done.14 = bf16[640,192]{1,0:T(8,128)(2,1)S(1)} collective-permute-done((bf16[640,192]{1,0:T(8,128)(2,1)S(1)}, bf16[640,192]{1,0:T(8,128)(2,1)S(1)}, u32[]{:S(2)}, u32[]{:S(2)}) %collective-permute-start.14) | collective-permute-done | bytes 245792 | tf_op jit(solution)/shard_map/ppermute | solution.py:239
  207.6 1.8 select_bitcast_fusion.15
  217.7 2.0 select_bitcast_fusion.5
  220.4 8.0 %multiply_convert_fusion = (bf16[640,3072]{1,0:T(8,128)(2,1)}, f32[640,3072]{1,0:T(8,128)}) fusion(f32[3072]{0:T(1024)S(1)} %reshape.1290, bf16[768,3072]{1,0:T(8,128)(2,1)S(1)} %bitcast.431, f32[640,768]{1,0:T(8,128)S(1)} %get-tuple-element.241, f32[768]{0:T(1024)S(1)} %copy-done.56, f32[768]{0:T(1024)S(1)} %copy-done.44, f32[640]{0:T(1024)S(1)} %add_rsqrt_fusion, ...), kind=kOutput, calls=%fused_computation.9 | convolution fusion | flops 3042017280 | bytes 18504704 | tf_op jit(solution)/shard_map/dot_general | solution.py:33
  228.3 10.4 %fusion.104 = (bf16[3072]{0:T(1024)(128)(2,1)S(1)}, bf16[640,3072]{1,0:T(8,128)(2,1)S(1)}) fusion(f32[640,3072]{1,0:T(8,128)} %get-tuple-element.243, f32[3072]{0:T(1024)S(1)} %reshape.1290, bf16[3072,768]{1,0:T(8,128)(2,1)S(1)} %bitcast.429, bf16[1,640,768]{2,1,0:T(8,128)(2,1)S(1)} %copy-done.34, f32[640]{0:T(1024)S(1)} %fusion.83), kind=kOutput, calls=%fused_computation.373 | convolution fusion | flops 3064624128 | bytes 17519104 | tf_op jit(solution)/shard_map/dot_general | solution.py:33
  238.7 3.7 multiply_reduce_fusion
  242.4 2.2 fusion.91
  247.2 4.8 convolution_convert_fusion
  254.4 4.4 convolution_convert_fusion.1
  265.0 2.0 collective-permute-start.33
  268.4 2.8 add_convert_fusion.1
  271.2 6.5 %collective-permute-done.31.refs_1_ = bf16[640,192]{1,0:T(8,128)(2,1)S(1)} collective-permute-done((bf16[640,192]{1,0:T(8,128)(2,1)S(1)}, bf16[640,192]{1,0:T(8,128)(2,1)S(1)}, u32[]{:S(2)}, u32[]{:S(2)}) %collective-permute-start.31) | collective-permute-done | bytes 245792 | tf_op jit(solution)/shard_map/ppermute | solution.py:239
  277.6 11.2 %collective-permute-done.32.refs_2_ = bf16[640,192]{1,0:T(8,128)(2,1)S(1)} collective-permute-done((bf16[640,192]{1,0:T(8,128)(2,1)S(1)}, bf16[640,192]{1,0:T(8,128)(2,1)S(1)}, u32[]{:S(2)}, u32[]{:S(2)}) %collective-permute-start.32) | collective-permute-done | bytes 245792 | tf_op jit(solution)/shard_map/ppermute | solution.py:239
  288.8 26.0 %attend_back_first.1 = (bf16[1024,384]{1,0:T(8,128)(2,1)S(1)}, bf16[2560,192]{1,0:T(8,128)(2,1)S(1)}, f32[2560,192]{1,0:T(8,128)}) custom-call(s32[1,5]{1,0:T(1,128)S(1)} %copy-done.1, s32[1]{0:T(128)} %bitcast.15.here, bf16[2560,576]{1,0:T(8,128)(2,1)} %get-tuple-element.52.packed, bf16[2560,192]{1,0:T(8,128)(2,1)S(1)} %get-tuple-element.42.mixed, ...), custom_call_target="tpu_custom_call" | custom-call | tf_op jit(solution)/shard_map/attend_back_first/pallas_call | solution.py:194
  318.4 29.7 %collective-permute-done.42 = bf16[2,2,2,24,768]{4,3,1,2,0:T(8,128)(2,1)S(1)} collective-permute-done((bf16[2,2,2,24,768]{4,3,1,2,0:T(8,128)(2,1)S(1)}, bf16[2,2,2,24,768]{4,3,1,2,0:T(8,128)(2,1)S(1)}, u32[]{:S(2)}, u32[]{:S(2)}) %collective-permute-start.42) | collective-permute-done | bytes 294944 | tf_op jit(solution)/shard_map/ppermute | solution.py:239
  350.8 20.2 %attend_back_second.1 = bf16[2560,576]{1,0:T(8,128)(2,1)} custom-call(s32[1,5]{1,0:T(1,128)S(1)} %copy-done.1, bf16[2560,576]{1,0:T(8,128)(2,1)} %get-tuple-element.52.packed, bf16[2560,192]{1,0:T(8,128)(2,1)S(1)} %get-tuple-element.42.mixed, f32[5,3,512]{2,1,0:T(4,128)S(1)} %get-tuple-element.53.totals, bf16[2560,192]{1,0:T(8,128)(2,1)S(1)} %get-tuple-element.62.grad, ...), custom_call_target="tpu_custom_call" | custom-call | tf_op jit(solution)/shard_map/attend_back_second/pallas_call | solution.py:214
  371.0 3.8 dynamic-slice_bitcast_fusion
  376.0 6.5 %fusion.19 = bf16[1,640,768]{2,1,0:T(8,128)(2,1)} fusion(f32[640,768]{1,0:T(8,128)S(1)} %copy-done.12, bf16[640,3072]{1,0:T(8,128)(2,1)S(1)} %copy-done.59, bf16[3072,768]{1,0:T(8,128)(2,1)} %bitcast.430, f32[768]{0:T(1024)S(1)} %copy-done.55, f32[640]{0:T(1024)S(1)} %fusion.83), kind=kOutput, calls=%fused_computation.81 | convolution fusion | flops 3021864960 | bytes 11605504 | tf_op jit(solution)/shard_map/dot_general | solution.py:33
  383.7 2.4 copy.147
  386.0 2.3 copy.148
  388.3 2.3 copy.149
  390.6 8.1 %collective-permute-start.37 = (bf16[640,576]{0,1:T(8,128)(2,1)}, bf16[640,576]{0,1:T(8,128)(2,1)S(1)}, u32[]{:S(2)}, u32[]{:S(2)}) collective-permute-start(bf16[640,576]{0,1:T(8,128)(2,1)} %copy.147), channel_id=1, source_target_pairs={{0,1},{1,0},{2,3},{3,2},{4,5},{5,4},{6,7},{7,6},{8,9},{9,8},{10,11... | collective-permute-start | bytes 2211848 | tf_op jit(solution)/shard_map/ppermute | solution.py:239
  399.2 1.9 collective-permute-start.39
  405.7 40.0 %collective-permute-done.54 = bf16[2,24,768]{2,1,0:T(8,128)(2,1)S(1)} collective-permute-done((bf16[2,24,768]{2,1,0:T(8,128)(2,1)S(1)}, bf16[2,24,768]{2,1,0:T(8,128)(2,1)S(1)}, u32[]{:S(2)}, u32[]{:S(2)}) %collective-permute-start.54) | collective-permute-done | bytes 73760 | tf_op jit(solution)/shard_map/ppermute | solution.py:239
  445.7 3.6 collective-permute-start.55
  449.4 15.2 %collective-permute-done.55 = bf16[24,768]{1,0:T(8,128)(2,1)S(1)} collective-permute-done((bf16[24,768]{1,0:T(8,128)(2,1)S(1)}, bf16[24,768]{1,0:T(8,128)(2,1)S(1)}, u32[]{:S(2)}, u32[]{:S(2)}) %collective-permute-start.55) | collective-permute-done | bytes 36896 | tf_op jit(solution)/shard_map/ppermute | solution.py:239
  466.6 9.4 %collective-permute-done.59 = bf16[2,2,96,768]{3,2,0,1:T(8,128)(2,1)S(1)} collective-permute-done((bf16[2,2,96,768]{3,2,0,1:T(8,128)(2,1)S(1)}, bf16[2,2,96,768]{3,2,0,1:T(8,128)(2,1)S(1)}, u32[]{:S(2)}, u32[]{:S(2)}) %collective-permute-start.59) | collective-permute-done | bytes 589856 | tf_op jit(solution)/shard_map/ppermute | solution.py:239
  479.8 2.5 copy.150
  493.9 2.0 convolution_convert_fusion.6
  495.9 2.1 convolution_convert_fusion.5
  503.1 2.7 select_reduce_fusion
  506.7 3.9 concatenate.29
  512.7 2.9 collective-permute-start.61
  516.9 9.8 %collective-permute-done.61 = bf16[96,768]{1,0:T(8,128)(2,1)S(1)} collective-permute-done((bf16[96,768]{1,0:T(8,128)(2,1)S(1)}, bf16[96,768]{1,0:T(8,128)(2,1)S(1)}, u32[]{:S(2)}, u32[]{:S(2)}) %collective-permute-start.61) | collective-permute-done | bytes 147488 | tf_op jit(solution)/shard_map/ppermute | solution.py:239
  533.2 8.9 %collective-permute-done.49 = bf16[2,2,2,24,1152]{4,3,1,2,0:T(8,128)(2,1)S(1)} collective-permute-done((bf16[2,2,2,24,1152]{4,3,1,2,0:T(8,128)(2,1)S(1)}, bf16[2,2,2,24,1152]{4,3,1,2,0:T(8,128)(2,1)S(1)}, u32[]{:S(2)}, u32[]{:S(2)}) %collective-permute-start.49) | collective-permute-done | bytes 442400 | tf_op jit(solution)/shard_map/ppermute | solution.py:239
  543.1 2.7 collective-permute-done.44
  546.0 3.2 collective-permute-done.50
  550.5 3.7 collective-permute-done.51
  556.1 1.8 collective-permute-start.46
  561.1 2.5 collective-permute-start.47
  563.8 2.4 collective-permute-done.47
  (427 shorter events, 127.7 us)
Async XLA Ops:
  4.3 11.3 %collective-permute-start = (bf16[24,1280]{1,0:T(8,128)(2,1)S(1)}, bf16[24,1280]{1,0:T(8,128)(2,1)S(1)}, u32[]{:S(2)}, u32[]{:S(2)}) collective-permute-start(bf16[24,1280]{1,0:T(8,128)(2,1)S(1)} %concatenate.24), channel_id=1, source_target_pairs={{0,2},{1,3},{2,0},{3,1},{4,6},{5,7},{6,4},{7,5},{8,10},{9,11},{10,... | collective-permute-start | bytes 184328 | tf_op jit(solution)/shard_map/ppermute | solution.py:239
  8.7 5.3 collective-permute-start.5
  14.1 5.9 %collective-permute-start.6 = (bf16[2,24,1152]{2,1,0:T(8,128)(2,1)S(1)}, bf16[2,24,1152]{2,1,0:T(8,128)(2,1)S(1)}, u32[]{:S(2)}, u32[]{:S(2)}) collective-permute-start(bf16[2,24,1152]{2,1,0:T(8,128)(2,1)S(1)} %pad_maximum_fusion.27), channel_id=1, source_target_pairs={{0,1},{1,0},{2,3},{3,2},{4,5},{5,4},{6,7},{7,6},{8,9},{9,8},{10,11... | collective-permute-start | bytes 331784 | tf_op jit(solution)/shard_map/ppermute | solution.py:239
  15.6 5.7 collective-permute-start.1
  21.3 5.0 collective-permute-start.16
  26.4 8.1 %collective-permute-start.17 = (bf16[2,24,768]{2,1,0:T(8,128)(2,1)S(1)}, bf16[2,24,768]{2,1,0:T(8,128)(2,1)S(1)}, u32[]{:S(2)}, u32[]{:S(2)}) collective-permute-start(bf16[2,24,768]{2,1,0:T(8,128)(2,1)S(1)} %pad_maximum_fusion.28), channel_id=1, source_target_pairs={{0,1},{1,0},{2,3},{3,2},{4,5},{5,4},{6,7},{7,6},{8,9},{9,8},{10,11... | collective-permute-start | bytes 221192 | tf_op jit(solution)/shard_map/ppermute | solution.py:239
  28.2 40.4 %copy-start.45 = (pred[640]{0:T(1024)(128)(4,1)}, pred[640]{0:T(1024)(128)(4,1)S(1)}, u32[]{:S(2)}) copy-start(pred[640]{0:T(1024)(128)(4,1)S(1)} %get-tuple-element.126) | copy-start | bytes 1924
  28.3 17.2 %collective-permute-start.7 = (bf16[2,2,24,1152]{3,2,0,1:T(8,128)(2,1)S(1)}, bf16[2,2,24,1152]{3,2,0,1:T(8,128)(2,1)S(1)}, u32[]{:S(2)}, u32[]{:S(2)}) collective-permute-start(bf16[2,2,24,1152]{3,2,0,1:T(8,128)(2,1)S(1)} %pad_maximum_fusion.24), channel_id=1, source_target_pairs={{0,8},{4,12},{8,0},{12,4},{16,24},{20,28},{24,16},{28,20},{1,9},{5... | collective-permute-start | bytes 663560 | tf_op jit(solution)/shard_map/ppermute | solution.py:239
  29.8 16.2 %collective-permute-start.2 = (bf16[2,2,24,1280]{3,2,0,1:T(8,128)(2,1)S(1)}, bf16[2,2,24,1280]{3,2,0,1:T(8,128)(2,1)S(1)}, u32[]{:S(2)}, u32[]{:S(2)}) collective-permute-start(bf16[2,2,24,1280]{3,2,0,1:T(8,128)(2,1)S(1)} %pad_maximum_fusion.23), channel_id=1, source_target_pairs={{0,16},{4,20},{8,24},{12,28},{16,0},{20,4},{24,8},{28,12},{1,17},{... | collective-permute-start | bytes 737288 | tf_op jit(solution)/shard_map/ppermute | solution.py:239
  31.4 11.4 %collective-permute-start.21 = (bf16[24,3072]{1,0:T(8,128)(2,1)S(1)}, bf16[24,3072]{1,0:T(8,128)(2,1)S(1)}, u32[]{:S(2)}, u32[]{:S(2)}) collective-permute-start(bf16[24,3072]{1,0:T(8,128)(2,1)S(1)} %copy-done.41), channel_id=1, source_target_pairs={{0,2},{1,3},{2,0},{3,1},{4,6},{5,7},{6,4},{7,5},{8,10},{9,11},{10,... | collective-permute-start | bytes 442376 | tf_op jit(solution)/shard_map/ppermute | solution.py:239
  34.4 10.9 %collective-permute-start.26 = (bf16[96,768]{1,0:T(8,128)(2,1)S(1)}, bf16[96,768]{1,0:T(8,128)(2,1)S(1)}, u32[]{:S(2)}, u32[]{:S(2)}) collective-permute-start(bf16[96,768]{1,0:T(8,128)(2,1)S(1)} %copy-done.42), channel_id=1, source_target_pairs={{0,2},{1,3},{2,0},{3,1},{4,6},{5,7},{6,4},{7,5},{8,10},{9,11},{10,... | collective-permute-start | bytes 442376 | tf_op jit(solution)/shard_map/ppermute | solution.py:239
  42.8 9.9 %collective-permute-start.22 = (bf16[2,24,3072]{2,1,0:T(8,128)(2,1)S(1)}, bf16[2,24,3072]{2,1,0:T(8,128)(2,1)S(1)}, u32[]{:S(2)}, u32[]{:S(2)}) collective-permute-start(bf16[2,24,3072]{2,1,0:T(8,128)(2,1)S(1)} %pad_maximum_fusion.20), channel_id=1, source_target_pairs={{0,1},{1,0},{2,3},{3,2},{4,5},{5,4},{6,7},{7,6},{8,9},{9,8},{10,11... | collective-permute-start | bytes 884744 | tf_op jit(solution)/shard_map/ppermute | solution.py:239
  45.4 12.5 %collective-permute-start.27 = (bf16[2,96,768]{2,1,0:T(8,128)(2,1)S(1)}, bf16[2,96,768]{2,1,0:T(8,128)(2,1)S(1)}, u32[]{:S(2)}, u32[]{:S(2)}) collective-permute-start(bf16[2,96,768]{2,1,0:T(8,128)(2,1)S(1)} %pad_maximum_fusion.21), channel_id=1, source_target_pairs={{0,1},{1,0},{2,3},{3,2},{4,5},{5,4},{6,7},{7,6},{8,9},{9,8},{10,11... | collective-permute-start | bytes 884744 | tf_op jit(solution)/shard_map/ppermute | solution.py:239
  45.6 13.2 %collective-permute-start.8 = (bf16[2,2,2,24,1152]{4,3,1,2,0:T(8,128)(2,1)S(1)}, bf16[2,2,2,24,1152]{4,3,1,2,0:T(8,128)(2,1)S(1)}, u32[]{:S(2)}, u32[]{:S(2)}) collective-permute-start(bf16[2,2,2,24,1152]{4,3,1,2,0:T(8,128)(2,1)S(1)} %pad_maximum_fusion.18), channel_id=1, source_target_pairs={{0,16},{4,20},{8,24},{12,28},{16,0},{20,4},{24,8},{28,12},{1,17},{... | collective-permute-start | bytes 1327112 | tf_op jit(solution)/shard_map/ppermute | solution.py:239
  46.1 12.9 %collective-permute-start.3 = (bf16[2,2,2,24,1280]{4,3,1,2,0:T(8,128)(2,1)S(1)}, bf16[2,2,2,24,1280]{4,3,1,2,0:T(8,128)(2,1)S(1)}, u32[]{:S(2)}, u32[]{:S(2)}) collective-permute-start(bf16[2,2,2,24,1280]{4,3,1,2,0:T(8,128)(2,1)S(1)} %pad_maximum_fusion.17), channel_id=1, source_target_pairs={{0,8},{4,12},{8,0},{12,4},{16,24},{20,28},{24,16},{28,20},{1,9},{5... | collective-permute-start | bytes 1474568 | tf_op jit(solution)/shard_map/ppermute | solution.py:239
  59.0 2.5 collective-permute-start.9
  59.2 3.6 collective-permute-start.4
  68.3 23.6 %collective-permute-start.18 = (bf16[2,2,24,768]{3,2,1,0:T(8,128)(2,1)S(1)}, bf16[2,2,24,768]{3,2,1,0:T(8,128)(2,1)}, u32[]{:S(2)}, u32[]{:S(2)}) collective-permute-start(bf16[2,2,24,768]{3,2,1,0:T(8,128)(2,1)S(1)} %pad_maximum_fusion.25), channel_id=1, source_target_pairs={{0,16},{4,20},{8,24},{12,28},{16,0},{20,4},{24,8},{28,12},{1,17},{... | collective-permute-start | bytes 442376 | tf_op jit(solution)/shard_map/ppermute | solution.py:239
  81.1 32.8 %collective-permute-start.10 = (bf16[640,576]{0,1:T(8,128)(2,1)}, bf16[640,576]{0,1:T(8,128)(2,1)}, u32[]{:S(2)}, u32[]{:S(2)}) collective-permute-start(bf16[640,576]{0,1:T(8,128)(2,1)} %copy.127), channel_id=1, source_target_pairs={{0,1},{1,0},{2,3},{3,2},{4,5},{5,4},{6,7},{7,6},{8,9},{9,8},{10,11... | collective-permute-start | bytes 2211848 | tf_op jit(solution)/shard_map/ppermute | solution.py:239
  83.5 52.2 %collective-permute-start.11 = (bf16[640,576]{0,1:T(8,128)(2,1)}, bf16[640,576]{0,1:T(8,128)(2,1)}, u32[]{:S(2)}, u32[]{:S(2)}) collective-permute-start(bf16[640,576]{0,1:T(8,128)(2,1)} %copy.128), channel_id=1, source_target_pairs={{0,2},{1,3},{2,0},{3,1},{4,6},{5,7},{6,4},{7,5},{8,10},{9,11},{10,... | collective-permute-start | bytes 2211848 | tf_op jit(solution)/shard_map/ppermute | solution.py:239
  86.6 50.6 %collective-permute-start.12 = (bf16[640,576]{0,1:T(8,128)(2,1)}, bf16[640,576]{0,1:T(8,128)(2,1)}, u32[]{:S(2)}, u32[]{:S(2)}) collective-permute-start(bf16[640,576]{0,1:T(8,128)(2,1)} %copy.129), channel_id=1, source_target_pairs={{0,3},{1,2},{2,1},{3,0},{4,7},{5,6},{6,5},{7,4},{8,11},{9,10},{10,... | collective-permute-start | bytes 2211848 | tf_op jit(solution)/shard_map/ppermute | solution.py:239
  88.0 14.5 %collective-permute-start.23 = (bf16[2,2,24,3072]{3,2,1,0:T(8,128)(2,1)}, bf16[2,2,24,3072]{3,2,1,0:T(8,128)(2,1)S(1)}, u32[]{:S(2)}, u32[]{:S(2)}) collective-permute-start(bf16[2,2,24,3072]{3,2,1,0:T(8,128)(2,1)} %pad_maximum_fusion.15), channel_id=1, source_target_pairs={{0,16},{4,20},{8,24},{12,28},{16,0},{20,4},{24,8},{28,12},{1,17},{... | collective-permute-start | bytes 1769480 | tf_op jit(solution)/shard_map/ppermute | solution.py:239
  91.9 88.7 %collective-permute-start.28 = (bf16[2,2,96,768]{3,2,1,0:T(8,128)(2,1)}, bf16[2,2,96,768]{3,2,1,0:T(8,128)(2,1)}, u32[]{:S(2)}, u32[]{:S(2)}) collective-permute-start(bf16[2,2,96,768]{3,2,1,0:T(8,128)(2,1)} %pad_maximum_fusion.16), channel_id=1, source_target_pairs={{0,8},{4,12},{8,0},{12,4},{16,24},{20,28},{24,16},{28,20},{1,9},{5... | collective-permute-start | bytes 1769480 | tf_op jit(solution)/shard_map/ppermute | solution.py:239
  102.6 9.9 %collective-permute-start.19 = (bf16[2,2,2,24,768]{4,3,2,1,0:T(8,128)(2,1)S(1)}, bf16[2,2,2,24,768]{4,3,2,1,0:T(8,128)(2,1)S(1)}, u32[]{:S(2)}, u32[]{:S(2)}) collective-permute-start(bf16[2,2,2,24,768]{4,3,2,1,0:T(8,128)(2,1)S(1)} %pad_maximum_fusion.19), channel_id=1, source_target_pairs={{0,8},{4,12},{8,0},{12,4},{16,24},{20,28},{24,16},{28,20},{1,9},{5... | collective-permute-start | bytes 884744 | tf_op jit(solution)/shard_map/ppermute | solution.py:239
  112.5 95.1 %collective-permute-start.24 = (bf16[2,2,2,24,3072]{4,3,2,1,0:T(8,128)(2,1)}, bf16[2,2,2,24,3072]{4,3,2,1,0:T(8,128)(2,1)}, u32[]{:S(2)}, u32[]{:S(2)}) collective-permute-start(bf16[2,2,2,24,3072]{4,3,2,1,0:T(8,128)(2,1)} %pad_maximum_fusion.9), channel_id=1, source_target_pairs={{0,8},{4,12},{8,0},{12,4},{16,24},{20,28},{24,16},{28,20},{1,9},{5... | collective-permute-start | bytes 3538952 | tf_op jit(solution)/shard_map/ppermute | solution.py:239
  113.9 95.9 %collective-permute-start.20 = (bf16[2,2,2,2,24,768]{5,4,3,2,1,0:T(8,128)(2,1)}, bf16[2,2,2,2,24,768]{5,4,3,2,1,0:T(8,128)(2,1)}, u32[]{:S(2)}, u32[]{:S(2)}) collective-permute-start(bf16[2,2,2,2,24,768]{5,4,3,2,1,0:T(8,128)(2,1)} %pad_maximum_fusion.14), channel_id=1, source_target_pairs={{0,4},{4,0},{8,12},{12,8},{16,20},{20,16},{24,28},{28,24},{1,5},{5... | collective-permute-start | bytes 1769480 | tf_op jit(solution)/shard_map/ppermute | solution.py:239
  167.0 25.0 %collective-permute-start.13 = (bf16[640,192]{1,0:T(8,128)(2,1)S(1)}, bf16[640,192]{1,0:T(8,128)(2,1)S(1)}, u32[]{:S(2)}, u32[]{:S(2)}) collective-permute-start(bf16[640,192]{1,0:T(8,128)(2,1)S(1)} %get-tuple-element.189), channel_id=1, source_target_pairs={{0,1},{1,0},{2,3},{3,2},{4,5},{5,4},{6,7},{7,6},{8,9},{9,8},{10,11... | collective-permute-start | bytes 737288 | tf_op jit(solution)/shard_map/ppermute | solution.py:239
  181.9 25.6 %collective-permute-start.14 = (bf16[640,192]{1,0:T(8,128)(2,1)S(1)}, bf16[640,192]{1,0:T(8,128)(2,1)S(1)}, u32[]{:S(2)}, u32[]{:S(2)}) collective-permute-start(bf16[640,192]{1,0:T(8,128)(2,1)S(1)} %get-tuple-element.188), channel_id=1, source_target_pairs={{0,2},{1,3},{2,0},{3,1},{4,6},{5,7},{6,4},{7,5},{8,10},{9,11},{10,... | collective-permute-start | bytes 737288 | tf_op jit(solution)/shard_map/ppermute | solution.py:239
  182.6 29.2 %collective-permute-start.29 = (bf16[2,2,2,96,768]{4,3,2,1,0:T(8,128)(2,1)S(1)}, bf16[2,2,2,96,768]{4,3,2,1,0:T(8,128)(2,1)S(1)}, u32[]{:S(2)}, u32[]{:S(2)}) collective-permute-start(bf16[2,2,2,96,768]{4,3,2,1,0:T(8,128)(2,1)S(1)} %pad_maximum_fusion.10), channel_id=1, source_target_pairs={{0,16},{4,20},{8,24},{12,28},{16,0},{20,4},{24,8},{28,12},{1,17},{... | collective-permute-start | bytes 3538952 | tf_op jit(solution)/shard_map/ppermute | solution.py:239
  192.0 17.7 %collective-permute-start.15 = (bf16[640,192]{1,0:T(8,128)(2,1)S(1)}, bf16[640,192]{1,0:T(8,128)(2,1)S(1)}, u32[]{:S(2)}, u32[]{:S(2)}) collective-permute-start(bf16[640,192]{1,0:T(8,128)(2,1)S(1)} %get-tuple-element.187), channel_id=1, source_target_pairs={{0,3},{1,2},{2,1},{3,0},{4,7},{5,6},{6,5},{7,4},{8,11},{9,10},{10,... | collective-permute-start | bytes 737288 | tf_op jit(solution)/shard_map/ppermute | solution.py:239
  209.6 5.8 %collective-permute-start.25 = (bf16[2,2,2,2,24,3072]{5,4,3,2,1,0:T(8,128)(2,1)S(1)}, bf16[2,2,2,2,24,3072]{5,4,3,2,1,0:T(8,128)(2,1)S(1)}, u32[]{:S(2)}, u32[]{:S(2)}) collective-permute-start(bf16[2,2,2,2,24,3072]{5,4,3,2,1,0:T(8,128)(2,1)S(1)} %pad_maximum_fusion.3), channel_id=1, source_target_pairs={{0,4},{4,0},{8,12},{12,8},{16,20},{20,16},{24,28},{28,24},{1,5},{5... | collective-permute-start | bytes 7077896 | tf_op jit(solution)/shard_map/ppermute | solution.py:239
  212.3 5.4 collective-permute-start.30
  252.6 14.5 %collective-permute-start.35 = (bf16[2,2,2,2,24,3072]{5,4,2,3,0,1:T(8,128)(2,1)S(1)}, bf16[2,2,2,2,24,3072]{5,4,2,3,0,1:T(8,128)(2,1)S(1)}, u32[]{:S(2)}, u32[]{:S(2)}) collective-permute-start(bf16[2,2,2,2,24,3072]{5,4,2,3,0,1:T(8,128)(2,1)S(1)} %select_bitcast_fusion.1), channel_id=1, source_target_pairs={{0,4},{4,0},{8,12},{12,8},{16,20},{20,16},{24,28},{28,24},{1,5},{5... | collective-permute-start | bytes 7077896 | tf_op jit(solution)/shard_map/ppermute | solution.py:239
  259.5 8.9 %collective-permute-start.34 = (bf16[2,2,2,2,96,768]{5,4,2,3,1,0:T(8,128)(2,1)S(1)}, bf16[2,2,2,2,96,768]{5,4,2,3,1,0:T(8,128)(2,1)}, u32[]{:S(2)}, u32[]{:S(2)}) collective-permute-start(bf16[2,2,2,2,96,768]{5,4,2,3,1,0:T(8,128)(2,1)S(1)} %select_bitcast_fusion.3), channel_id=1, source_target_pairs={{0,4},{4,0},{8,12},{12,8},{16,20},{20,16},{24,28},{28,24},{1,5},{5... | collective-permute-start | bytes 7077896 | tf_op jit(solution)/shard_map/ppermute | solution.py:239
  261.3 3.7 collective-permute-start.36
  261.7 15.9 %collective-permute-start.31 = (bf16[640,192]{1,0:T(8,128)(2,1)S(1)}, bf16[640,192]{1,0:T(8,128)(2,1)S(1)}, u32[]{:S(2)}, u32[]{:S(2)}) collective-permute-start(bf16[640,192]{1,0:T(8,128)(2,1)S(1)} %convolution_convert_fusion.9), channel_id=1, source_target_pairs={{0,1},{1,0},{2,3},{3,2},{4,5},{5,4},{6,7},{7,6},{8,9},{9,8},{10,11... | collective-permute-start | bytes 737288 | tf_op jit(solution)/shard_map/ppermute | solution.py:239
  263.3 25.5 %collective-permute-start.32 = (bf16[640,192]{1,0:T(8,128)(2,1)S(1)}, bf16[640,192]{1,0:T(8,128)(2,1)S(1)}, u32[]{:S(2)}, u32[]{:S(2)}) collective-permute-start(bf16[640,192]{1,0:T(8,128)(2,1)S(1)} %convolution_convert_fusion.8), channel_id=1, source_target_pairs={{0,2},{1,3},{2,0},{3,1},{4,6},{5,7},{6,4},{7,5},{8,10},{9,11},{10,... | collective-permute-start | bytes 737288 | tf_op jit(solution)/shard_map/ppermute | solution.py:239
  265.0 23.9 %collective-permute-start.33 = (bf16[640,192]{1,0:T(8,128)(2,1)S(1)}, bf16[640,192]{1,0:T(8,128)(2,1)S(1)}, u32[]{:S(2)}, u32[]{:S(2)}) collective-permute-start(bf16[640,192]{1,0:T(8,128)(2,1)S(1)} %convolution_convert_fusion.7), channel_id=1, source_target_pairs={{0,3},{1,2},{2,1},{3,0},{4,7},{5,6},{6,5},{7,4},{8,11},{9,10},{10,... | collective-permute-start | bytes 737288 | tf_op jit(solution)/shard_map/ppermute | solution.py:239
  315.0 33.3 %collective-permute-start.40 = (bf16[2,2,2,96,768]{4,3,1,2,0:T(8,128)(2,1)S(1)}, bf16[2,2,2,96,768]{4,3,1,2,0:T(8,128)(2,1)S(1)}, u32[]{:S(2)}, u32[]{:S(2)}) collective-permute-start(bf16[2,2,2,96,768]{4,3,1,2,0:T(8,128)(2,1)S(1)} %select_bitcast_fusion.11), channel_id=1, source_target_pairs={{0,16},{4,20},{8,24},{12,28},{16,0},{20,4},{24,8},{28,12},{1,17},{... | collective-permute-start | bytes 3538952 | tf_op jit(solution)/shard_map/ppermute | solution.py:239
  316.2 32.5 %collective-permute-start.41 = (bf16[2,2,2,24,3072]{4,3,1,2,0:T(8,128)(2,1)S(1)}, bf16[2,2,2,24,3072]{4,3,1,2,0:T(8,128)(2,1)S(1)}, u32[]{:S(2)}, u32[]{:S(2)}) collective-permute-start(bf16[2,2,2,24,3072]{4,3,1,2,0:T(8,128)(2,1)S(1)} %select_bitcast_fusion.9), channel_id=1, source_target_pairs={{0,8},{4,12},{8,0},{12,4},{16,24},{20,28},{24,16},{28,20},{1,9},{5... | collective-permute-start | bytes 3538952 | tf_op jit(solution)/shard_map/ppermute | solution.py:239
  316.9 31.3 %collective-permute-start.42 = (bf16[2,2,2,24,768]{4,3,1,2,0:T(8,128)(2,1)S(1)}, bf16[2,2,2,24,768]{4,3,1,2,0:T(8,128)(2,1)S(1)}, u32[]{:S(2)}, u32[]{:S(2)}) collective-permute-start(bf16[2,2,2,24,768]{4,3,1,2,0:T(8,128)(2,1)S(1)} %select_bitcast_fusion.43), channel_id=1, source_target_pairs={{0,8},{4,12},{8,0},{12,4},{16,24},{20,28},{24,16},{28,20},{1,9},{5... | collective-permute-start | bytes 884744 | tf_op jit(solution)/shard_map/ppermute | solution.py:239
  375.4 25.6 %collective-permute-start.53 = (bf16[2,2,24,768]{3,2,0,1:T(8,128)(2,1)}, bf16[2,2,24,768]{3,2,0,1:T(8,128)(2,1)}, u32[]{:S(2)}, u32[]{:S(2)}) collective-permute-start(bf16[2,2,24,768]{3,2,0,1:T(8,128)(2,1)} %select_bitcast_fusion.59), channel_id=1, source_target_pairs={{0,16},{4,20},{8,24},{12,28},{16,0},{20,4},{24,8},{28,12},{1,17},{... | collective-permute-start | bytes 442376 | tf_op jit(solution)/shard_map/ppermute | solution.py:239
  390.6 86.6 %collective-permute-start.37 = (bf16[640,576]{0,1:T(8,128)(2,1)}, bf16[640,576]{0,1:T(8,128)(2,1)S(1)}, u32[]{:S(2)}, u32[]{:S(2)}) collective-permute-start(bf16[640,576]{0,1:T(8,128)(2,1)} %copy.147), channel_id=1, source_target_pairs={{0,1},{1,0},{2,3},{3,2},{4,5},{5,4},{6,7},{7,6},{8,9},{9,8},{10,11... | collective-permute-start | bytes 2211848 | tf_op jit(solution)/shard_map/ppermute | solution.py:239
  398.7 79.4 %collective-permute-start.38 = (bf16[640,576]{0,1:T(8,128)(2,1)}, bf16[640,576]{0,1:T(8,128)(2,1)S(1)}, u32[]{:S(2)}, u32[]{:S(2)}) collective-permute-start(bf16[640,576]{0,1:T(8,128)(2,1)} %copy.148), channel_id=1, source_target_pairs={{0,2},{1,3},{2,0},{3,1},{4,6},{5,7},{6,4},{7,5},{8,10},{9,11},{10,... | collective-permute-start | bytes 2211848 | tf_op jit(solution)/shard_map/ppermute | solution.py:239
  399.2 79.8 %collective-permute-start.39 = (bf16[640,576]{0,1:T(8,128)(2,1)}, bf16[640,576]{0,1:T(8,128)(2,1)S(1)}, u32[]{:S(2)}, u32[]{:S(2)}) collective-permute-start(bf16[640,576]{0,1:T(8,128)(2,1)} %copy.149), channel_id=1, source_target_pairs={{0,3},{1,2},{2,1},{3,0},{4,7},{5,6},{6,5},{7,4},{8,11},{9,10},{10,... | collective-permute-start | bytes 2211848 | tf_op jit(solution)/shard_map/ppermute | solution.py:239
  402.1 63.5 %copy-start.8 = (bf16[2,2,2,24,3072]{4,3,1,2,0:T(8,128)(2,1)S(1)}, bf16[2,2,2,24,3072]{4,3,1,2,0:T(8,128)(2,1)}, u32[]{:S(2)}) copy-start(bf16[2,2,2,24,3072]{4,3,1,2,0:T(8,128)(2,1)} %add_convert_fusion.2) | copy-start | bytes 3538948
  402.1 43.6 %collective-permute-start.54 = (bf16[2,24,768]{2,1,0:T(8,128)(2,1)S(1)}, bf16[2,24,768]{2,1,0:T(8,128)(2,1)S(1)}, u32[]{:S(2)}, u32[]{:S(2)}) collective-permute-start(bf16[2,24,768]{2,1,0:T(8,128)(2,1)S(1)} %select_bitcast_fusion.72), channel_id=1, source_target_pairs={{0,1},{1,0},{2,3},{3,2},{4,5},{5,4},{6,7},{7,6},{8,9},{9,8},{10,11... | collective-permute-start | bytes 221192 | tf_op jit(solution)/shard_map/ppermute | solution.py:239
  404.6 61.0 %collective-permute-start.56 = (bf16[2,2,24,3072]{3,2,0,1:T(8,128)(2,1)S(1)}, bf16[2,2,24,3072]{3,2,0,1:T(8,128)(2,1)S(1)}, u32[]{:S(2)}, u32[]{:S(2)}) collective-permute-start(bf16[2,2,24,3072]{3,2,0,1:T(8,128)(2,1)S(1)} %select_bitcast_fusion.23), channel_id=1, source_target_pairs={{0,16},{4,20},{8,24},{12,28},{16,0},{20,4},{24,8},{28,12},{1,17},{... | collective-permute-start | bytes 1769480 | tf_op jit(solution)/shard_map/ppermute | solution.py:239
  445.7 18.9 %collective-permute-start.55 = (bf16[24,768]{1,0:T(8,128)(2,1)S(1)}, bf16[24,768]{1,0:T(8,128)(2,1)S(1)}, u32[]{:S(2)}, u32[]{:S(2)}) collective-permute-start(bf16[24,768]{1,0:T(8,128)(2,1)S(1)} %select_bitcast_fusion.81), channel_id=1, source_target_pairs={{0,2},{1,3},{2,0},{3,1},{4,6},{5,7},{6,4},{7,5},{8,10},{9,11},{10,... | collective-permute-start | bytes 110600 | tf_op jit(solution)/shard_map/ppermute | solution.py:239
  464.6 11.5 %collective-permute-start.59 = (bf16[2,2,96,768]{3,2,0,1:T(8,128)(2,1)S(1)}, bf16[2,2,96,768]{3,2,0,1:T(8,128)(2,1)S(1)}, u32[]{:S(2)}, u32[]{:S(2)}) collective-permute-start(bf16[2,2,96,768]{3,2,0,1:T(8,128)(2,1)S(1)} %select_bitcast_fusion.25), channel_id=1, source_target_pairs={{0,8},{4,12},{8,0},{12,4},{16,24},{20,28},{24,16},{28,20},{1,9},{5... | collective-permute-start | bytes 1769480 | tf_op jit(solution)/shard_map/ppermute | solution.py:239
  466.6 49.0 %collective-permute-start.57 = (bf16[2,24,3072]{2,1,0:T(8,128)(2,1)}, bf16[2,24,3072]{2,1,0:T(8,128)(2,1)}, u32[]{:S(2)}, u32[]{:S(2)}) collective-permute-start(bf16[2,24,3072]{2,1,0:T(8,128)(2,1)} %select_bitcast_fusion.41), channel_id=1, source_target_pairs={{0,1},{1,0},{2,3},{3,2},{4,5},{5,4},{6,7},{7,6},{8,9},{9,8},{10,11... | collective-permute-start | bytes 884744 | tf_op jit(solution)/shard_map/ppermute | solution.py:239
  477.1 33.6 %collective-permute-start.60 = (bf16[2,96,768]{2,1,0:T(8,128)(2,1)}, bf16[2,96,768]{2,1,0:T(8,128)(2,1)}, u32[]{:S(2)}, u32[]{:S(2)}) collective-permute-start(bf16[2,96,768]{2,1,0:T(8,128)(2,1)} %select_bitcast_fusion.40), channel_id=1, source_target_pairs={{0,1},{1,0},{2,3},{3,2},{4,5},{5,4},{6,7},{7,6},{8,9},{9,8},{10,11... | collective-permute-start | bytes 884744 | tf_op jit(solution)/shard_map/ppermute | solution.py:239
  502.0 27.5 %collective-permute-start.48 = (bf16[2,2,2,2,24,1152]{5,4,2,3,1,0:T(8,128)(2,1)}, bf16[2,2,2,2,24,1152]{5,4,2,3,1,0:T(8,128)(2,1)}, u32[]{:S(2)}, u32[]{:S(2)}) collective-permute-start(bf16[2,2,2,2,24,1152]{5,4,2,3,1,0:T(8,128)(2,1)} %select_bitcast_fusion.19), channel_id=1, source_target_pairs={{0,4},{4,0},{8,12},{12,8},{16,20},{20,16},{24,28},{28,24},{1,5},{5... | collective-permute-start | bytes 2654216 | tf_op jit(solution)/shard_map/ppermute | solution.py:239
  510.7 21.5 %collective-permute-start.43 = (bf16[2,2,2,2,24,1280]{5,4,3,2,1,0:T(8,128)(2,1)S(1)}, bf16[2,2,2,2,24,1280]{5,4,3,2,1,0:T(8,128)(2,1)S(1)}, u32[]{:S(2)}, u32[]{:S(2)}) collective-permute-start(bf16[2,2,2,2,24,1280]{5,4,3,2,1,0:T(8,128)(2,1)S(1)} %select_bitcast_fusion.16), channel_id=1, source_target_pairs={{0,4},{4,0},{8,12},{12,8},{16,20},{20,16},{24,28},{28,24},{1,5},{5... | collective-permute-start | bytes 2949128 | tf_op jit(solution)/shard_map/ppermute | solution.py:239
  512.7 14.0 %collective-permute-start.61 = (bf16[96,768]{1,0:T(8,128)(2,1)S(1)}, bf16[96,768]{1,0:T(8,128)(2,1)S(1)}, u32[]{:S(2)}, u32[]{:S(2)}) collective-permute-start(bf16[96,768]{1,0:T(8,128)(2,1)S(1)} %select_bitcast_fusion.56), channel_id=1, source_target_pairs={{0,2},{1,3},{2,0},{3,1},{4,6},{5,7},{6,4},{7,5},{8,10},{9,11},{10,... | collective-permute-start | bytes 442376 | tf_op jit(solution)/shard_map/ppermute | solution.py:239
  516.7 12.0 %collective-permute-start.58 = (bf16[24,3072]{1,0:T(8,128)(2,1)S(1)}, bf16[24,3072]{1,0:T(8,128)(2,1)S(1)}, u32[]{:S(2)}, u32[]{:S(2)}) collective-permute-start(bf16[24,3072]{1,0:T(8,128)(2,1)S(1)} %select_bitcast_fusion.57), channel_id=1, source_target_pairs={{0,2},{1,3},{2,0},{3,1},{4,6},{5,7},{6,4},{7,5},{8,10},{9,11},{10,... | collective-permute-start | bytes 442376 | tf_op jit(solution)/shard_map/ppermute | solution.py:239
  531.1 11.1 %collective-permute-start.49 = (bf16[2,2,2,24,1152]{4,3,1,2,0:T(8,128)(2,1)S(1)}, bf16[2,2,2,24,1152]{4,3,1,2,0:T(8,128)(2,1)S(1)}, u32[]{:S(2)}, u32[]{:S(2)}) collective-permute-start(bf16[2,2,2,24,1152]{4,3,1,2,0:T(8,128)(2,1)S(1)} %select_bitcast_fusion.37), channel_id=1, source_target_pairs={{0,16},{4,20},{8,24},{12,28},{16,0},{20,4},{24,8},{28,12},{1,17},{... | collective-permute-start | bytes 1327112 | tf_op jit(solution)/shard_map/ppermute | solution.py:239
  532.6 13.2 %collective-permute-start.44 = (bf16[2,2,2,24,1280]{4,3,2,1,0:T(8,128)(2,1)S(1)}, bf16[2,2,2,24,1280]{4,3,2,1,0:T(8,128)(2,1)S(1)}, u32[]{:S(2)}, u32[]{:S(2)}) collective-permute-start(bf16[2,2,2,24,1280]{4,3,2,1,0:T(8,128)(2,1)S(1)} %select_bitcast_fusion.34), channel_id=1, source_target_pairs={{0,8},{4,12},{8,0},{12,4},{16,24},{20,28},{24,16},{28,20},{1,9},{5... | collective-permute-start | bytes 1474568 | tf_op jit(solution)/shard_map/ppermute | solution.py:239
  542.4 6.8 %collective-permute-start.50 = (bf16[2,2,24,1152]{3,2,0,1:T(8,128)(2,1)S(1)}, bf16[2,2,24,1152]{3,2,0,1:T(8,128)(2,1)S(1)}, u32[]{:S(2)}, u32[]{:S(2)}) collective-permute-start(bf16[2,2,24,1152]{3,2,0,1:T(8,128)(2,1)S(1)} %select_bitcast_fusion.53), channel_id=1, source_target_pairs={{0,8},{4,12},{8,0},{12,4},{16,24},{20,28},{24,16},{28,20},{1,9},{5... | collective-permute-start | bytes 663560 | tf_op jit(solution)/shard_map/ppermute | solution.py:239
  549.3 4.8 collective-permute-start.51
  549.4 6.5 %collective-permute-start.45 = (bf16[2,2,24,1280]{3,2,1,0:T(8,128)(2,1)S(1)}, bf16[2,2,24,1280]{3,2,1,0:T(8,128)(2,1)S(1)}, u32[]{:S(2)}, u32[]{:S(2)}) collective-permute-start(bf16[2,2,24,1280]{3,2,1,0:T(8,128)(2,1)S(1)} %select_bitcast_fusion.50), channel_id=1, source_target_pairs={{0,16},{4,20},{8,24},{12,28},{16,0},{20,4},{24,8},{28,12},{1,17},{... | collective-permute-start | bytes 737288 | tf_op jit(solution)/shard_map/ppermute | solution.py:239
  554.2 5.4 collective-permute-start.52
  556.1 4.9 collective-permute-start.46
  561.1 5.2 collective-permute-start.47
  (60 other events, 492.9 us)

commit v3 on v2

v3 whole, which is shorter than its diff:
```python
import functools

import jax
import jax.numpy as jnp
from jax import lax
from jax.experimental import pallas as pl
from jax.experimental.layout import Layout, with_layout_constraint
from jax.experimental.pallas import tpu as pltpu
from jax.sharding import PartitionSpec as P

HEAD = 64
PASSES = 5
PASS_SLOTS = 512

masked_value = -1e30
both = ("seq", "blk")
f32 = jnp.float32
bf16 = jnp.bfloat16


def layer_norm(values, gain, offset):
    centre = values - jnp.mean(values, axis=-1, keepdims=True)
    spread = jnp.mean(centre * centre, axis=-1, keepdims=True)
    return centre * lax.rsqrt(spread + 1e-05) * gain + offset


def gelu_tanh(values):
    return jax.nn.gelu(values, approximate=True)


def contract(left, right, dims):
    return lax.dot_general(left, right, (dims, ((), ())), preferred_element_type=f32)


def tile_visible(length):
    key_place = lax.broadcasted_iota(jnp.int32, (PASS_SLOTS, PASS_SLOTS), 0)
    query_place = lax.broadcasted_iota(jnp.int32, (PASS_SLOTS, PASS_SLOTS), 1)
    return (key_place <= query_place) & (key_place < length)


def place_pieces(here, pieces, shelf, whole):
    span = pieces[0].shape[1]
    for step, piece in enumerate(pieces):
        shelf[here ^ step] = piece[...]
    for at in range(len(pieces)):
        whole[:, at * span : (at + 1) * span] = shelf[at]


def hand_out(here, whole, shelf, pieces):
    span = pieces[0].shape[1]
    for at in range(len(pieces)):
        shelf[at] = whole[:, at * span : (at + 1) * span]
    for step, piece in enumerate(pieces):
        piece[...] = shelf[here ^ step]


def turned(rows):
    return rows.astype(f32).T.astype(bf16)


def forward_kernel(groups, lengths, here, *refs):
    pieces, refs = refs[:groups], refs[groups:]
    packed, mixed, totals = refs[:3]
    outs, refs = refs[3 : 3 + groups], refs[3 + groups :]
    shelf, out_shelf, key_rows = refs
    place_pieces(here[0], pieces, shelf, packed)
    key_rows[...] = turned(packed[HEAD : 2 * HEAD, :])
    for query_index in range(PASSES):
        query_span = slice(query_index * PASS_SLOTS, (query_index + 1) * PASS_SLOTS)
        queries = packed[:HEAD, query_span] * jnp.asarray(0.125, bf16)
        top = jnp.full((1, PASS_SLOTS), masked_value, f32)
        total = jnp.zeros((1, PASS_SLOTS), f32)
        acc = jnp.zeros((HEAD, PASS_SLOTS), f32)
        for key_index in range(query_index + 1):
            key_span = slice(key_index * PASS_SLOTS, (key_index + 1) * PASS_SLOTS)
            scores = contract(key_rows[key_span, :], queries, ((1,), (0,)))
            scores = jnp.where(tile_visible(lengths[0, key_index]), scores, masked_value)
            newest = jnp.maximum(top, jnp.max(scores, axis=0, keepdims=True))
            shares = jnp.exp(scores - newest)
            fade = jnp.exp(top - newest)
            total = total * fade + jnp.sum(shares, axis=0, keepdims=True)
            values = packed[2 * HEAD :, key_span]
            acc = acc * fade + contract(values, shares.astype(bf16), ((1,), (0,)))
            top = newest
        mixed[:, query_span] = (acc / total).astype(bf16)
        totals[query_index : query_index + 1, :] = top + jnp.log(total)
    hand_out(here[0], mixed, out_shelf, outs)


def backward_kernel(groups, lengths, here, packed, mixed, totals, *refs):
    pieces, refs = refs[:groups], refs[groups:]
    outs, refs = refs[:groups], refs[groups:]
    shelf, out_shelf, grad, rows, grad_rows, grad_query, result = refs
    place_pieces(here[0], pieces, shelf, grad)
    rows[...] = turned(packed[...])
    grad_rows[...] = turned(grad[...])
    grad_query[...] = jnp.zeros_like(grad_query)
    eighth = jnp.asarray(0.125, bf16)

    def key_pass(key_index, _):
        key_at = pl.multiple_of(key_index * PASS_SLOTS, PASS_SLOTS)
        key_span = pl.ds(key_at, PASS_SLOTS)
        keys = rows[key_span, HEAD : 2 * HEAD] * eighth
        keys_turned = packed[HEAD : 2 * HEAD, key_span] * eighth
        values = rows[key_span, 2 * HEAD :]
        shown = tile_visible(lengths[0, key_index])

        def query_pass(query_index, carried):
            grad_key, grad_value = carried
            query_at = pl.multiple_of(query_index * PASS_SLOTS, PASS_SLOTS)
            query_span = pl.ds(query_at, PASS_SLOTS)
            grads = grad[:, query_span]
            product = grads.astype(f32) * mixed[:, query_span].astype(f32)
            delta = jnp.sum(product, axis=0, keepdims=True)
            scores = contract(keys, packed[:HEAD, query_span], ((1,), (0,)))
            shares = jnp.exp(scores - totals[pl.ds(query_index, 1), :])
            shares = jnp.where(shown, shares, 0.0)
            grad_shares = contract(values, grads, ((1,), (0,)))
            grad_scores = (shares * (grad_shares - delta)).astype(bf16)
            grad_query[:, query_span] += contract(keys_turned, grad_scores, ((1,), (0,)))
            grad_value += contract(shares.astype(bf16), grad_rows[query_span, :], ((1,), (0,)))
            queries = rows[query_span, :HEAD] * eighth
            grad_key += contract(grad_scores, queries, ((1,), (0,)))
            return grad_key, grad_value

        empty = jnp.zeros((PASS_SLOTS, HEAD), f32)
        grad_key, grad_value = lax.fori_loop(key_index, PASSES, query_pass, (empty, empty))
        result[HEAD : 2 * HEAD, key_span] = grad_key.T.astype(bf16)
        result[2 * HEAD :, key_span] = grad_value.T.astype(bf16)
        return 0

    lax.fori_loop(0, PASSES, key_pass, 0)
    result[:HEAD, :] = grad_query[...].astype(bf16)
    hand_out(here[0], result, out_shelf, outs)


in_vmem = functools.partial(pl.BlockSpec, memory_space=pltpu.VMEM)
in_smem = functools.partial(pl.BlockSpec, memory_space=pltpu.SMEM)


def attend(lengths, here, pieces):
    groups = len(pieces)
    triple, span = pieces[0].shape
    slots = span * groups
    return pl.pallas_call(
        functools.partial(forward_kernel, groups),
        out_shape=[
            jax.ShapeDtypeStruct((triple, slots), bf16),
            jax.ShapeDtypeStruct((HEAD, slots), bf16),
            jax.ShapeDtypeStruct((PASSES, PASS_SLOTS), f32),
        ]
        + [jax.ShapeDtypeStruct((HEAD, span), bf16)] * groups,
        in_specs=[in_smem(), in_smem()] + [in_vmem()] * groups,
        out_specs=[in_vmem()] * (3 + groups),
        scratch_shapes=[
            pltpu.VMEM((groups, triple, span), bf16),
            pltpu.VMEM((groups, HEAD, span), bf16),
            pltpu.VMEM((slots, HEAD), bf16),
        ],
        compiler_params=pltpu.CompilerParams(vmem_limit_bytes=32 << 20),
        cost_estimate=pl.CostEstimate(flops=10**10, transcendentals=0, bytes_accessed=10**6),
        name="attend",
    )(lengths, here, *pieces)


def attend_back(lengths, here, packed, mixed, totals, pieces):
    groups = len(pieces)
    triple, slots = packed.shape
    span = slots // groups
    return pl.pallas_call(
        functools.partial(backward_kernel, groups),
        out_shape=[jax.ShapeDtypeStruct((triple, span), bf16)] * groups,
        in_specs=[in_smem(), in_smem()] + [in_vmem()] * (3 + groups),
        out_specs=[in_vmem()] * groups,
        scratch_shapes=[
            pltpu.VMEM((groups, HEAD, span), bf16),
            pltpu.VMEM((groups, triple, span), bf16),
            pltpu.VMEM((HEAD, slots), bf16),
            pltpu.VMEM((slots, triple), bf16),
            pltpu.VMEM((slots, HEAD), bf16),
            pltpu.VMEM((HEAD, slots), f32),
            pltpu.VMEM((triple, slots), bf16),
        ],
        compiler_params=pltpu.CompilerParams(vmem_limit_bytes=32 << 20),
        cost_estimate=pl.CostEstimate(
            flops=15 * 10**9, transcendentals=0, bytes_accessed=10**6
        ),
        name="attend_back",
    )(lengths, here, packed, mixed, totals, *pieces)


def row_major(values):
    return with_layout_constraint(values, Layout(tuple(range(values.ndim))))


def after(values, *others):
    return lax.optimization_barrier((values, others))[0]


def swap_with(values, axis, step):
    size = lax.axis_size(axis)
    return lax.ppermute(values, axis, [(i, i ^ step) for i in range(size)])


def axis_bits(axis):
    size = lax.axis_size(axis)
    assert size & (size - 1) == 0
    return [(axis, 1 << n) for n in reversed(range(size.bit_length() - 1))]


def bit_order(flip):
    places = axis_bits("seq") + axis_bits("blk")
    near = axis_bits("seq")
    far = near[:-1][::-1] if flip else near[:-1]
    return places, axis_bits("blk") + far + near[-1:]


def own_bit(bit):
    return (lax.axis_index(bit[0]) & bit[1]) != 0


class Gather:
    def __init__(self, piece, flip):
        self.places, self.order = bit_order(flip)
        self.shape = piece.shape
        self.piece = piece
        self.done = []

    def grow(self, count=None):
        count = len(self.order) if count is None else count
        for bit in self.order[:count]:
            other = swap_with(self.piece, *bit)
            self.done = sorted(self.done + [bit], key=self.places.index)
            mine = own_bit(bit)
            low = jnp.where(mine, other, self.piece)
            high = jnp.where(mine, self.piece, other)
            self.piece = jnp.stack([low, high], axis=self.done.index(bit))
        self.order = self.order[count:]
        return self.piece

    def whole(self):
        return self.grow().reshape((-1,) + self.shape[1:])


class Scatter:
    def __init__(self, whole, flip):
        self.left, order = bit_order(flip)
        self.order = order[::-1]
        rows = whole.shape[0] >> len(order)
        self.piece = whole.reshape((2,) * len(order) + (rows,) + whole.shape[1:])

    def send(self):
        bit, self.order = self.order[0], self.order[1:]
        at = self.left.index(bit)
        self.left = [place for place in self.left if place != bit]
        low = lax.index_in_dim(self.piece, 0, at, keepdims=False)
        high = lax.index_in_dim(self.piece, 1, at, keepdims=False)
        mine = own_bit(bit)
        self.bit = bit
        self.sent = jnp.where(mine, low, high)
        self.kept = jnp.where(mine, high, low)
        return (self.sent, self.kept)

    def receive(self):
        other = swap_with(self.sent, *self.bit)
        self.piece = (self.kept.astype(f32) + other.astype(f32)).astype(bf16)

    def finish(self):
        while self.order:
            self.send()
            self.receive()
        return self.piece


def swap_pieces(pieces):
    return [swap_with(piece, "blk", step) if step else piece for step, piece in enumerate(pieces)]


def in_order(pieces):
    here = lax.axis_index("blk")
    result = jnp.zeros((len(pieces),) + pieces[0].shape, pieces[0].dtype)
    for step, piece in enumerate(pieces):
        result = lax.dynamic_update_index_in_dim(result, piece, here ^ step, 0)
    return result


def at_group(values, group):
    return lax.dynamic_index_in_dim(values, group, 0, keepdims=False)


def by_head(rows, groups):
    count = rows.shape[0]
    return rows.reshape(count, 3, groups, -1, HEAD).transpose(0, 3, 2, 1, 4).reshape(count, -1)


def by_kind(rows, groups):
    count = rows.shape[0]
    return rows.reshape(count, -1, groups, 3, HEAD).transpose(0, 3, 2, 1, 4).reshape(count, -1)


def norm_parts(values):
    centre = values - jnp.mean(values, axis=-1, keepdims=True)
    spread = jnp.mean(centre * centre, axis=-1, keepdims=True)
    scale = lax.rsqrt(spread + 1e-05)
    return centre * scale, scale


def norm_back(values, gain, grad):
    hat, scale = norm_parts(values)
    edge = grad * gain
    part = scale * (
        edge
        - jnp.mean(edge, axis=-1, keepdims=True)
        - hat * jnp.mean(edge * hat, axis=-1, keepdims=True)
    )
    return part, jnp.sum(grad * hat, axis=0), jnp.sum(grad, axis=0)


def on_device(states, cotangent, lengths, w_qkv, w_out, w_up, w_down, vectors, up_bias):
    _, row_count, width = states.shape
    groups = lax.axis_size("blk")
    own = w_qkv.shape[0]
    wide = w_up.shape[1]
    ratio = wide // width
    vector_count = vectors.shape[0]
    heads = width // HEAD // groups
    span = 3 * HEAD
    small = vector_count + ratio

    here = lax.axis_index("blk").astype(jnp.int32)
    parts = by_head(w_qkv, groups)
    middle_column = parts.shape[1] // 2
    extra = [vectors.T, up_bias.reshape(own, ratio), jnp.zeros((own, -small % 128), bf16)]
    streams = [
        Gather(jnp.concatenate([parts[:, :middle_column]] + extra, axis=1), False),
        Gather(parts[:, middle_column:], True),
    ]
    blk_steps = len(axis_bits("blk"))
    begun = [stream.grow(blk_steps) for stream in streams]
    w_out, w_up, w_down = after((w_out, w_up, w_down), begun)
    later = [Gather(w_up, False), Gather(w_down, True), Gather(w_out, False)]
    for one in later:
        one.grow(blk_steps)
    first = [stream.whole() for stream in streams]
    for one in later:
        one.piece = after(one.piece, first)
        one.grow(1)
    full_qkv = jnp.concatenate([first[0][:, :middle_column], first[1]], axis=1)
    head_qkv = [full_qkv[:, h * groups * span : (h + 1) * groups * span] for h in range(heads)]
    corner = first[0][:, middle_column : middle_column + small]
    table = corner[:, :vector_count].astype(f32).T
    bias_up = corner[:, vector_count:].astype(f32).reshape(wide)

    slots = lax.axis_index("blk") * row_count + jnp.arange(row_count, dtype=jnp.int32)
    pass_of = (slots // PASS_SLOTS)[:, None] == jnp.arange(PASSES, dtype=jnp.int32)[None, :]
    bounds = jnp.sum(jnp.where(pass_of, lengths[0][None, :], 0), axis=1)
    live = (slots % PASS_SLOTS < bounds).astype(f32)[:, None]

    added = jnp.zeros((row_count, width), f32)
    for index in range(PASSES):
        added = jnp.where(pass_of[:, index : index + 1], table[index], added)
    start = states[0].astype(f32) + added
    normed_a = layer_norm(start, table[5], table[6]).astype(bf16)
    bias_three = jnp.concatenate([table[7], jnp.zeros_like(table[7]), table[8]])
    bias_three = by_head(bias_three[None], groups).reshape(heads, -1, 1)
    sending = []
    for h in range(heads):
        rows = contract(head_qkv[h], normed_a, ((0,), (1,))) + bias_three[h]
        rows = rows.astype(bf16).reshape(groups, span, row_count)
        sending.append([row_major(at_group(rows, here ^ step)) for step in range(groups)])
    for one in later:
        one.piece = after(one.piece, sending)
    kept = []
    arrived = []
    returned = []
    for h in range(heads):
        pieces = swap_pieces(after(sending[h], arrived))
        arrived = pieces
        packed, mixed, totals, *pieces = attend(lengths, here[None], pieces)
        kept.append((packed, mixed, totals))
        returned.append(in_order(swap_pieces(pieces)))
    full_up, full_down, full_out = [one.whole() for one in later]
    heads_out = jnp.stack(returned, axis=1).reshape(width, row_count)
    middle = start + live * (contract(heads_out, full_out, ((0,), (0,))) + table[9])
    normed_b = layer_norm(middle, table[10], table[11]).astype(bf16)
    up_sum = contract(normed_b, full_up, ((1,), (0,))) + bias_up
    activated, gelu_pull = jax.vjp(gelu_tanh, up_sum)
    hidden = activated.astype(bf16)
    incoming = cotangent[0].astype(f32)
    grad_branch = (live * incoming).astype(bf16)
    grad_hidden = contract(grad_branch, full_down, ((1,), (1,)))
    grad_upsum = gelu_pull(grad_hidden)[0].astype(bf16)
    grad_normb = contract(grad_upsum, full_up, ((1,), (1,)))
    middle_part, gain_grad_b, shift_grad_b = norm_back(middle, table[10], grad_normb)
    grad_middle = incoming + middle_part
    grad_attn = (live * grad_middle).astype(bf16)
    grad_heads = contract(full_out, grad_attn, ((1,), (1,))).astype(bf16)
    grad_heads = grad_heads.reshape(groups, heads, HEAD, row_count)
    sending = [
        [row_major(at_group(grad_heads[:, h], here ^ step)) for step in range(groups)]
        for h in range(heads)
    ]
    arrived = []
    late = []
    parts = []
    for h in range(heads):
        pieces = swap_pieces(after(sending[h], arrived))
        arrived = pieces
        if late:
            for one in late:
                one.piece = after(one.piece, parts[-1])
            sent = [one.send() for one in late]
            for one in late:
                one.receive()
            pieces = after(pieces, sent)
        back = attend_back(lengths, here[None], *kept[h], pieces)
        if not late:
            hidden_late, grad_branch_late, grad_upsum_late, grad_attn_late = after(
                (hidden, grad_branch, grad_upsum, grad_attn), back
            )
            grad_down = contract(hidden_late, grad_branch_late, ((0,), (0,))).astype(bf16)
            grad_up = contract(normed_b, grad_upsum_late, ((0,), (0,))).astype(bf16)
            grad_out = contract(heads_out, grad_attn_late, ((1,), (0,))).astype(bf16)
            late = [Scatter(grad_down, True), Scatter(grad_up, False), Scatter(grad_out, False)]
        parts.append(back)
    grad_projected = [in_order(swap_pieces(back)) for back in parts]
    for one in late:
        one.piece = after(one.piece, parts[-1])
    grad_down, grad_up, grad_out = [one.finish() for one in late]
    outcome = middle + live * (contract(hidden, full_down, ((1,), (0,))) + table[12])

    grad_projected = [part.reshape(groups * span, row_count) for part in grad_projected]
    grad_qkv = [
        row_major(contract(normed_a, part, ((0,), (1,))).astype(bf16)) for part in grad_projected
    ]
    grad_qkv = [Scatter(part, h % 2 == 1).finish() for h, part in enumerate(grad_qkv)]
    sums = [jnp.sum(part.astype(f32), axis=1) for part in grad_projected]
    column_sums = by_kind(jnp.concatenate(sums)[None], groups)[0]
    grad_norma = sum(
        contract(part, weights, ((0,), (1,))) for part, weights in zip(grad_projected, head_qkv)
    )
    start_part, gain_grad_a, shift_grad_a = norm_back(start, table[5], grad_norma)
    grad_start = grad_middle + start_part
    grad_embed = [
        jnp.sum(jnp.where(pass_of[:, index : index + 1], grad_start, 0.0), axis=0)
        for index in range(PASSES)
    ]
    vector_grads = jnp.stack(
        grad_embed
        + [
            gain_grad_a,
            shift_grad_a,
            column_sums[:width],
            column_sums[2 * width :],
            jnp.sum(grad_attn.astype(f32), axis=0),
            gain_grad_b,
            shift_grad_b,
            jnp.sum(grad_branch.astype(f32), axis=0),
        ]
    )
    bias_grads = jnp.sum(grad_upsum.astype(f32), axis=0)
    extra = [vector_grads.T.astype(bf16), bias_grads.reshape(width, ratio).astype(bf16)]
    extra = jnp.concatenate(extra + [jnp.zeros((width, -small % 128), bf16)], axis=1)
    extra = Scatter(extra, False).finish().astype(f32)
    return (
        outcome.astype(bf16)[None],
        grad_start.astype(bf16)[None],
        by_kind(jnp.concatenate(grad_qkv, axis=1).astype(f32), groups),
        grad_out.astype(f32),
        grad_up.astype(f32),
        grad_down.astype(f32),
        extra[:, :vector_count].T,
        extra[:, vector_count:small].reshape(own * ratio),
    )


def solution(mesh):
    split = P(both, None)
    return jax.shard_map(
        on_device,
        mesh=mesh,
        in_specs=(
            P("seq", "blk", None),
            P("seq", "blk", None),
            P("seq", None),
            split,
            split,
            split,
            split,
            P(None, both),
            P(both),
        ),
        out_specs=(
            P("seq", "blk", None),
            P("seq", "blk", None),
            split,
            split,
            split,
            split,
            P(None, both),
            P(both),
        ),
        check_vma=False,
    )
```

time: 578 us -> 572 us (0.990)
  starting transfers between devices: 82.6 us -> 110 us
  waiting for transfers between devices: 243 us -> 217 us
  local copies, waits for them, and re-layouts: 59.1 us -> 34.8 us
  other arithmetic: 49.7 us -> 59.7 us
    ppermute x62 -> x96, starting transfers between devices: 82.6 us -> 110 us  [swap_with(): return lax.ppermute(values, axis, [(i, i ^ step) for i in range(size)])]
    ppermute x62 -> x96, waiting for transfers between devices: 243 us -> 217 us  [swap_with(): return lax.ppermute(values, axis, [(i, i ^ step) for i in range(size)])]
    another operation x17 -> x8, local copies, waits for them, and re-layouts: 13.8 us -> 0.49 us  [the longest x6 10.5 us: row_major(): return with_layout_constraint(values, Layout(tuple(range(values.ndim))))]
    unnamed x130 -> x204, local copies, waits for them, and re-layouts: 17.8 us -> 6.69 us
    select_n x25 -> x35, other arithmetic: 6.05 us -> 14.5 us  [send(): self.sent = jnp.where(mine, low, high)]
    another operation x50, other arithmetic: 16.2 us -> 8.68 us  [grow(): self.piece = jnp.stack([low, high], axis=self.done.index(bit))]
    convert_element_type x20 -> x31, other arithmetic: 12.5 us -> 17.6 us  [receive(): self.piece = (self.kept.astype(f32) + other.astype(f32)).astype(bf16)]
    dot_general x24 -> x18, matrix products: 58.2 us -> 63.1 us  [contract(): lax.dot_general(left, right, (dims, ((), ())), preferred_element_type=f32)]
  transfers between devices with their start and end apart: 62 -> 96, of which waited for: 33 -> 51; matrix products, arithmetic and copies ran while one was open for 18% -> 17% of each run, Pallas kernels for 5% -> 10%
where the time goes in v3:
time: 572 us; the launch traced here: 564 us
  waiting for transfers between devices  217 us (38%)
  starting transfers between devices  110 us (19%)
  Pallas kernels  75.7 us (13%)
  matrix products  63.1 us (11%)
  other arithmetic  59.7 us (10%)
  local copies, waits for them, and re-layouts  34.8 us (6%)
    ppermute x96, waiting for transfers between devices, swap_with(): return lax.ppermute(values, axis, [(i, i ^ step) for i in range(size)])  217 us
    ppermute x96, starting transfers between devices, swap_with(): return lax.ppermute(values, axis, [(i, i ^ step) for i in range(size)])  110 us
    dot_general x18, matrix products, contract(): lax.dot_general(left, right, (dims, ((), ())), preferred_element_type=f32)  63.1 us
    pallas_call x3, Pallas kernels, attend_back(): pl.pallas_call(functools.partial(backward_kernel, groups), out_shape=[jax...  53.5 us
    pallas_call x3, Pallas kernels, attend(): pl.pallas_call(functools.partial(forward_kernel, groups), out_shape=[jax....  22.2 us
    convert_element_type x31, other arithmetic, receive(): self.piece = (self.kept.astype(f32) + other.astype(f32)).astype(bf16)  17.6 us
    select_n x35, other arithmetic, send(): self.sent = jnp.where(mine, low, high)  14.5 us
  transfers between devices with their start and end apart: 96, of which 51 were waited for; matrix products, arithmetic and copies ran while one was open for 17% of the time, Pallas kernels for 10%

profile of v3, /device:TPU:0, one launch (start us, length us, event | category | flops | bytes accessed | tf_op | source)
XLA Modules:
  0.0 564.1 jit_solution(5854282432712056287)
XLA Ops:
  2.1 4.1 collective-permute-start.11
  19.4 3.1 collective-permute-start.28
  29.7 3.2 collective-permute-start.33
  34.3 4.7 collective-permute-done.33
  42.3 6.6 %collective-permute-done.34 = bf16[2,24,3072]{2,1,0:T(8,128)(2,1)S(1)} collective-permute-done((bf16[2,24,3072]{2,1,0:T(8,128)(2,1)S(1)}, bf16[2,24,3072]{2,1,0:T(8,128)(2,1)S(1)}, u32[]{:S(2)}, u32[]{:S(2)}) %collective-permute-start.34) | collective-permute-done | bytes 294944 | tf_op jit(solution)/shard_map/ppermute | solution.py:202
  48.9 3.1 collective-permute-done.39
  59.4 2.7 slice_reduce_fusion
  64.0 2.6 add_convert_fusion.9
  66.6 2.7 fusion.37
  75.0 3.7 collective-permute-start.7
  89.1 5.8 %collective-permute-done.6.refs_2_ = bf16[192,640]{1,0:T(8,128)(2,1)S(1)} collective-permute-done((bf16[192,640]{1,0:T(8,128)(2,1)}, bf16[192,640]{1,0:T(8,128)(2,1)S(1)}, u32[]{:S(2)}, u32[]{:S(2)}) %collective-permute-start.6) | collective-permute-done | bytes 245792 | tf_op jit(solution)/shard_map/ppermute | solution.py:202
  94.9 5.0 collective-permute-start.16
  99.9 7.3 %attend.3 = (bf16[192,2560]{1,0:T(8,128)(2,1)S(1)}, bf16[64,2560]{1,0:T(8,128)(2,1)S(1)}, f32[5,512]{1,0:T(8,128)S(1)}, bf16[64,640]{1,0:T(8,128)(2,1)S(1)}, bf1...) custom-call(s32[1,5]{1,0:T(1,128)S(1)} %copy-done, s32[1]{0:T(128)} %bitcast.16.here, ...), custom_call_target="tpu_custom_call" | custom-call | flops 10000000000 | bytes 1000000 | tf_op jit(solution)/shard_map/attend/pallas_call | solution.py:145
  107.3 4.4 collective-permute-done.8
  111.7 6.5 %collective-permute-done.9 = bf16[64,640]{1,0:T(8,128)(2,1)S(1)} collective-permute-done((bf16[64,640]{1,0:T(8,128)(2,1)S(1)}, bf16[64,640]{1,0:T(8,128)(2,1)S(1)}, u32[]{:S(2)}, u32[]{:S(2)}) %collective-permute-start.9) | collective-permute-done | bytes 81952 | tf_op jit(solution)/shard_map/ppermute | solution.py:202
  119.7 5.7 %collective-permute-done.10 = bf16[64,640]{1,0:T(8,128)(2,1)S(1)} collective-permute-done((bf16[64,640]{1,0:T(8,128)(2,1)S(1)}, bf16[64,640]{1,0:T(8,128)(2,1)S(1)}, u32[]{:S(2)}, u32[]{:S(2)}) %collective-permute-start.10) | collective-permute-done | bytes 81952 | tf_op jit(solution)/shard_map/ppermute | solution.py:202
  127.2 11.9 %collective-permute-done.17.refs_2_ = bf16[192,640]{1,0:T(8,128)(2,1)S(1)} collective-permute-done((bf16[192,640]{1,0:T(8,128)(2,1)S(1)}, bf16[192,640]{1,0:T(8,128)(2,1)S(1)}, u32[]{:S(2)}, u32[]{:S(2)}) %collective-permute-start.17) | collective-permute-done | bytes 245792 | tf_op jit(solution)/shard_map/ppermute | solution.py:202
  139.1 5.2 collective-permute-start.22
  144.2 7.4 %attend.4 = (bf16[192,2560]{1,0:T(8,128)(2,1)S(1)}, bf16[64,2560]{1,0:T(8,128)(2,1)S(1)}, f32[5,512]{1,0:T(8,128)S(1)}, bf16[64,640]{1,0:T(8,128)(2,1)S(1)}, bf1...) custom-call(s32[1,5]{1,0:T(1,128)S(1)} %copy-done, s32[1]{0:T(128)} %bitcast.16.here, ...), custom_call_target="tpu_custom_call" | custom-call | flops 10000000000 | bytes 1000000 | tf_op jit(solution)/shard_map/attend/pallas_call | solution.py:145
  151.9 4.4 collective-permute-done.19
  157.2 5.6 collective-permute-done.20
  165.1 4.8 collective-permute-done.21
  175.3 9.1 %collective-permute-done.23.refs_2_ = bf16[192,640]{1,0:T(8,128)(2,1)S(1)} collective-permute-done((bf16[192,640]{1,0:T(8,128)(2,1)S(1)}, bf16[192,640]{1,0:T(8,128)(2,1)S(1)}, u32[]{:S(2)}, u32[]{:S(2)}) %collective-permute-start.23) | collective-permute-done | bytes 245792 | tf_op jit(solution)/shard_map/ppermute | solution.py:202
  184.4 7.5 %attend.5 = (bf16[192,2560]{1,0:T(8,128)(2,1)S(1)}, bf16[64,2560]{1,0:T(8,128)(2,1)S(1)}, f32[5,512]{1,0:T(8,128)S(1)}, bf16[64,640]{1,0:T(8,128)(2,1)S(1)}, bf1...) custom-call(s32[1,5]{1,0:T(1,128)S(1)} %copy-done, s32[1]{0:T(128)} %bitcast.16.here, ...), custom_call_target="tpu_custom_call" | custom-call | flops 10000000000 | bytes 1000000 | tf_op jit(solution)/shard_map/attend/pallas_call | solution.py:145
  191.9 5.5 collective-permute-start.25
  201.5 4.8 collective-permute-done.26
  212.2 2.6 collective-permute-done.42
  215.8 8.0 %multiply_convert_fusion = (bf16[640,3072]{1,0:T(8,128)(2,1)}, f32[640,3072]{1,0:T(8,128)}) fusion(f32[3072]{0:T(1024)S(1)} %copy-done.82, bf16[768,3072]{1,0:T(8,128)(2,1)S(1)} %bitcast.558, f32[640,768]{1,0:T(8,128)S(1)} %get-tuple-element.334, f32[768]{0:T(1024)S(1)} %copy-done.90, f32[768]{0:T(1024)S(1)} %copy-done.81, f32[640]{0:T(1024)S(1)} %add_rsqrt_fusion, ...), kind=kOutput, calls=%fused_computation.9 | convolution fusion | flops 3042017280 | bytes 18504704 | tf_op jit(solution)/shard_map/dot_general | solution.py:32
  223.8 12.3 %fusion.93 = (bf16[3072]{0:T(1024)(128)(2,1)}, bf16[640,3072]{1,0:T(8,128)(2,1)}) fusion(f32[640,3072]{1,0:T(8,128)} %get-tuple-element.336, f32[3072]{0:T(1024)S(1)} %copy-done.82, bf16[3072,768]{1,0:T(8,128)(2,1)S(1)} %bitcast.556, bf16[1,640,768]{2,1,0:T(8,128)(2,1)S(1)} %copy-done.39, f32[640]{0:T(1024)S(1)} %copy-done.80), kind=kOutput, calls=%fused_computation.375 | convolution fusion | flops 3064624128 | bytes 17519104 | tf_op jit(solution)/shard_map/dot_general | solution.py:32
  236.1 6.5 %multiply_reduce_fusion = (bf16[768]{0:T(1024)(128)(2,1)S(1)}, f32[640]{0:T(1024)S(1)}, f32[640]{0:T(1024)S(1)}, bf16[768]{0:T(1024)(128)(2,1)}, f32[640,768]{1,0:T(8,128)S(1)}) fusion(f32[640,768]{1,0:T(8,128)S(1)} %get-tuple-element.334, f32[640]{0:T(1024)S(1)} %add_rsqrt_fusion, f32[640]{0:T(1024)S(1)} %broadcast_multiply_fusion.4, ...), kind=kOutput, calls=%fused_computation.43 | convolution fusion | flops 3024319744 | bytes 12599296 | tf_op jit(solution)/shard_map/dot_general | solution.py:32
  242.6 2.8 fusion.82
  248.5 3.4 collective-permute-start.45
  251.8 4.2 fusion.17
  257.2 17.7 %attend_back.3 = (bf16[192,640]{1,0:T(8,128)(2,1)S(1)}, bf16[192,640]{1,0:T(8,128)(2,1)S(1)}, bf16[192,640]{1,0:T(8,128)(2,1)S(1)}, bf16[192,640]{1,0:T(8,128)(2,1)S(1)}) custom-call(s32[1,5]{1,0:T(1,128)S(1)} %copy-done, s32[1]{0:T(128)} %bitcast.16.here, bf16[192,2560]{1,0:T(8,128)(2,1)S(1)} %get-tuple-element.128.packed, ...), custom_call_target="tpu_custom_call" | custom-call | flops 15000000512 | bytes 1000000 | tf_op jit(solution)/shard_map/attend_back/pallas_call | solution.py:170
  274.9 4.3 convolution_convert_fusion.1
  283.8 4.9 convolution_convert_fusion
  288.7 2.8 select_bitcast_fusion.1
  298.5 2.6 convolution_convert_fusion.5
  301.1 5.9 %collective-permute-done.49.refs_1_ = bf16[64,640]{1,0:T(8,128)(2,1)S(1)} collective-permute-done((bf16[64,640]{1,0:T(8,128)(2,1)S(1)}, bf16[64,640]{1,0:T(8,128)(2,1)S(1)}, u32[]{:S(2)}, u32[]{:S(2)}) %collective-permute-start.49) | collective-permute-done | bytes 81952 | tf_op jit(solution)/shard_map/ppermute | solution.py:202
  309.3 4.8 collective-permute-done.51.refs_3_
  315.5 13.1 %collective-permute-done.47 = bf16[192,640]{1,0:T(8,128)(2,1)S(1)} collective-permute-done((bf16[192,640]{1,0:T(8,128)(2,1)S(1)}, bf16[192,640]{1,0:T(8,128)(2,1)S(1)}, u32[]{:S(2)}, u32[]{:S(2)}) %collective-permute-start.47) | collective-permute-done | bytes 245792 | tf_op jit(solution)/shard_map/ppermute | solution.py:202
  331.0 3.1 add_convert_fusion.1
  334.2 3.8 add_convert_fusion
  338.0 17.9 %attend_back.4 = (bf16[192,640]{1,0:T(8,128)(2,1)S(1)}, bf16[192,640]{1,0:T(8,128)(2,1)S(1)}, bf16[192,640]{1,0:T(8,128)(2,1)S(1)}, bf16[192,640]{1,0:T(8,128)(2,1)S(1)}) custom-call(s32[1,5]{1,0:T(1,128)S(1)} %copy-done, s32[1]{0:T(128)} %bitcast.16.here, bf16[192,2560]{1,0:T(8,128)(2,1)S(1)} %get-tuple-element.139.packed, bf16[64,2560]{1,0:T(8,128)(2,1)S(1)} %copy-done.2, ...), custom_call_target="tpu_custom_call" | custom-call | flops 15000000512 | bytes 1000000 | tf_op jit(solution)/shard_map/attend_back/pallas_call | solution.py:170
  356.1 2.9 collective-permute-start.53
  362.2 6.0 %collective-permute-done.52 = bf16[192,640]{1,0:T(8,128)(2,1)S(1)} collective-permute-done((bf16[192,640]{1,0:T(8,128)(2,1)S(1)}, bf16[192,640]{1,0:T(8,128)(2,1)S(1)}, u32[]{:S(2)}, u32[]{:S(2)}) %collective-permute-start.52) | collective-permute-done | bytes 245792 | tf_op jit(solution)/shard_map/ppermute | solution.py:202
  370.7 6.3 %collective-permute-done.54 = bf16[192,640]{1,0:T(8,128)(2,1)S(1)} collective-permute-done((bf16[192,640]{1,0:T(8,128)(2,1)S(1)}, bf16[192,640]{1,0:T(8,128)(2,1)S(1)}, u32[]{:S(2)}, u32[]{:S(2)}) %collective-permute-start.54) | collective-permute-done | bytes 245792 | tf_op jit(solution)/shard_map/ppermute | solution.py:202
  395.7 7.3 %collective-permute-done.79 = bf16[2,2,2,24,768]{4,3,1,2,0:T(8,128)(2,1)S(1)} collective-permute-done((bf16[2,2,2,24,768]{4,3,1,2,0:T(8,128)(2,1)S(1)}, bf16[2,2,2,24,768]{4,3,1,2,0:T(8,128)(2,1)S(1)}, u32[]{:S(2)}, u32[]{:S(2)}) %collective-permute-start.79) | collective-permute-done | bytes 294944 | tf_op jit(solution)/shard_map/ppermute | solution.py:202
  403.8 2.7 collective-permute-start.57
  406.6 3.5 collective-permute-done.65
  413.1 22.7 %collective-permute-done.87 = bf16[2,2,2,96,768]{4,3,1,2,0:T(8,128)(2,1)S(1)} collective-permute-done((bf16[2,2,2,96,768]{4,3,1,2,0:T(8,128)(2,1)S(1)}, bf16[2,2,2,96,768]{4,3,1,2,0:T(8,128)(2,1)S(1)}, u32[]{:S(2)}, u32[]{:S(2)}) %collective-permute-start.87) | collective-permute-done | bytes 1179680 | tf_op jit(solution)/shard_map/ppermute | solution.py:202
  436.9 17.9 %attend_back.5 = (bf16[192,640]{1,0:T(8,128)(2,1)S(1)}, bf16[192,640]{1,0:T(8,128)(2,1)S(1)}, bf16[192,640]{1,0:T(8,128)(2,1)S(1)}, bf16[192,640]{1,0:T(8,128)(2,1)S(1)}) custom-call(s32[1,5]{1,0:T(1,128)S(1)} %copy-done, s32[1]{0:T(128)} %bitcast.16.here, bf16[192,2560]{1,0:T(8,128)(2,1)S(1)} %get-tuple-element.161.packed, ...), custom_call_target="tpu_custom_call" | custom-call | flops 15000000512 | bytes 1000000 | tf_op jit(solution)/shard_map/attend_back/pallas_call | solution.py:170
  464.0 4.5 collective-permute-done.80
  469.6 6.9 %collective-permute-done.72 = bf16[2,24,768]{2,1,0:T(8,128)(2,1)S(1)} collective-permute-done((bf16[2,24,768]{2,1,0:T(8,128)(2,1)S(1)}, bf16[2,24,768]{2,1,0:T(8,128)(2,1)S(1)}, u32[]{:S(2)}, u32[]{:S(2)}) %collective-permute-start.72) | collective-permute-done | bytes 73760 | tf_op jit(solution)/shard_map/ppermute | solution.py:202
  476.6 4.7 collective-permute-done.67
  481.3 4.8 collective-permute-done.73
  486.1 4.8 collective-permute-done.68
  492.5 2.8 collective-permute-done.81
  501.6 4.1 multiply_reduce_fusion.1
  505.8 2.6 select_reduce_fusion
  537.6 5.1 collective-permute-done.85
  543.2 2.7 collective-permute-done.89
  553.7 3.2 collective-permute-done.77
  558.2 3.6 collective-permute-done.78
  (601 shorter events, 183.7 us)
Async XLA Ops:
  24.6 8.4 %collective-permute-start.29 = (bf16[2,24,768]{2,1,0:T(8,128)(2,1)S(1)}, bf16[2,24,768]{2,1,0:T(8,128)(2,1)S(1)}, u32[]{:S(2)}, u32[]{:S(2)}) collective-permute-start(bf16[2,24,768]{2,1,0:T(8,128)(2,1)S(1)} %pad_maximum_fusion.26), channel_id=1, source_target_pairs={{0,1},{1,0},{2,3},{3,2},{4,5},{5,4},{6,7},{7,6},{8,9},{9,8},{10,11... | collective-permute-start | bytes 221192 | tf_op jit(solution)/shard_map/ppermute | solution.py:202
  28.2 13.2 %collective-permute-start.2 = (bf16[2,2,24,1280]{3,2,0,1:T(8,128)(2,1)S(1)}, bf16[2,2,24,1280]{3,2,0,1:T(8,128)(2,1)S(1)}, u32[]{:S(2)}, u32[]{:S(2)}) collective-permute-start(bf16[2,2,24,1280]{3,2,0,1:T(8,128)(2,1)S(1)} %pad_maximum_fusion.21), channel_id=1, source_target_pairs={{0,16},{4,20},{8,24},{12,28},{16,0},{20,4},{24,8},{28,12},{1,17},{... | collective-permute-start | bytes 737288 | tf_op jit(solution)/shard_map/ppermute | solution.py:202
  29.7 9.3 %collective-permute-start.33 = (bf16[24,3072]{1,0:T(8,128)(2,1)S(1)}, bf16[24,3072]{1,0:T(8,128)(2,1)S(1)}, u32[]{:S(2)}, u32[]{:S(2)}) collective-permute-start(bf16[24,3072]{1,0:T(8,128)(2,1)S(1)} %copy-done.53), channel_id=1, source_target_pairs={{0,2},{1,3},{2,0},{3,1},{4,6},{5,7},{6,4},{7,5},{8,10},{9,11},{10,... | collective-permute-start | bytes 442376 | tf_op jit(solution)/shard_map/ppermute | solution.py:202
  32.9 8.2 %collective-permute-start.38 = (bf16[96,768]{1,0:T(8,128)(2,1)S(1)}, bf16[96,768]{1,0:T(8,128)(2,1)S(1)}, u32[]{:S(2)}, u32[]{:S(2)}) collective-permute-start(bf16[96,768]{1,0:T(8,128)(2,1)S(1)} %copy-done.54), channel_id=1, source_target_pairs={{0,2},{1,3},{2,0},{3,1},{4,6},{5,7},{6,4},{7,5},{8,10},{9,11},{10,... | collective-permute-start | bytes 442376 | tf_op jit(solution)/shard_map/ppermute | solution.py:202
  33.2 19.7 %collective-permute-start.14 = (bf16[2,2,2,24,1152]{4,3,1,2,0:T(8,128)(2,1)S(1)}, bf16[2,2,2,24,1152]{4,3,1,2,0:T(8,128)(2,1)S(1)}, u32[]{:S(2)}, u32[]{:S(2)}) collective-permute-start(bf16[2,2,2,24,1152]{4,3,1,2,0:T(8,128)(2,1)S(1)} %pad_maximum_fusion.17), channel_id=1, source_target_pairs={{0,16},{4,20},{8,24},{12,28},{16,0},{20,4},{24,8},{28,12},{1,17},{... | collective-permute-start | bytes 1327112 | tf_op jit(solution)/shard_map/ppermute | solution.py:202
  39.1 9.7 %collective-permute-start.34 = (bf16[2,24,3072]{2,1,0:T(8,128)(2,1)S(1)}, bf16[2,24,3072]{2,1,0:T(8,128)(2,1)S(1)}, u32[]{:S(2)}, u32[]{:S(2)}) collective-permute-start(bf16[2,24,3072]{2,1,0:T(8,128)(2,1)S(1)} %pad_maximum_fusion.19), channel_id=1, source_target_pairs={{0,1},{1,0},{2,3},{3,2},{4,5},{5,4},{6,7},{7,6},{8,9},{9,8},{10,11... | collective-permute-start | bytes 884744 | tf_op jit(solution)/shard_map/ppermute | solution.py:202
  41.2 10.8 %collective-permute-start.39 = (bf16[2,96,768]{2,1,0:T(8,128)(2,1)S(1)}, bf16[2,96,768]{2,1,0:T(8,128)(2,1)S(1)}, u32[]{:S(2)}, u32[]{:S(2)}) collective-permute-start(bf16[2,96,768]{2,1,0:T(8,128)(2,1)S(1)} %pad_maximum_fusion.20), channel_id=1, source_target_pairs={{0,1},{1,0},{2,3},{3,2},{4,5},{5,4},{6,7},{7,6},{8,9},{9,8},{10,11... | collective-permute-start | bytes 884744 | tf_op jit(solution)/shard_map/ppermute | solution.py:202
  41.4 11.8 %collective-permute-start.3 = (bf16[2,2,2,24,1280]{4,3,1,2,0:T(8,128)(2,1)S(1)}, bf16[2,2,2,24,1280]{4,3,1,2,0:T(8,128)(2,1)S(1)}, u32[]{:S(2)}, u32[]{:S(2)}) collective-permute-start(bf16[2,2,2,24,1280]{4,3,1,2,0:T(8,128)(2,1)S(1)} %pad_maximum_fusion.16), channel_id=1, source_target_pairs={{0,8},{4,12},{8,0},{12,4},{16,24},{20,28},{24,16},{28,20},{1,9},{5... | collective-permute-start | bytes 1474568 | tf_op jit(solution)/shard_map/ppermute | solution.py:202
  74.4 13.3 %collective-permute-start.5 = (bf16[192,640]{1,0:T(8,128)(2,1)}, bf16[192,640]{1,0:T(8,128)(2,1)S(1)}, u32[]{:S(2)}, u32[]{:S(2)}) collective-permute-start(bf16[192,640]{1,0:T(8,128)(2,1)} %get-tuple-element.96), channel_id=1, source_target_pairs={{0,1},{1,0},{2,3},{3,2},{4,5},{5,4},{6,7},{7,6},{8,9},{9,8},{10,11... | collective-permute-start | bytes 737288 | tf_op jit(solution)/shard_map/ppermute | solution.py:202
  74.4 20.5 %collective-permute-start.6 = (bf16[192,640]{1,0:T(8,128)(2,1)}, bf16[192,640]{1,0:T(8,128)(2,1)S(1)}, u32[]{:S(2)}, u32[]{:S(2)}) collective-permute-start(bf16[192,640]{1,0:T(8,128)(2,1)} %get-tuple-element.97), channel_id=1, source_target_pairs={{0,2},{1,3},{2,0},{3,1},{4,6},{5,7},{6,4},{7,5},{8,10},{9,11},{10,... | collective-permute-start | bytes 737288 | tf_op jit(solution)/shard_map/ppermute | solution.py:202
  75.0 19.9 %collective-permute-start.7 = (bf16[192,640]{1,0:T(8,128)(2,1)}, bf16[192,640]{1,0:T(8,128)(2,1)S(1)}, u32[]{:S(2)}, u32[]{:S(2)}) collective-permute-start(bf16[192,640]{1,0:T(8,128)(2,1)} %get-tuple-element.98), channel_id=1, source_target_pairs={{0,3},{1,2},{2,1},{3,0},{4,7},{5,6},{6,5},{7,4},{8,11},{9,10},{10,... | collective-permute-start | bytes 737288 | tf_op jit(solution)/shard_map/ppermute | solution.py:202
  84.4 85.6 %collective-permute-start.35 = (bf16[2,2,24,3072]{3,2,1,0:T(8,128)(2,1)S(1)}, bf16[2,2,24,3072]{3,2,1,0:T(8,128)(2,1)S(1)}, u32[]{:S(2)}, u32[]{:S(2)}) collective-permute-start(bf16[2,2,24,3072]{3,2,1,0:T(8,128)(2,1)S(1)} %copy-done.34), channel_id=1, source_target_pairs={{0,16},{4,20},{8,24},{12,28},{16,0},{20,4},{24,8},{28,12},{1,17},{... | collective-permute-start | bytes 1769480 | tf_op jit(solution)/shard_map/ppermute | solution.py:202
  86.0 86.7 %collective-permute-start.40 = (bf16[2,2,96,768]{3,2,1,0:T(8,128)(2,1)}, bf16[2,2,96,768]{3,2,1,0:T(8,128)(2,1)S(1)}, u32[]{:S(2)}, u32[]{:S(2)}) collective-permute-start(bf16[2,2,96,768]{3,2,1,0:T(8,128)(2,1)} %pad_maximum_fusion.15), channel_id=1, source_target_pairs={{0,8},{4,12},{8,0},{12,4},{16,24},{20,28},{24,16},{28,20},{1,9},{5... | collective-permute-start | bytes 1769480 | tf_op jit(solution)/shard_map/ppermute | solution.py:202
  87.6 37.8 %collective-permute-start.31 = (bf16[2,2,2,24,768]{4,3,2,1,0:T(8,128)(2,1)S(1)}, bf16[2,2,2,24,768]{4,3,2,1,0:T(8,128)(2,1)S(1)}, u32[]{:S(2)}, u32[]{:S(2)}) collective-permute-start(bf16[2,2,2,24,768]{4,3,2,1,0:T(8,128)(2,1)S(1)} %pad_maximum_fusion.18), channel_id=1, source_target_pairs={{0,8},{4,12},{8,0},{12,4},{16,24},{20,28},{24,16},{28,20},{1,9},{5... | collective-permute-start | bytes 884744 | tf_op jit(solution)/shard_map/ppermute | solution.py:202
  94.9 32.2 %collective-permute-start.16 = (bf16[192,640]{1,0:T(8,128)(2,1)S(1)}, bf16[192,640]{1,0:T(8,128)(2,1)S(1)}, u32[]{:S(2)}, u32[]{:S(2)}) collective-permute-start(bf16[192,640]{1,0:T(8,128)(2,1)S(1)} %get-tuple-element.104), channel_id=1, source_target_pairs={{0,1},{1,0},{2,3},{3,2},{4,5},{5,4},{6,7},{7,6},{8,9},{9,8},{10,11... | collective-permute-start | bytes 737288 | tf_op jit(solution)/shard_map/ppermute | solution.py:202
  118.2 7.2 %collective-permute-start.10 = (bf16[64,640]{1,0:T(8,128)(2,1)S(1)}, bf16[64,640]{1,0:T(8,128)(2,1)S(1)}, u32[]{:S(2)}, u32[]{:S(2)}) collective-permute-start(bf16[64,640]{1,0:T(8,128)(2,1)S(1)} %get-tuple-element.102), channel_id=1, source_target_pairs={{0,3},{1,2},{2,1},{3,0},{4,7},{5,6},{6,5},{7,4},{8,11},{9,10},{10,... | collective-permute-start | bytes 245768 | tf_op jit(solution)/shard_map/ppermute | solution.py:202
  125.4 13.6 %collective-permute-start.17 = (bf16[192,640]{1,0:T(8,128)(2,1)S(1)}, bf16[192,640]{1,0:T(8,128)(2,1)S(1)}, u32[]{:S(2)}, u32[]{:S(2)}) collective-permute-start(bf16[192,640]{1,0:T(8,128)(2,1)S(1)} %get-tuple-element.105), channel_id=1, source_target_pairs={{0,2},{1,3},{2,0},{3,1},{4,6},{5,7},{6,4},{7,5},{8,10},{9,11},{10,... | collective-permute-start | bytes 737288 | tf_op jit(solution)/shard_map/ppermute | solution.py:202
  125.5 13.6 %collective-permute-start.18 = (bf16[192,640]{1,0:T(8,128)(2,1)S(1)}, bf16[192,640]{1,0:T(8,128)(2,1)S(1)}, u32[]{:S(2)}, u32[]{:S(2)}) collective-permute-start(bf16[192,640]{1,0:T(8,128)(2,1)S(1)} %get-tuple-element.106), channel_id=1, source_target_pairs={{0,3},{1,2},{2,1},{3,0},{4,7},{5,6},{6,5},{7,4},{8,11},{9,10},{10,... | collective-permute-start | bytes 737288 | tf_op jit(solution)/shard_map/ppermute | solution.py:202
  127.1 79.9 %collective-permute-start.32 = (bf16[2,2,2,2,24,768]{5,4,3,2,1,0:T(8,128)(2,1)S(1)}, bf16[2,2,2,2,24,768]{5,4,3,2,1,0:T(8,128)(2,1)S(1)}, u32[]{:S(2)}, u32[]{:S(2)}) collective-permute-start(bf16[2,2,2,2,24,768]{5,4,3,2,1,0:T(8,128)(2,1)S(1)} %pad_maximum_fusion.13), channel_id=1, source_target_pairs={{0,4},{4,0},{8,12},{12,8},{16,20},{20,16},{24,28},{28,24},{1,5},{5... | collective-permute-start | bytes 1769480 | tf_op jit(solution)/shard_map/ppermute | solution.py:202
  139.1 35.5 %collective-permute-start.22 = (bf16[192,640]{1,0:T(8,128)(2,1)S(1)}, bf16[192,640]{1,0:T(8,128)(2,1)S(1)}, u32[]{:S(2)}, u32[]{:S(2)}) collective-permute-start(bf16[192,640]{1,0:T(8,128)(2,1)S(1)} %copy-done.52), channel_id=1, source_target_pairs={{0,1},{1,0},{2,3},{3,2},{4,5},{5,4},{6,7},{7,6},{8,9},{9,8},{10,11... | collective-permute-start | bytes 737288 | tf_op jit(solution)/shard_map/ppermute | solution.py:202
  162.7 7.2 %collective-permute-start.21 = (bf16[64,640]{1,0:T(8,128)(2,1)S(1)}, bf16[64,640]{1,0:T(8,128)(2,1)S(1)}, u32[]{:S(2)}, u32[]{:S(2)}) collective-permute-start(bf16[64,640]{1,0:T(8,128)(2,1)S(1)} %get-tuple-element.110), channel_id=1, source_target_pairs={{0,3},{1,2},{2,1},{3,0},{4,7},{5,6},{6,5},{7,4},{8,11},{9,10},{10,... | collective-permute-start | bytes 245768 | tf_op jit(solution)/shard_map/ppermute | solution.py:202
  170.0 14.4 %collective-permute-start.23 = (bf16[192,640]{1,0:T(8,128)(2,1)S(1)}, bf16[192,640]{1,0:T(8,128)(2,1)S(1)}, u32[]{:S(2)}, u32[]{:S(2)}) collective-permute-start(bf16[192,640]{1,0:T(8,128)(2,1)S(1)} %copy-done.51), channel_id=1, source_target_pairs={{0,2},{1,3},{2,0},{3,1},{4,6},{5,7},{6,4},{7,5},{8,10},{9,11},{10,... | collective-permute-start | bytes 737288 | tf_op jit(solution)/shard_map/ppermute | solution.py:202
  170.0 14.4 %collective-permute-start.24 = (bf16[192,640]{1,0:T(8,128)(2,1)S(1)}, bf16[192,640]{1,0:T(8,128)(2,1)S(1)}, u32[]{:S(2)}, u32[]{:S(2)}) collective-permute-start(bf16[192,640]{1,0:T(8,128)(2,1)S(1)} %copy-done.50), channel_id=1, source_target_pairs={{0,3},{1,2},{2,1},{3,0},{4,7},{5,6},{6,5},{7,4},{8,11},{9,10},{10,... | collective-permute-start | bytes 737288 | tf_op jit(solution)/shard_map/ppermute | solution.py:202
  172.7 33.6 %collective-permute-start.36 = (bf16[2,2,2,24,3072]{4,3,2,1,0:T(8,128)(2,1)S(1)}, bf16[2,2,2,24,3072]{4,3,2,1,0:T(8,128)(2,1)S(1)}, u32[]{:S(2)}, u32[]{:S(2)}) collective-permute-start(bf16[2,2,2,24,3072]{4,3,2,1,0:T(8,128)(2,1)S(1)} %pad_maximum_fusion.8), channel_id=1, source_target_pairs={{0,8},{4,12},{8,0},{12,4},{16,24},{20,28},{24,16},{28,20},{1,9},{5... | collective-permute-start | bytes 3538952 | tf_op jit(solution)/shard_map/ppermute | solution.py:202
  174.6 32.7 %collective-permute-start.41 = (bf16[2,2,2,96,768]{4,3,2,1,0:T(8,128)(2,1)S(1)}, bf16[2,2,2,96,768]{4,3,2,1,0:T(8,128)(2,1)S(1)}, u32[]{:S(2)}, u32[]{:S(2)}) collective-permute-start(bf16[2,2,2,96,768]{4,3,2,1,0:T(8,128)(2,1)S(1)} %pad_maximum_fusion.9), channel_id=1, source_target_pairs={{0,16},{4,20},{8,24},{12,28},{16,0},{20,4},{24,8},{28,12},{1,17},{... | collective-permute-start | bytes 3538952 | tf_op jit(solution)/shard_map/ppermute | solution.py:202
  191.9 8.0 %collective-permute-start.25 = (bf16[64,640]{1,0:T(8,128)(2,1)S(1)}, bf16[64,640]{1,0:T(8,128)(2,1)S(1)}, u32[]{:S(2)}, u32[]{:S(2)}) collective-permute-start(bf16[64,640]{1,0:T(8,128)(2,1)S(1)} %get-tuple-element.116), channel_id=1, source_target_pairs={{0,1},{1,0},{2,3},{3,2},{4,5},{5,4},{6,7},{7,6},{8,9},{9,8},{10,11... | collective-permute-start | bytes 245768 | tf_op jit(solution)/shard_map/ppermute | solution.py:202
  197.4 8.9 %collective-permute-start.26 = (bf16[64,640]{1,0:T(8,128)(2,1)S(1)}, bf16[64,640]{1,0:T(8,128)(2,1)S(1)}, u32[]{:S(2)}, u32[]{:S(2)}) collective-permute-start(bf16[64,640]{1,0:T(8,128)(2,1)S(1)} %get-tuple-element.117), channel_id=1, source_target_pairs={{0,2},{1,3},{2,0},{3,1},{4,6},{5,7},{6,4},{7,5},{8,10},{9,11},{10,... | collective-permute-start | bytes 245768 | tf_op jit(solution)/shard_map/ppermute | solution.py:202
  247.4 8.6 %collective-permute-start.43 = (bf16[64,640]{1,0:T(8,128)(2,1)S(1)}, bf16[64,640]{1,0:T(8,128)(2,1)S(1)}, u32[]{:S(2)}, u32[]{:S(2)}) collective-permute-start(bf16[64,640]{1,0:T(8,128)(2,1)S(1)} %get-tuple-element.132), channel_id=1, source_target_pairs={{0,1},{1,0},{2,3},{3,2},{4,5},{5,4},{6,7},{7,6},{8,9},{9,8},{10,11... | collective-permute-start | bytes 245768 | tf_op jit(solution)/shard_map/ppermute | solution.py:202
  247.4 9.8 %collective-permute-start.44 = (bf16[64,640]{1,0:T(8,128)(2,1)S(1)}, bf16[64,640]{1,0:T(8,128)(2,1)S(1)}, u32[]{:S(2)}, u32[]{:S(2)}) collective-permute-start(bf16[64,640]{1,0:T(8,128)(2,1)S(1)} %get-tuple-element.133), channel_id=1, source_target_pairs={{0,2},{1,3},{2,0},{3,1},{4,6},{5,7},{6,4},{7,5},{8,10},{9,11},{10,... | collective-permute-start | bytes 245768 | tf_op jit(solution)/shard_map/ppermute | solution.py:202
  248.5 8.8 %collective-permute-start.45 = (bf16[64,640]{1,0:T(8,128)(2,1)S(1)}, bf16[64,640]{1,0:T(8,128)(2,1)S(1)}, u32[]{:S(2)}, u32[]{:S(2)}) collective-permute-start(bf16[64,640]{1,0:T(8,128)(2,1)S(1)} %get-tuple-element.134), channel_id=1, source_target_pairs={{0,3},{1,2},{2,1},{3,0},{4,7},{5,6},{6,5},{7,4},{8,11},{9,10},{10,... | collective-permute-start | bytes 245768 | tf_op jit(solution)/shard_map/ppermute | solution.py:202
  282.7 48.2 %collective-permute-start.58 = (bf16[2,2,2,2,96,768]{5,4,2,3,1,0:T(8,128)(2,1)}, bf16[2,2,2,2,96,768]{5,4,2,3,1,0:T(8,128)(2,1)}, u32[]{:S(2)}, u32[]{:S(2)}) collective-permute-start(bf16[2,2,2,2,96,768]{5,4,2,3,1,0:T(8,128)(2,1)} %select_bitcast_fusion.3), channel_id=1, source_target_pairs={{0,4},{4,0},{8,12},{12,8},{16,20},{20,16},{24,28},{28,24},{1,5},{5... | collective-permute-start | bytes 7077896 | tf_op jit(solution)/shard_map/ppermute | solution.py:202
  291.5 42.6 %collective-permute-start.59 = (bf16[2,2,2,2,24,3072]{5,4,2,3,0,1:T(8,128)(2,1)}, bf16[2,2,2,2,24,3072]{5,4,2,3,0,1:T(8,128)(2,1)}, u32[]{:S(2)}, u32[]{:S(2)}) collective-permute-start(bf16[2,2,2,2,24,3072]{5,4,2,3,0,1:T(8,128)(2,1)} %select_bitcast_fusion.1), channel_id=1, source_target_pairs={{0,4},{4,0},{8,12},{12,8},{16,20},{20,16},{24,28},{28,24},{1,5},{5... | collective-permute-start | bytes 7077896 | tf_op jit(solution)/shard_map/ppermute | solution.py:202
  295.0 19.3 %collective-permute-start.46 = (bf16[192,640]{1,0:T(8,128)(2,1)S(1)}, bf16[192,640]{1,0:T(8,128)(2,1)S(1)}, u32[]{:S(2)}, u32[]{:S(2)}) collective-permute-start(bf16[192,640]{1,0:T(8,128)(2,1)S(1)} %get-tuple-element.136), channel_id=1, source_target_pairs={{0,1},{1,0},{2,3},{3,2},{4,5},{5,4},{6,7},{7,6},{8,9},{9,8},{10,11... | collective-permute-start | bytes 737288 | tf_op jit(solution)/shard_map/ppermute | solution.py:202
  296.5 10.4 %collective-permute-start.49 = (bf16[64,640]{1,0:T(8,128)(2,1)S(1)}, bf16[64,640]{1,0:T(8,128)(2,1)S(1)}, u32[]{:S(2)}, u32[]{:S(2)}) collective-permute-start(bf16[64,640]{1,0:T(8,128)(2,1)S(1)} %get-tuple-element.143), channel_id=1, source_target_pairs={{0,1},{1,0},{2,3},{3,2},{4,5},{5,4},{6,7},{7,6},{8,9},{9,8},{10,11... | collective-permute-start | bytes 245768 | tf_op jit(solution)/shard_map/ppermute | solution.py:202
  297.1 11.2 %collective-permute-start.50 = (bf16[64,640]{1,0:T(8,128)(2,1)S(1)}, bf16[64,640]{1,0:T(8,128)(2,1)S(1)}, u32[]{:S(2)}, u32[]{:S(2)}) collective-permute-start(bf16[64,640]{1,0:T(8,128)(2,1)S(1)} %get-tuple-element.144), channel_id=1, source_target_pairs={{0,2},{1,3},{2,0},{3,1},{4,6},{5,7},{6,4},{7,5},{8,10},{9,11},{10,... | collective-permute-start | bytes 245768 | tf_op jit(solution)/shard_map/ppermute | solution.py:202
  308.3 20.3 %collective-permute-start.47 = (bf16[192,640]{1,0:T(8,128)(2,1)S(1)}, bf16[192,640]{1,0:T(8,128)(2,1)S(1)}, u32[]{:S(2)}, u32[]{:S(2)}) collective-permute-start(bf16[192,640]{1,0:T(8,128)(2,1)S(1)} %get-tuple-element.137), channel_id=1, source_target_pairs={{0,2},{1,3},{2,0},{3,1},{4,6},{5,7},{6,4},{7,5},{8,10},{9,11},{10,... | collective-permute-start | bytes 737288 | tf_op jit(solution)/shard_map/ppermute | solution.py:202
  314.2 14.5 %collective-permute-start.60 = (bf16[2,2,2,2,24,768]{5,4,2,3,0,1:T(8,128)(2,1)S(1)}, bf16[2,2,2,2,24,768]{5,4,2,3,0,1:T(8,128)(2,1)S(1)}, u32[]{:S(2)}, u32[]{:S(2)}) collective-permute-start(bf16[2,2,2,2,24,768]{5,4,2,3,0,1:T(8,128)(2,1)S(1)} %select_bitcast_fusion.26), channel_id=1, source_target_pairs={{0,4},{4,0},{8,12},{12,8},{16,20},{20,16},{24,28},{28,24},{1,5},{5... | collective-permute-start | bytes 1769480 | tf_op jit(solution)/shard_map/ppermute | solution.py:202
  314.3 56.4 %collective-permute-start.48 = (bf16[192,640]{1,0:T(8,128)(2,1)S(1)}, bf16[192,640]{1,0:T(8,128)(2,1)S(1)}, u32[]{:S(2)}, u32[]{:S(2)}) collective-permute-start(bf16[192,640]{1,0:T(8,128)(2,1)S(1)} %get-tuple-element.138), channel_id=1, source_target_pairs={{0,3},{1,2},{2,1},{3,0},{4,7},{5,6},{6,5},{7,4},{8,11},{9,10},{10,... | collective-permute-start | bytes 737288 | tf_op jit(solution)/shard_map/ppermute | solution.py:202
  328.6 108.3 %collective-permute-start.55 = (bf16[64,640]{1,0:T(8,128)(2,1)}, bf16[64,640]{1,0:T(8,128)(2,1)S(1)}, u32[]{:S(2)}, u32[]{:S(2)}) collective-permute-start(bf16[64,640]{1,0:T(8,128)(2,1)} %get-tuple-element.165), channel_id=1, source_target_pairs={{0,1},{1,0},{2,3},{3,2},{4,5},{5,4},{6,7},{7,6},{8,9},{9,8},{10,11... | collective-permute-start | bytes 245768 | tf_op jit(solution)/shard_map/ppermute | solution.py:202
  328.7 108.2 %collective-permute-start.56 = (bf16[64,640]{1,0:T(8,128)(2,1)}, bf16[64,640]{1,0:T(8,128)(2,1)S(1)}, u32[]{:S(2)}, u32[]{:S(2)}) collective-permute-start(bf16[64,640]{1,0:T(8,128)(2,1)} %get-tuple-element.166), channel_id=1, source_target_pairs={{0,2},{1,3},{2,0},{3,1},{4,6},{5,7},{6,4},{7,5},{8,10},{9,11},{10,... | collective-permute-start | bytes 245768 | tf_op jit(solution)/shard_map/ppermute | solution.py:202
  355.9 12.3 %collective-permute-start.52 = (bf16[192,640]{1,0:T(8,128)(2,1)S(1)}, bf16[192,640]{1,0:T(8,128)(2,1)S(1)}, u32[]{:S(2)}, u32[]{:S(2)}) collective-permute-start(bf16[192,640]{1,0:T(8,128)(2,1)S(1)} %get-tuple-element.158), channel_id=1, source_target_pairs={{0,1},{1,0},{2,3},{3,2},{4,5},{5,4},{6,7},{7,6},{8,9},{9,8},{10,11... | collective-permute-start | bytes 737288 | tf_op jit(solution)/shard_map/ppermute | solution.py:202
  356.1 14.0 %collective-permute-start.53 = (bf16[192,640]{1,0:T(8,128)(2,1)S(1)}, bf16[192,640]{1,0:T(8,128)(2,1)S(1)}, u32[]{:S(2)}, u32[]{:S(2)}) collective-permute-start(bf16[192,640]{1,0:T(8,128)(2,1)S(1)} %get-tuple-element.159), channel_id=1, source_target_pairs={{0,2},{1,3},{2,0},{3,1},{4,6},{5,7},{6,4},{7,5},{8,10},{9,11},{10,... | collective-permute-start | bytes 737288 | tf_op jit(solution)/shard_map/ppermute | solution.py:202
  368.2 8.8 %collective-permute-start.54 = (bf16[192,640]{1,0:T(8,128)(2,1)S(1)}, bf16[192,640]{1,0:T(8,128)(2,1)S(1)}, u32[]{:S(2)}, u32[]{:S(2)}) collective-permute-start(bf16[192,640]{1,0:T(8,128)(2,1)S(1)} %get-tuple-element.160), channel_id=1, source_target_pairs={{0,3},{1,2},{2,1},{3,0},{4,7},{5,6},{6,5},{7,4},{8,11},{9,10},{10,... | collective-permute-start | bytes 737288 | tf_op jit(solution)/shard_map/ppermute | solution.py:202
  370.0 40.5 %collective-permute-start.83 = (bf16[2,2,2,24,3072]{4,3,1,2,0:T(8,128)(2,1)}, bf16[2,2,2,24,3072]{4,3,1,2,0:T(8,128)(2,1)}, u32[]{:S(2)}, u32[]{:S(2)}) collective-permute-start(bf16[2,2,2,24,3072]{4,3,1,2,0:T(8,128)(2,1)} %select_bitcast_fusion.9), channel_id=1, source_target_pairs={{0,8},{4,12},{8,0},{12,4},{16,24},{20,28},{24,16},{28,20},{1,9},{5... | collective-permute-start | bytes 3538952 | tf_op jit(solution)/shard_map/ppermute | solution.py:202
  382.3 8.8 %collective-permute-start.69 = (bf16[2,2,2,2,24,768]{5,4,2,3,1,0:T(8,128)(2,1)}, bf16[2,2,2,2,24,768]{5,4,2,3,1,0:T(8,128)(2,1)}, u32[]{:S(2)}, u32[]{:S(2)}) collective-permute-start(bf16[2,2,2,2,24,768]{5,4,2,3,1,0:T(8,128)(2,1)} %select_bitcast_fusion.23), channel_id=1, source_target_pairs={{0,4},{4,0},{8,12},{12,8},{16,20},{20,16},{24,28},{28,24},{1,5},{5... | collective-permute-start | bytes 1769480 | tf_op jit(solution)/shard_map/ppermute | solution.py:202
  391.2 11.9 %collective-permute-start.79 = (bf16[2,2,2,24,768]{4,3,1,2,0:T(8,128)(2,1)S(1)}, bf16[2,2,2,24,768]{4,3,1,2,0:T(8,128)(2,1)S(1)}, u32[]{:S(2)}, u32[]{:S(2)}) collective-permute-start(bf16[2,2,2,24,768]{4,3,1,2,0:T(8,128)(2,1)S(1)} %copy-done.49), channel_id=1, source_target_pairs={{0,8},{4,12},{8,0},{12,4},{16,24},{20,28},{24,16},{28,20},{1,9},{5... | collective-permute-start | bytes 884744 | tf_op jit(solution)/shard_map/ppermute | solution.py:202
  393.5 10.2 %collective-permute-start.70 = (bf16[2,2,2,24,768]{4,3,1,2,0:T(8,128)(2,1)S(1)}, bf16[2,2,2,24,768]{4,3,1,2,0:T(8,128)(2,1)S(1)}, u32[]{:S(2)}, u32[]{:S(2)}) collective-permute-start(bf16[2,2,2,24,768]{4,3,1,2,0:T(8,128)(2,1)S(1)} %select_bitcast_fusion.40), channel_id=1, source_target_pairs={{0,16},{4,20},{8,24},{12,28},{16,0},{20,4},{24,8},{28,12},{1,17},{... | collective-permute-start | bytes 884744 | tf_op jit(solution)/shard_map/ppermute | solution.py:202
  403.8 33.1 %collective-permute-start.57 = (bf16[64,640]{1,0:T(8,128)(2,1)S(1)}, bf16[64,640]{1,0:T(8,128)(2,1)S(1)}, u32[]{:S(2)}, u32[]{:S(2)}) collective-permute-start(bf16[64,640]{1,0:T(8,128)(2,1)S(1)} %copy-done.61), channel_id=1, source_target_pairs={{0,3},{1,2},{2,1},{3,0},{4,7},{5,6},{6,5},{7,4},{8,11},{9,10},{10,... | collective-permute-start | bytes 245768 | tf_op jit(solution)/shard_map/ppermute | solution.py:202
  410.0 25.8 %collective-permute-start.87 = (bf16[2,2,2,96,768]{4,3,1,2,0:T(8,128)(2,1)S(1)}, bf16[2,2,2,96,768]{4,3,1,2,0:T(8,128)(2,1)S(1)}, u32[]{:S(2)}, u32[]{:S(2)}) collective-permute-start(bf16[2,2,2,96,768]{4,3,1,2,0:T(8,128)(2,1)S(1)} %copy-done.35), channel_id=1, source_target_pairs={{0,16},{4,20},{8,24},{12,28},{16,0},{20,4},{24,8},{28,12},{1,17},{... | collective-permute-start | bytes 3538952 | tf_op jit(solution)/shard_map/ppermute | solution.py:202
  410.5 51.2 %collective-permute-start.71 = (bf16[2,2,24,768]{3,2,0,1:T(8,128)(2,1)S(1)}, bf16[2,2,24,768]{3,2,0,1:T(8,128)(2,1)S(1)}, u32[]{:S(2)}, u32[]{:S(2)}) collective-permute-start(bf16[2,2,24,768]{3,2,0,1:T(8,128)(2,1)S(1)} %select_bitcast_fusion.58), channel_id=1, source_target_pairs={{0,8},{4,12},{8,0},{12,4},{16,24},{20,28},{24,16},{28,20},{1,9},{5... | collective-permute-start | bytes 442376 | tf_op jit(solution)/shard_map/ppermute | solution.py:202
  435.8 27.5 %collective-permute-start.66 = (bf16[2,2,24,768]{3,2,0,1:T(8,128)(2,1)S(1)}, bf16[2,2,24,768]{3,2,0,1:T(8,128)(2,1)S(1)}, u32[]{:S(2)}, u32[]{:S(2)}) collective-permute-start(bf16[2,2,24,768]{3,2,0,1:T(8,128)(2,1)S(1)} %select_bitcast_fusion.59), channel_id=1, source_target_pairs={{0,16},{4,20},{8,24},{12,28},{16,0},{20,4},{24,8},{28,12},{1,17},{... | collective-permute-start | bytes 442376 | tf_op jit(solution)/shard_map/ppermute | solution.py:202
  454.9 41.1 %collective-permute-start.61 = (bf16[192,640]{1,0:T(8,128)(2,1)S(1)}, bf16[192,640]{1,0:T(8,128)(2,1)}, u32[]{:S(2)}, u32[]{:S(2)}) collective-permute-start(bf16[192,640]{1,0:T(8,128)(2,1)S(1)} %get-tuple-element.176), channel_id=1, source_target_pairs={{0,1},{1,0},{2,3},{3,2},{4,5},{5,4},{6,7},{7,6},{8,9},{9,8},{10,11... | collective-permute-start | bytes 737288 | tf_op jit(solution)/shard_map/ppermute | solution.py:202
  457.2 40.5 %collective-permute-start.62 = (bf16[192,640]{1,0:T(8,128)(2,1)S(1)}, bf16[192,640]{1,0:T(8,128)(2,1)}, u32[]{:S(2)}, u32[]{:S(2)}) collective-permute-start(bf16[192,640]{1,0:T(8,128)(2,1)S(1)} %get-tuple-element.177), channel_id=1, source_target_pairs={{0,2},{1,3},{2,0},{3,1},{4,6},{5,7},{6,4},{7,5},{8,10},{9,11},{10,... | collective-permute-start | bytes 737288 | tf_op jit(solution)/shard_map/ppermute | solution.py:202
  458.1 41.2 %collective-permute-start.63 = (bf16[192,640]{1,0:T(8,128)(2,1)S(1)}, bf16[192,640]{1,0:T(8,128)(2,1)S(1)}, u32[]{:S(2)}, u32[]{:S(2)}) collective-permute-start(bf16[192,640]{1,0:T(8,128)(2,1)S(1)} %get-tuple-element.178), channel_id=1, source_target_pairs={{0,3},{1,2},{2,1},{3,0},{4,7},{5,6},{6,5},{7,4},{8,11},{9,10},{10,... | collective-permute-start | bytes 737288 | tf_op jit(solution)/shard_map/ppermute | solution.py:202
  463.3 66.7 %collective-permute-start.84 = (bf16[2,2,24,3072]{3,2,0,1:T(8,128)(2,1)}, bf16[2,2,24,3072]{3,2,0,1:T(8,128)(2,1)}, u32[]{:S(2)}, u32[]{:S(2)}) collective-permute-start(bf16[2,2,24,3072]{3,2,0,1:T(8,128)(2,1)} %select_bitcast_fusion.21), channel_id=1, source_target_pairs={{0,16},{4,20},{8,24},{12,28},{16,0},{20,4},{24,8},{28,12},{1,17},{... | collective-permute-start | bytes 1769480 | tf_op jit(solution)/shard_map/ppermute | solution.py:202
  468.5 8.0 %collective-permute-start.72 = (bf16[2,24,768]{2,1,0:T(8,128)(2,1)S(1)}, bf16[2,24,768]{2,1,0:T(8,128)(2,1)S(1)}, u32[]{:S(2)}, u32[]{:S(2)}) collective-permute-start(bf16[2,24,768]{2,1,0:T(8,128)(2,1)S(1)} %select_bitcast_fusion.72), channel_id=1, source_target_pairs={{0,1},{1,0},{2,3},{3,2},{4,5},{5,4},{6,7},{7,6},{8,9},{9,8},{10,11... | collective-permute-start | bytes 221192 | tf_op jit(solution)/shard_map/ppermute | solution.py:202
  495.3 37.2 %collective-permute-start.88 = (bf16[2,2,96,768]{3,2,0,1:T(8,128)(2,1)}, bf16[2,2,96,768]{3,2,0,1:T(8,128)(2,1)}, u32[]{:S(2)}, u32[]{:S(2)}) collective-permute-start(bf16[2,2,96,768]{3,2,0,1:T(8,128)(2,1)} %select_bitcast_fusion.20), channel_id=1, source_target_pairs={{0,8},{4,12},{8,0},{12,4},{16,24},{20,28},{24,16},{28,20},{1,9},{5... | collective-permute-start | bytes 1769480 | tf_op jit(solution)/shard_map/ppermute | solution.py:202
  509.5 15.0 %collective-permute-start.82 = (bf16[24,768]{1,0:T(8,128)(2,1)S(1)}, bf16[24,768]{1,0:T(8,128)(2,1)S(1)}, u32[]{:S(2)}, u32[]{:S(2)}) collective-permute-start(bf16[24,768]{1,0:T(8,128)(2,1)S(1)} %select_bitcast_fusion.80), channel_id=1, source_target_pairs={{0,2},{1,3},{2,0},{3,1},{4,6},{5,7},{6,4},{7,5},{8,10},{9,11},{10,... | collective-permute-start | bytes 110600 | tf_op jit(solution)/shard_map/ppermute | solution.py:202
  521.0 13.8 %collective-permute-start.74 = (bf16[2,2,2,2,24,768]{5,4,2,3,0,1:T(8,128)(2,1)}, bf16[2,2,2,2,24,768]{5,4,2,3,0,1:T(8,128)(2,1)}, u32[]{:S(2)}, u32[]{:S(2)}) collective-permute-start(bf16[2,2,2,2,24,768]{5,4,2,3,0,1:T(8,128)(2,1)} %select_bitcast_fusion.22), channel_id=1, source_target_pairs={{0,4},{4,0},{8,12},{12,8},{16,20},{20,16},{24,28},{28,24},{1,5},{5... | collective-permute-start | bytes 1769480 | tf_op jit(solution)/shard_map/ppermute | solution.py:202
  531.3 11.4 %collective-permute-start.85 = (bf16[2,24,3072]{2,1,0:T(8,128)(2,1)S(1)}, bf16[2,24,3072]{2,1,0:T(8,128)(2,1)S(1)}, u32[]{:S(2)}, u32[]{:S(2)}) collective-permute-start(bf16[2,24,3072]{2,1,0:T(8,128)(2,1)S(1)} %select_bitcast_fusion.38), channel_id=1, source_target_pairs={{0,1},{1,0},{2,3},{3,2},{4,5},{5,4},{6,7},{7,6},{8,9},{9,8},{10,11... | collective-permute-start | bytes 884744 | tf_op jit(solution)/shard_map/ppermute | solution.py:202
  533.8 12.0 %collective-permute-start.89 = (bf16[2,96,768]{2,1,0:T(8,128)(2,1)S(1)}, bf16[2,96,768]{2,1,0:T(8,128)(2,1)S(1)}, u32[]{:S(2)}, u32[]{:S(2)}) collective-permute-start(bf16[2,96,768]{2,1,0:T(8,128)(2,1)S(1)} %select_bitcast_fusion.37), channel_id=1, source_target_pairs={{0,1},{1,0},{2,3},{3,2},{4,5},{5,4},{6,7},{7,6},{8,9},{9,8},{10,11... | collective-permute-start | bytes 884744 | tf_op jit(solution)/shard_map/ppermute | solution.py:202
  536.1 9.8 %collective-permute-start.75 = (bf16[2,2,2,24,768]{4,3,1,2,0:T(8,128)(2,1)S(1)}, bf16[2,2,2,24,768]{4,3,1,2,0:T(8,128)(2,1)S(1)}, u32[]{:S(2)}, u32[]{:S(2)}) collective-permute-start(bf16[2,2,2,24,768]{4,3,1,2,0:T(8,128)(2,1)S(1)} %select_bitcast_fusion.39), channel_id=1, source_target_pairs={{0,8},{4,12},{8,0},{12,4},{16,24},{20,28},{24,16},{28,20},{1,9},{5... | collective-permute-start | bytes 884744 | tf_op jit(solution)/shard_map/ppermute | solution.py:202
  542.8 10.1 %collective-permute-start.86 = (bf16[24,3072]{1,0:T(8,128)(2,1)S(1)}, bf16[24,3072]{1,0:T(8,128)(2,1)S(1)}, u32[]{:S(2)}, u32[]{:S(2)}) collective-permute-start(bf16[24,3072]{1,0:T(8,128)(2,1)S(1)} %select_bitcast_fusion.55), channel_id=1, source_target_pairs={{0,2},{1,3},{2,0},{3,1},{4,6},{5,7},{6,4},{7,5},{8,10},{9,11},{10,... | collective-permute-start | bytes 442376 | tf_op jit(solution)/shard_map/ppermute | solution.py:202
  547.7 9.8 %collective-permute-start.90 = (bf16[96,768]{1,0:T(8,128)(2,1)S(1)}, bf16[96,768]{1,0:T(8,128)(2,1)S(1)}, u32[]{:S(2)}, u32[]{:S(2)}) collective-permute-start(bf16[96,768]{1,0:T(8,128)(2,1)S(1)} %select_bitcast_fusion.54), channel_id=1, source_target_pairs={{0,2},{1,3},{2,0},{3,1},{4,6},{5,7},{6,4},{7,5},{8,10},{9,11},{10,... | collective-permute-start | bytes 442376 | tf_op jit(solution)/shard_map/ppermute | solution.py:202
  (133 other events, 1316.8 us)
